TPU v7x, 32 devices: a whole 2x2x4 slice. The times are simulated.
32 devices in a mesh: tp: 4 (over z), sy: 4 (over x, core), sx: 2 (over y).
Axes of the slice: x: 2, y: 2, z: 4, core: 2. Of those that a mesh axis runs over, the one named last changes fastest.
Arguments:
- queries: bfloat16 [24, 4, 32, 16, 128], P('tp', None, 'sy', 'sx'), may hold values from -8 to 8
- key_vectors: bfloat16 [24, 4, 32, 16, 128], P('tp', None, 'sy', 'sx'), may hold values from -8 to 8
- value_vectors: bfloat16 [24, 4, 32, 16, 128], P('tp', None, 'sy', 'sx'), may hold values from -6 to 6
- out_grad: bfloat16 [24, 4, 32, 16, 128], P('tp', None, 'sy', 'sx'), may hold values from -6 to 6
- cell_valid: int32 [32, 16], replicated, may hold values from 0 to 1, as said below
Outputs:
- query_grad: bfloat16 [24, 4, 32, 16, 128], P('tp', None, 'sy', 'sx')
- key_grad: bfloat16 [24, 4, 32, 16, 128], P('tp', None, 'sy', 'sx')
- value_grad: bfloat16 [24, 4, 32, 16, 128], P('tp', None, 'sy', 'sx')
Inputs may be any that keep to these rules, and one draw needn't show every extreme that they name: cell_valid is 1 exactly on one rectangle of cells and 0 elsewhere; the rectangle holds the rows 8 to 27 and the columns 4 to 11.
All inputs are finite; a program needn't handle non-finite values.
Results may differ from a plain program's by a relative error of at most 0.0085.
Values may be sent and summed in bfloat16 or wider, within the bound.
No kernel may reach another device: no remote copies, remote signals or barrier semaphores. Data moves between devices by JAX's collectives and lax.ppermute only.
A program may use at most 64 MiB of HBM per device.

v0:
```python
import math

import jax
import jax.numpy as jnp
from jax import lax
from jax.sharding import PartitionSpec as P


def extended(block, sides, width):
    for axis, dim in sides:
        count = lax.axis_size(axis)
        forward = [(i, i + 1) for i in range(count - 1)]
        backward = [(target, source) for source, target in forward]
        low = lax.ppermute(
            lax.slice_in_dim(block, block.shape[dim] - width, None, axis=dim), axis, forward
        )
        high = lax.ppermute(lax.slice_in_dim(block, 0, width, axis=dim), axis, backward)
        block = jnp.concatenate([low, block, high], axis=dim)
    return block


def passed_along(block, axis, distance):
    devices = range(lax.axis_size(axis))
    route = [(i - distance, i) for i in devices if i - distance in devices]
    return lax.ppermute(block, axis, route)


def window_mask(cell_rim, frames, tile_size):
    rim_span = 3 * tile_size
    offset = jnp.arange(rim_span)[None, :] - tile_size - jnp.arange(tile_size)[:, None]
    inside = jnp.abs(offset) <= tile_size
    key_ok = cell_rim == 1
    query_ok = key_ok[tile_size : 2 * tile_size, tile_size : 2 * tile_size]
    cell_pairs = (
        inside[:, None, :, None]
        & inside[None, :, None, :]
        & key_ok[None, None]
        & query_ok[:, :, None, None]
    )
    allowed = jnp.broadcast_to(
        cell_pairs[None, :, :, None], (frames, tile_size, tile_size, frames, rim_span, rim_span)
    )
    allowed = allowed.reshape(frames * tile_size * tile_size, frames * rim_span * rim_span)
    query_live = jnp.broadcast_to(query_ok[None], (frames, tile_size, tile_size)).reshape(-1)
    return (allowed, query_live)


def contract_last(left_rows, right_rows):
    return lax.dot_general(
        left_rows, right_rows, (((1,), (1,)), ((), ())), preferred_element_type=jnp.float32
    )


def contract_first(left_rows, right_rows):
    return lax.dot_general(
        left_rows, right_rows, (((0,), (0,)), ((), ())), preferred_element_type=jnp.float32
    )


def query_pass(query_rows, grad_rows, key_rows, value_rows, allowed, query_live, score_scale):
    scores = contract_last(query_rows, key_rows) * score_scale
    masked = jnp.where(allowed, scores, -jnp.inf)
    row_max = jnp.where(query_live, jnp.max(masked, axis=1), 0.0)
    unnormed = jnp.where(allowed, jnp.exp(scores - row_max[:, None]), 0.0)
    row_total = jnp.sum(unnormed, axis=1) + jnp.where(query_live, 0.0, 1.0)
    probs = unnormed / row_total[:, None]
    probs_low = probs.astype(jnp.bfloat16)
    attended = jnp.dot(probs_low, value_rows, preferred_element_type=jnp.float32)
    row_delta = jnp.sum(grad_rows.astype(jnp.float32) * attended, axis=1)
    dprobs = contract_last(grad_rows, value_rows)
    dscores_low = (probs * (dprobs - row_delta[:, None])).astype(jnp.bfloat16)
    query_part = jnp.dot(dscores_low, key_rows, preferred_element_type=jnp.float32) * score_scale
    return (probs_low, dscores_low, query_part, row_max, row_total, row_delta)


def local(queries, key_vectors, value_vectors, out_grad, cell_valid):
    tile_size = queries.shape[2]
    frames = queries.shape[1]
    width = queries.shape[-1]
    score_scale = 1.0 / math.sqrt(width)
    row_place = lax.axis_index("sy") * tile_size
    column_place = lax.axis_index("sx") * tile_size
    cell_rim = lax.dynamic_slice(
        jnp.pad(cell_valid, tile_size), (row_place, column_place), (3 * tile_size, 3 * tile_size)
    )
    allowed, query_live = window_mask(cell_rim, frames, tile_size)
    pair_local = jnp.stack([key_vectors, value_vectors], 1)
    pair_rims = extended(pair_local, (("sy", 3), ("sx", 4)), tile_size)

    def head_returned(inputs):
        query_head, grad_head, pair_rim = inputs
        query_rows = query_head.reshape(-1, width)
        grad_rows = grad_head.reshape(-1, width)
        probs_low, dscores_low, query_part, row_max, row_total, row_delta = query_pass(
            query_rows,
            grad_rows,
            pair_rim[0].reshape(-1, width),
            pair_rim[1].reshape(-1, width),
            allowed,
            query_live,
            score_scale,
        )
        key_part = (contract_first(dscores_low, query_rows) * score_scale).astype(jnp.bfloat16)
        value_part = contract_first(probs_low, grad_rows).astype(jnp.bfloat16)
        side_parts = jnp.stack([key_part, value_part]).reshape(pair_rim.shape)
        return (query_part.astype(jnp.bfloat16).reshape(query_head.shape), side_parts)

    query_grad, side_parts = lax.map(head_returned, (queries, out_grad, pair_rims))
    upper_band = side_parts[:, :, :, 0:tile_size]
    middle_rows = side_parts[:, :, :, tile_size : 2 * tile_size]
    lower_band = side_parts[:, :, :, 2 * tile_size : 3 * tile_size]
    below_parts = passed_along(upper_band, "sy", -1)
    above_parts = passed_along(lower_band, "sy", 1)
    row_sum = (
        middle_rows.astype(jnp.float32)
        + below_parts.astype(jnp.float32)
        + above_parts.astype(jnp.float32)
    )
    left_tile = row_sum[:, :, :, :, 0:tile_size]
    centre_tile = row_sum[:, :, :, :, tile_size : 2 * tile_size]
    right_tile = row_sum[:, :, :, :, 2 * tile_size : 3 * tile_size]
    right_parts = passed_along(left_tile, "sx", -1)
    left_parts = passed_along(right_tile, "sx", 1)
    side_total = centre_tile + right_parts + left_parts
    key_grad = side_total[:, 0].astype(jnp.bfloat16)
    value_grad = side_total[:, 1].astype(jnp.bfloat16)
    return (query_grad, key_grad, value_grad)


def solution(mesh):
    return jax.shard_map(
        local,
        mesh=mesh,
        in_specs=(
            P("tp", None, "sy", "sx", None),
            P("tp", None, "sy", "sx", None),
            P("tp", None, "sy", "sx", None),
            P("tp", None, "sy", "sx", None),
            P(),
        ),
        out_specs=(
            P("tp", None, "sy", "sx", None),
            P("tp", None, "sy", "sx", None),
            P("tp", None, "sy", "sx", None),
        ),
        check_vma=False,
    )
```

profile of v0, /device:TPU:1, one launch (start us, length us, event | category | flops | bytes accessed | tf_op | source)
XLA Modules:
  0.0 270.7 jit_solution(11856255851156721384)
XLA Ops:
  0.6 1.2 pad_maximum_fusion.2
  1.9 2.1 collective-permute-start.1
  3.9 4.5 %collective-permute-start = (bf16[6,2,4,8,8,128]{5,4,3,2,1,0:T(8,128)(2,1)S(1)}, bf16[6,2,4,8,8,128]{5,4,3,2,1,0:T(8,128)(2,1)S(1)}, u32[]{:S(2)}, u32[]{:S(2)}) collective-permute-start(bf16[6,2,4,8,8,128]{5,4,3,2,1,0:T(8,128)(2,1)S(1)} %pad_maximum_fusion.2), channel_id=1, source_target_pairs={{0,2},{2,4},{4,6},{1,3},{3,5},{5,7},{8,10},{10,12},{12,14},{9,11},... | collective-permute-start | bytes 2359304 | tf_op jit(solution)/shard_map/ppermute | solution.py:14
  8.4 7.7 %collective-permute-done.1 = bf16[6,2,4,8,8,128]{5,4,3,2,1,0:T(8,128)(2,1)S(1)} collective-permute-done((bf16[6,2,4,8,8,128]{5,4,3,2,1,0:T(8,128)(2,1)S(1)}, bf16[6,2,4,8,8,128]{5,4,3,2,1,0:T(8,128)(2,1)S(1)}, u32[]{:S(2)}, u32[]{:S(2)}) %collective-permute-start.1) | collective-permute-done | bytes 786464 | tf_op jit(solution)/shard_map/ppermute | solution.py:17
  16.2 1.2 collective-permute-done
  17.3 2.8 %pad_maximum_fusion.1 = bf16[6,2,4,24,8,128]{5,4,3,2,1,0:T(8,128)(2,1)} fusion(bf16[6,2,4,8,8,128]{5,4,3,2,1,0:T(8,128)(2,1)S(1)} %collective-permute-done.1, bf16[6,1,4,8,8,128]{5,4,3,2,1,0:T(8,128)(2,1)} %bitcast.78, bf16[6,1,4,8,8,128]{5,4,3,2,1,0:T(8,128)(2,1)} %bitcast.81, bf16[6,2,4,8,8,128]{5,4,3,2,1,0:T(8,128)(2,1)S(1)} %collective-permute-done), kind=kLoop, calls=%fused_computation.30 | loop fusion | flops 3538944 | bytes 4718592 | tf_op jit(solution)/shard_map/concatenate | solution.py:18
  20.1 1.3 collective-permute-start.3
  21.4 6.8 %collective-permute-start.2 = (bf16[6,2,4,24,8,128]{5,4,3,2,1,0:T(8,128)(2,1)}, bf16[6,2,4,24,8,128]{5,4,3,2,1,0:T(8,128)(2,1)}, u32[]{:S(2)}, u32[]{:S(2)}) collective-permute-start(bf16[6,2,4,24,8,128]{5,4,3,2,1,0:T(8,128)(2,1)} %pad_maximum_fusion.1), channel_id=1, source_target_pairs={{0,1},{2,3},{4,5},{6,7},{8,9},{10,11},{12,13},{14,15},{16,17},{18,... | collective-permute-start | bytes 7077896 | tf_op jit(solution)/shard_map/ppermute | solution.py:14
  28.8 38.2 %collective-permute-done.3 = bf16[6,2,4,24,8,128]{5,4,3,2,1,0:T(8,128)(2,1)} collective-permute-done((bf16[6,2,4,24,8,128]{5,4,3,2,1,0:T(8,128)(2,1)}, bf16[6,2,4,24,8,128]{5,4,3,2,1,0:T(8,128)(2,1)}, u32[]{:S(2)}, u32[]{:S(2)}) %collective-permute-start.3) | collective-permute-done | bytes 2359328 | tf_op jit(solution)/shard_map/ppermute | solution.py:17
  67.0 3.2 %collective-permute-done.2 = bf16[6,2,4,24,8,128]{5,4,3,2,1,0:T(8,128)(2,1)} collective-permute-done((bf16[6,2,4,24,8,128]{5,4,3,2,1,0:T(8,128)(2,1)}, bf16[6,2,4,24,8,128]{5,4,3,2,1,0:T(8,128)(2,1)}, u32[]{:S(2)}, u32[]{:S(2)}) %collective-permute-start.2) | collective-permute-done | bytes 2359328 | tf_op jit(solution)/shard_map/ppermute | solution.py:14
  70.2 6.1 %pad_maximum_fusion = bf16[6,2,4,24,24,128]{5,4,3,2,1,0:T(8,128)(2,1)} fusion(bf16[6,2,4,24,8,128]{5,4,3,2,1,0:T(8,128)(2,1)} %collective-permute-done.3, bf16[6,2,4,8,8,128]{5,4,3,2,1,0:T(8,128)(2,1)S(1)} %collective-permute-done.1, bf16[6,1,4,8,8,128]{5,4,3,2,1,0:T(8,128)(2,1)S(1)} %bitcast.79, bf16[6,1,4,8,8,128]{5,4,3,2,1,0:T(8,128)(2,1)S(1)} %bitcast.82, ...), kind=kLoop, calls=%fused_computation.28 | loop fusion | flops 42467328 | bytes 14155776 | tf_op jit(solution)/shard_map/concatenate | solution.py:18
  76.2 132.3 %while.13 = (s32[]{:T(128)}, bf16[6,4,8,8,128]{4,3,2,1,0:T(8,128)(2,1)}, bf16[6,2,4,24,24,128]{5,4,3,2,0,1:T(8,128)(2,1)}, bf16[6,4,8,8,128]{4,3,2,1,0:T(8,128)(...) while((s32[]{:T(128)}, ...), condition=%wide.region_4.5_spmd.clone, body=%wide.region_0.4_spmd.clone.sunk | while | flops 917635072 | bytes 39895592 | solution.py:108
  76.3 0.9 constant_dynamic-slice_fusion.6
  77.4 2.5 constant_dynamic-slice_fusion.7
  79.8 1.0 broadcast_in_dim.87
  80.8 8.7 %reshape.113 = pred[256,2304]{1,0:T(32,128)(4,1)} reshape(pred[4,8,8,4,24,24]{5,4,3,2,1,0:T(8,128)(4,1)S(1)} %broadcast_in_dim.87) | data formatting | bytes 1179648 | tf_op jit(solution)/shard_map/reshape | solution.py:43
  89.5 2.0 select_reduce_fusion.2
  92.2 0.8 fusion.61
  97.1 1.2 fusion.66
  98.4 0.9 constant_dynamic-slice_fusion.6
  99.4 2.5 constant_dynamic-slice_fusion.7
  101.8 1.0 broadcast_in_dim.87
  102.9 8.7 %reshape.113 = pred[256,2304]{1,0:T(32,128)(4,1)} reshape(pred[4,8,8,4,24,24]{5,4,3,2,1,0:T(8,128)(4,1)S(1)} %broadcast_in_dim.87) | data formatting | bytes 1179648 | tf_op jit(solution)/shard_map/reshape | solution.py:43
  111.6 2.0 select_reduce_fusion.2
  119.1 1.2 fusion.66
  120.4 0.9 constant_dynamic-slice_fusion.6
  121.4 2.5 constant_dynamic-slice_fusion.7
  123.9 1.0 broadcast_in_dim.87
  124.9 8.7 %reshape.113 = pred[256,2304]{1,0:T(32,128)(4,1)} reshape(pred[4,8,8,4,24,24]{5,4,3,2,1,0:T(8,128)(4,1)S(1)} %broadcast_in_dim.87) | data formatting | bytes 1179648 | tf_op jit(solution)/shard_map/reshape | solution.py:43
  133.6 2.0 select_reduce_fusion.2
  136.3 0.8 fusion.61
  141.1 1.3 fusion.66
  142.5 0.9 constant_dynamic-slice_fusion.6
  143.5 2.5 constant_dynamic-slice_fusion.7
  146.0 1.0 broadcast_in_dim.87
  147.0 8.7 %reshape.113 = pred[256,2304]{1,0:T(32,128)(4,1)} reshape(pred[4,8,8,4,24,24]{5,4,3,2,1,0:T(8,128)(4,1)S(1)} %broadcast_in_dim.87) | data formatting | bytes 1179648 | tf_op jit(solution)/shard_map/reshape | solution.py:43
  155.7 2.0 select_reduce_fusion.2
  158.4 0.8 fusion.61
  163.2 1.3 fusion.66
  164.6 0.9 constant_dynamic-slice_fusion.6
  165.6 2.5 constant_dynamic-slice_fusion.7
  168.1 1.0 broadcast_in_dim.87
  169.1 8.7 %reshape.113 = pred[256,2304]{1,0:T(32,128)(4,1)} reshape(pred[4,8,8,4,24,24]{5,4,3,2,1,0:T(8,128)(4,1)S(1)} %broadcast_in_dim.87) | data formatting | bytes 1179648 | tf_op jit(solution)/shard_map/reshape | solution.py:43
  177.8 2.0 select_reduce_fusion.2
  180.5 0.8 fusion.61
  185.3 1.3 fusion.66
  186.7 0.9 constant_dynamic-slice_fusion.6
  187.7 2.5 constant_dynamic-slice_fusion.7
  190.2 1.0 broadcast_in_dim.87
  191.2 8.7 %reshape.113 = pred[256,2304]{1,0:T(32,128)(4,1)} reshape(pred[4,8,8,4,24,24]{5,4,3,2,1,0:T(8,128)(4,1)S(1)} %broadcast_in_dim.87) | data formatting | bytes 1179648 | tf_op jit(solution)/shard_map/reshape | solution.py:43
  199.9 2.0 select_reduce_fusion.2
  202.6 0.8 fusion.61
  207.4 1.2 fusion.66
  208.6 3.2 %fusion.17 = (bf16[6,2,4,8,24,128]{5,4,3,2,0,1:T(8,128)(2,1)S(1)}, bf16[6,2,4,8,24,128]{5,4,3,2,0,1:T(8,128)(2,1)S(1)}) fusion(bf16[6,2,4,24,24,128]{5,4,3,2,0,1:T(8,128)(2,1)} %get-tuple-element.47), kind=kLoop, calls=%fused_computation.42 | loop fusion | bytes 9437184 | tf_op jit(solution)/shard_map/slice | solution.py:109
  211.8 1.9 collective-permute-start.4
  213.8 3.7 %collective-permute-start.5 = (bf16[6,2,4,8,24,128]{5,4,3,2,0,1:T(8,128)(2,1)S(1)}, bf16[6,2,4,8,24,128]{5,4,3,2,0,1:T(8,128)(2,1)S(1)}, u32[]{:S(2)}, u32[]{:S(2)}) collective-permute-start(bf16[6,2,4,8,24,128]{5,4,3,2,0,1:T(8,128)(2,1)S(1)} %get-tuple-element.100), channel_id=1, source_target_pairs={{0,2},{2,4},{4,6},{1,3},{3,5},{5,7},{8,10},{10,12},{12,14},{9,11},... | collective-permute-start | bytes 7077896 | tf_op jit(solution)/shard_map/ppermute | solution.py:25
  217.4 24.9 %collective-permute-done.4 = bf16[6,2,4,8,24,128]{5,4,3,2,0,1:T(8,128)(2,1)S(1)} collective-permute-done((bf16[6,2,4,8,24,128]{5,4,3,2,0,1:T(8,128)(2,1)S(1)}, bf16[6,2,4,8,24,128]{5,4,3,2,0,1:T(8,128)(2,1)S(1)}, u32[]{:S(2)}, u32[]{:S(2)}) %collective-permute-start.4) | collective-permute-done | bytes 2359328 | tf_op jit(solution)/shard_map/ppermute | solution.py:25
  242.3 0.9 collective-permute-done.5
  243.2 2.8 %convert_add_fusion = f32[6,2,4,8,24,128]{5,4,3,2,0,1:T(8,128)S(1)} fusion(bf16[6,2,4,8,24,128]{5,4,3,2,0,1:T(8,128)(2,1)S(1)} %collective-permute-done.5, bf16[6,2,4,8,24,128]{5,4,3,2,0,1:T(8,128)(2,1)S(1)} %collective-permute-done.4, bf16[6,2,4,24,24,128]{5,4,3,2,0,1:T(8,128)(2,1)} %get-tuple-element.47), kind=kLoop, calls=%fused_computation.29 | loop fusion | flops 5898240 | bytes 11796480 | tf_op jit(solution)/shard_map/add | solution.py:115
  246.5 1.3 collective-permute-start.6
  247.8 4.3 %collective-permute-start.7 = (f32[6,2,4,8,8,128]{5,4,3,2,0,1:T(8,128)S(1)}, f32[6,2,4,8,8,128]{5,4,3,2,0,1:T(8,128)S(1)}, u32[]{:S(2)}, u32[]{:S(2)}) collective-permute-start(f32[6,2,4,8,8,128]{5,4,3,2,0,1:T(8,128)S(1)} %get-tuple-element.102), channel_id=1, source_target_pairs={{0,1},{2,3},{4,5},{6,7},{8,9},{10,11},{12,13},{14,15},{16,17},{18,... | collective-permute-start | bytes 4718600 | tf_op jit(solution)/shard_map/ppermute | solution.py:25
  252.1 15.7 %collective-permute-done.6 = f32[6,2,4,8,8,128]{5,4,3,2,0,1:T(8,128)S(1)} collective-permute-done((f32[6,2,4,8,8,128]{5,4,3,2,0,1:T(8,128)S(1)}, f32[6,2,4,8,8,128]{5,4,3,2,0,1:T(8,128)S(1)}, u32[]{:S(2)}, u32[]{:S(2)}) %collective-permute-start.6) | collective-permute-done | bytes 1572896 | tf_op jit(solution)/shard_map/ppermute | solution.py:25
  267.8 1.6 collective-permute-done.7
  269.7 0.9 slice_bitcast_fusion
  (125 shorter events, 31.4 us)
Async XLA Ops:
  1.8 26.4 %copy-start.5 = (s32[32,16]{0,1:T(8,128)S(1)}, s32[32,16]{0,1:T(8,128)}, u32[]{:S(2)}) copy-start(s32[32,16]{0,1:T(8,128)} %param.11) | copy-start | bytes 6148
  1.8 68.3 %copy-start.3 = (bf16[6,4,8,8,128]{4,3,2,1,0:T(8,128)(2,1)S(1)}, bf16[6,4,8,8,128]{4,3,2,1,0:T(8,128)(2,1)}, u32[]{:S(2)}) copy-start(bf16[6,4,8,8,128]{4,3,2,1,0:T(8,128)(2,1)} %param.9) | copy-start | bytes 1179652
  1.9 68.3 %copy-start.4 = (bf16[6,4,8,8,128]{4,3,2,1,0:T(8,128)(2,1)S(1)}, bf16[6,4,8,8,128]{4,3,2,1,0:T(8,128)(2,1)}, u32[]{:S(2)}) copy-start(bf16[6,4,8,8,128]{4,3,2,1,0:T(8,128)(2,1)} %param.8) | copy-start | bytes 1179652
  1.9 14.3 %collective-permute-start.1 = (bf16[6,2,4,8,8,128]{5,4,3,2,1,0:T(8,128)(2,1)S(1)}, bf16[6,2,4,8,8,128]{5,4,3,2,1,0:T(8,128)(2,1)S(1)}, u32[]{:S(2)}, u32[]{:S(2)}) collective-permute-start(bf16[6,2,4,8,8,128]{5,4,3,2,1,0:T(8,128)(2,1)S(1)} %pad_maximum_fusion.2), channel_id=1, source_target_pairs={{2,0},{4,2},{6,4},{3,1},{5,3},{7,5},{10,8},{12,10},{14,12},{11,9},... | collective-permute-start | bytes 2359304 | tf_op jit(solution)/shard_map/ppermute | solution.py:17
  3.9 13.4 %collective-permute-start = (bf16[6,2,4,8,8,128]{5,4,3,2,1,0:T(8,128)(2,1)S(1)}, bf16[6,2,4,8,8,128]{5,4,3,2,1,0:T(8,128)(2,1)S(1)}, u32[]{:S(2)}, u32[]{:S(2)}) collective-permute-start(bf16[6,2,4,8,8,128]{5,4,3,2,1,0:T(8,128)(2,1)S(1)} %pad_maximum_fusion.2), channel_id=1, source_target_pairs={{0,2},{2,4},{4,6},{1,3},{3,5},{5,7},{8,10},{10,12},{12,14},{9,11},... | collective-permute-start | bytes 2359304 | tf_op jit(solution)/shard_map/ppermute | solution.py:14
  20.1 46.9 %collective-permute-start.3 = (bf16[6,2,4,24,8,128]{5,4,3,2,1,0:T(8,128)(2,1)}, bf16[6,2,4,24,8,128]{5,4,3,2,1,0:T(8,128)(2,1)}, u32[]{:S(2)}, u32[]{:S(2)}) collective-permute-start(bf16[6,2,4,24,8,128]{5,4,3,2,1,0:T(8,128)(2,1)} %pad_maximum_fusion.1), channel_id=1, source_target_pairs={{1,0},{3,2},{5,4},{7,6},{9,8},{11,10},{13,12},{15,14},{17,16},{19,... | collective-permute-start | bytes 7077896 | tf_op jit(solution)/shard_map/ppermute | solution.py:17
  21.4 48.8 %collective-permute-start.2 = (bf16[6,2,4,24,8,128]{5,4,3,2,1,0:T(8,128)(2,1)}, bf16[6,2,4,24,8,128]{5,4,3,2,1,0:T(8,128)(2,1)}, u32[]{:S(2)}, u32[]{:S(2)}) collective-permute-start(bf16[6,2,4,24,8,128]{5,4,3,2,1,0:T(8,128)(2,1)} %pad_maximum_fusion.1), channel_id=1, source_target_pairs={{0,1},{2,3},{4,5},{6,7},{8,9},{10,11},{12,13},{14,15},{16,17},{18,... | collective-permute-start | bytes 7077896 | tf_op jit(solution)/shard_map/ppermute | solution.py:14
  89.5 2.0 copy-start
  92.2 1.1 copy-start.1
  94.4 1.1 copy-start.2
  111.6 2.0 copy-start
  114.2 1.1 copy-start.1
  116.4 1.1 copy-start.2
  133.6 2.0 copy-start
  136.3 1.1 copy-start.1
  138.4 1.1 copy-start.2
  155.7 2.0 copy-start
  158.4 1.1 copy-start.1
  160.5 1.1 copy-start.2
  177.8 2.0 copy-start
  180.5 1.1 copy-start.1
  182.6 1.1 copy-start.2
  199.9 2.0 copy-start
  202.5 1.1 copy-start.1
  204.7 1.1 copy-start.2
  211.8 30.5 %collective-permute-start.4 = (bf16[6,2,4,8,24,128]{5,4,3,2,0,1:T(8,128)(2,1)S(1)}, bf16[6,2,4,8,24,128]{5,4,3,2,0,1:T(8,128)(2,1)S(1)}, u32[]{:S(2)}, u32[]{:S(2)}) collective-permute-start(bf16[6,2,4,8,24,128]{5,4,3,2,0,1:T(8,128)(2,1)S(1)} %get-tuple-element.99), channel_id=1, source_target_pairs={{2,0},{4,2},{6,4},{3,1},{5,3},{7,5},{10,8},{12,10},{14,12},{11,9},... | collective-permute-start | bytes 7077896 | tf_op jit(solution)/shard_map/ppermute | solution.py:25
  213.8 29.5 %collective-permute-start.5 = (bf16[6,2,4,8,24,128]{5,4,3,2,0,1:T(8,128)(2,1)S(1)}, bf16[6,2,4,8,24,128]{5,4,3,2,0,1:T(8,128)(2,1)S(1)}, u32[]{:S(2)}, u32[]{:S(2)}) collective-permute-start(bf16[6,2,4,8,24,128]{5,4,3,2,0,1:T(8,128)(2,1)S(1)} %get-tuple-element.100), channel_id=1, source_target_pairs={{0,2},{2,4},{4,6},{1,3},{3,5},{5,7},{8,10},{10,12},{12,14},{9,11},... | collective-permute-start | bytes 7077896 | tf_op jit(solution)/shard_map/ppermute | solution.py:25
  246.5 21.3 %collective-permute-start.6 = (f32[6,2,4,8,8,128]{5,4,3,2,0,1:T(8,128)S(1)}, f32[6,2,4,8,8,128]{5,4,3,2,0,1:T(8,128)S(1)}, u32[]{:S(2)}, u32[]{:S(2)}) collective-permute-start(f32[6,2,4,8,8,128]{5,4,3,2,0,1:T(8,128)S(1)} %get-tuple-element.101), channel_id=1, source_target_pairs={{1,0},{3,2},{5,4},{7,6},{9,8},{11,10},{13,12},{15,14},{17,16},{19,... | collective-permute-start | bytes 4718600 | tf_op jit(solution)/shard_map/ppermute | solution.py:25
  247.8 21.6 %collective-permute-start.7 = (f32[6,2,4,8,8,128]{5,4,3,2,0,1:T(8,128)S(1)}, f32[6,2,4,8,8,128]{5,4,3,2,0,1:T(8,128)S(1)}, u32[]{:S(2)}, u32[]{:S(2)}) collective-permute-start(f32[6,2,4,8,8,128]{5,4,3,2,0,1:T(8,128)S(1)} %get-tuple-element.102), channel_id=1, source_target_pairs={{0,1},{2,3},{4,5},{6,7},{8,9},{10,11},{12,13},{14,15},{16,17},{18,... | collective-permute-start | bytes 4718600 | tf_op jit(solution)/shard_map/ppermute | solution.py:25
where the time goes:
time: 275 us; the launch traced here: 271 us
  waiting for transfers between devices  93.3 us (34%)
  local copies, waits for them, and re-layouts  92.9 us (34%)
  other arithmetic  30.2 us (11%)
  matrix products  27.1 us (10%)
  starting transfers between devices  25.8 us (9%)
    reshape x6, local copies, waits for them, and re-layouts, window_mask(): allowed.reshape(frames * tile_size * tile_size, frames * rim_span * rim_s...  52.2 us
    ppermute x2, waiting for transfers between devices, extended(): lax.ppermute(lax.slice_in_dim(block, 0, width, axis=dim), axis, backward)  46 us
    ppermute x4, waiting for transfers between devices, passed_along(): return lax.ppermute(block, axis, route)  43 us
    slice x6, local copies, waits for them, and re-layouts, head_returned(): pair_rim[1].reshape(-1, width)  14.8 us
    dot_general x12, matrix products, contract_last(): lax.dot_general(left_rows, right_rows, (((1,), (1,)), ((), ())), preferre...  14.7 us
    ppermute x2, starting transfers between devices, extended(): lax.ppermute(lax.slice_in_dim(block, block.shape[dim] - width, None, axis...  11.3 us
    ppermute x4, starting transfers between devices, passed_along(): return lax.ppermute(block, axis, route)  11.2 us
    concatenate x2, other arithmetic, extended(): block = jnp.concatenate([low, block, high], axis=dim)  8.84 us
  transfers between devices with their start and end apart: 8, of which 8 were waited for; matrix products, arithmetic and copies ran while one was open for 0% of the time, Pallas kernels for 0%

commit v1 on v0

--- a/solution.py
+++ b/solution.py
@@ -1,9 +1,15 @@
+import functools
 import math
 
 import jax
 import jax.numpy as jnp
 from jax import lax
+from jax.experimental import pallas as pl
+from jax.experimental.pallas import tpu as pltpu
 from jax.sharding import PartitionSpec as P
+
+MASKED = -1e30
+VMEM_SPEC = pl.BlockSpec(memory_space=pltpu.VMEM)
 
 
 def extended(block, sides, width):
@@ -73,7 +79,7 @@
     return (probs_low, dscores_low, query_part, row_max, row_total, row_delta)
 
 
-def local(queries, key_vectors, value_vectors, out_grad, cell_valid):
+def general(queries, key_vectors, value_vectors, out_grad, cell_valid):
     tile_size = queries.shape[2]
     frames = queries.shape[1]
     width = queries.shape[-1]
@@ -127,6 +133,194 @@
     return (query_grad, key_grad, value_grad)
 
 
+def pairs_of(count, first):
+    low = range(first, count - 1, 2)
+    return [(i, i + 1) for i in low] + [(i + 1, i) for i in low]
+
+
+def bias_kernel(tile_size, place_ref, valid_ref, bias_ref):
+    valid = valid_ref[...] == 1
+    rows = lax.broadcasted_iota(jnp.int32, valid.shape, 0)
+    columns = lax.broadcasted_iota(jnp.int32, valid.shape, 1)
+    far = max(valid.shape)
+    top = jnp.min(jnp.where(valid, rows, far))
+    bottom = jnp.max(jnp.where(valid, rows, -1))
+    left = jnp.min(jnp.where(valid, columns, far))
+    right = jnp.max(jnp.where(valid, columns, -1))
+    shape = bias_ref.shape[2:]
+    key_cell = lax.broadcasted_iota(jnp.int32, shape, 0)
+    query_cell = lax.broadcasted_iota(jnp.int32, shape, 1) % (tile_size * tile_size)
+    key_row, key_column = key_cell // tile_size, key_cell % tile_size
+    query_row, query_column = query_cell // tile_size, query_cell % tile_size
+
+    def inside(row, column):
+        return (row >= top) & (row <= bottom) & (column >= left) & (column <= right)
+
+    for b in range(2):
+        q_row = query_row + place_ref[0] * tile_size
+        q_column = query_column + place_ref[3 + b] * tile_size
+        q_ok = inside(q_row, q_column)
+        for t in range(6):
+            k_row = key_row + place_ref[t // 2] * tile_size
+            k_column = key_column + place_ref[3 + t % 2] * tile_size
+            near = (jnp.abs(k_row - q_row) <= tile_size) & (
+                jnp.abs(k_column - q_column) <= tile_size
+            )
+            ok = near & q_ok & inside(k_row, k_column)
+            bias_ref[b, t] = jnp.where(ok, 0.0, MASKED)
+
+
+def window_bias(places, cell_valid, tile_size):
+    cells = tile_size * tile_size
+    return pl.pallas_call(
+        functools.partial(bias_kernel, tile_size),
+        out_shape=jax.ShapeDtypeStruct((2, 6, cells, 2 * cells), jnp.float32),
+        in_specs=[pl.BlockSpec(memory_space=pltpu.SMEM), VMEM_SPEC],
+        out_specs=VMEM_SPEC,
+        name="window_bias",
+    )(places, cell_valid)
+
+
+def head_kernel(
+    own_ref, partner_ref, even_ref, odd_ref, bias_ref,
+    own_dq_ref, partner_dq_ref, middle_ref, even_part_ref, odd_part_ref,
+    score_ref, dprob_ref, key_sum_ref, value_sum_ref,
+):
+    tokens, width = own_ref.shape[1:]
+    score_scale = 1.0 / math.sqrt(width)
+    exponent_scale = math.log2(math.e) / math.sqrt(width)
+    keys = [own_ref.at[0], partner_ref.at[0], even_ref.at[0], even_ref.at[2], odd_ref.at[0], odd_ref.at[2]]
+    values = [own_ref.at[1], partner_ref.at[1], even_ref.at[1], even_ref.at[3], odd_ref.at[1], odd_ref.at[3]]
+    key_parts = [middle_ref.at[0], middle_ref.at[2], even_part_ref.at[0], even_part_ref.at[2], odd_part_ref.at[0], odd_part_ref.at[2]]
+    value_parts = [middle_ref.at[1], middle_ref.at[3], even_part_ref.at[1], even_part_ref.at[3], odd_part_ref.at[1], odd_part_ref.at[3]]
+    for b, (side, dq_ref) in enumerate(((own_ref, own_dq_ref), (partner_ref, partner_dq_ref))):
+        query_rows = side[2]
+        grad_rows = side[3]
+        row_max = None
+        for t in range(6):
+            bias = bias_ref[b, t]
+            bias = jnp.concatenate([bias] * (tokens // bias.shape[1]), axis=1)
+            bias = jnp.concatenate([bias] * (tokens // bias.shape[0]), axis=0)
+            scores = contract_last(keys[t][...], query_rows) + bias
+            score_ref[t] = scores
+            tile_max = jnp.max(scores, axis=0, keepdims=True)
+            row_max = tile_max if row_max is None else jnp.maximum(row_max, tile_max)
+        live = row_max > 0.5 * MASKED
+        row_max = jnp.where(live, row_max, 0.0)
+        row_total = jnp.where(live, 0.0, 1.0)
+        row_delta = jnp.zeros_like(row_max)
+        for t in range(6):
+            unnormed = jnp.exp2((score_ref[t] - row_max) * exponent_scale)
+            dprobs = contract_last(values[t][...], grad_rows)
+            score_ref[t] = unnormed
+            dprob_ref[t] = dprobs
+            row_total = row_total + jnp.sum(unnormed, axis=0, keepdims=True)
+            row_delta = row_delta + jnp.sum(unnormed * dprobs, axis=0, keepdims=True)
+        inverse = 1.0 / row_total
+        row_delta = row_delta * inverse
+        query_grad = None
+        for t in range(6):
+            probs = score_ref[t] * inverse
+            dscores_low = (probs * (dprob_ref[t] - row_delta)).astype(jnp.bfloat16)
+            value_part = jnp.dot(
+                probs.astype(jnp.bfloat16), grad_rows, preferred_element_type=jnp.float32
+            )
+            key_part = jnp.dot(dscores_low, query_rows, preferred_element_type=jnp.float32)
+            if b == 0:
+                key_sum_ref[t] = key_part
+                value_sum_ref[t] = value_part
+            else:
+                key_total = (key_sum_ref[t] + key_part) * score_scale
+                key_parts[t][...] = key_total.astype(middle_ref.dtype if t < 2 else jnp.bfloat16)
+                value_total = value_sum_ref[t] + value_part
+                value_parts[t][...] = value_total.astype(middle_ref.dtype if t < 2 else jnp.bfloat16)
+            query_part = contract_first(dscores_low, keys[t][...])
+            query_grad = query_part if query_grad is None else query_grad + query_part
+        dq_ref[...] = (query_grad * score_scale).astype(jnp.bfloat16)
+
+
+def head_grads(own, partner, even, odd, bias):
+    tokens, width = own.shape[1:]
+    low = jnp.bfloat16
+    pairs = 2 * 6 * tokens * tokens
+    return pl.pallas_call(
+        head_kernel,
+        out_shape=(
+            jax.ShapeDtypeStruct((tokens, width), low),
+            jax.ShapeDtypeStruct((tokens, width), low),
+            jax.ShapeDtypeStruct((4, tokens, width), jnp.float32),
+            jax.ShapeDtypeStruct((4, tokens, width), low),
+            jax.ShapeDtypeStruct((4, tokens, width), low),
+        ),
+        in_specs=[VMEM_SPEC] * 5,
+        out_specs=[VMEM_SPEC] * 5,
+        scratch_shapes=[
+            pltpu.VMEM((6, tokens, tokens), jnp.float32),
+            pltpu.VMEM((6, tokens, tokens), jnp.float32),
+            pltpu.VMEM((6, tokens, width), jnp.float32),
+            pltpu.VMEM((6, tokens, width), jnp.float32),
+        ],
+        cost_estimate=pl.CostEstimate(
+            flops=10 * pairs * width, transcendentals=pairs, bytes_accessed=20 * tokens * width * 2
+        ),
+        name="head_grads",
+    )(own, partner, even, odd, bias)
+
+
+def swapped(queries, key_vectors, value_vectors, out_grad, cell_valid):
+    heads, frames, tile_size, _, width = queries.shape
+    tokens = frames * tile_size * tile_size
+    half = heads // 2
+    rows = lax.axis_size("sy")
+    row, column = lax.axis_index("sy"), lax.axis_index("sx")
+    swap = [(0, 1), (1, 0)]
+    even_pairs, odd_pairs = pairs_of(rows, 0), pairs_of(rows, 1)
+    arrays = [a.reshape(heads, tokens, width) for a in (key_vectors, value_vectors, queries, out_grad)]
+
+    def one_head(index):
+        return jnp.concatenate(
+            [lax.dynamic_slice_in_dim(a, index, 1, axis=0) for a in arrays], axis=0
+        )
+
+    even_row = row + 1 - 2 * (row % 2)
+    odd_row = row - 1 + 2 * (row % 2)
+    places = jnp.stack([row, even_row, odd_row, column, 1 - column]).astype(jnp.int32)
+    received = [lax.ppermute(one_head((1 - column) * half + h), "sx", swap) for h in range(half)]
+    bias = window_bias(places, cell_valid, tile_size)
+    local_grads, returned = [], []
+    for h in range(half):
+        own = one_head(column * half + h)
+        halo = jnp.concatenate([own[:2], received[h][:2]], axis=0)
+        even = lax.ppermute(halo, "sy", even_pairs)
+        odd = lax.ppermute(halo, "sy", odd_pairs)
+        own_dq, partner_dq, middle, even_part, odd_part = head_grads(
+            own, received[h], even, odd, bias
+        )
+        even_back = lax.ppermute(even_part, "sy", even_pairs)
+        odd_back = lax.ppermute(odd_part, "sy", odd_pairs)
+        total = middle + even_back.astype(jnp.float32) + odd_back.astype(jnp.float32)
+        total = total.astype(jnp.bfloat16)
+        local_grads.append(jnp.concatenate([own_dq[None], total[:2]], axis=0))
+        outgoing = jnp.concatenate([partner_dq[None], total[2:]], axis=0)
+        returned.append(lax.ppermute(outgoing, "sx", swap))
+    first = column == 0
+    outs = []
+    for i in range(3):
+        mine = jnp.stack([g[i] for g in local_grads])
+        theirs = jnp.stack([g[i] for g in returned])
+        out = jnp.concatenate(
+            [jnp.where(first, mine, theirs), jnp.where(first, theirs, mine)], axis=0
+        )
+        outs.append(out.reshape(queries.shape))
+    return tuple(outs)
+
+
+def local(queries, *rest):
+    if lax.axis_size("sx") == 2 and queries.shape[0] % 2 == 0:
+        return swapped(queries, *rest)
+    return general(queries, *rest)
+
+
 def solution(mesh):
     return jax.shard_map(
         local,

time: 275 us -> 74.7 us (0.27); the launches traced: 271 us -> 74.1 us
  local copies, waits for them, and re-layouts: 92.9 us -> 8.12 us
  waiting for transfers between devices: 93.3 us -> 12.6 us
  matrix products: 27.1 us -> 0 us
  other arithmetic: 30.2 us -> 5.29 us
  Pallas kernels: 0 us -> 18.3 us
  starting transfers between devices: 25.8 us -> 28.7 us
    ppermute x8 -> x18, waiting for transfers between devices: 93.3 us -> 12.6 us  [the longest x3 7.11 us: swapped(): returned.append(lax.ppermute(outgoing, 'sx', swap))]
    reshape x18 -> x0, local copies, waits for them, and re-layouts: 53.4 us -> none  [the longest x6 52.2 us: window_mask(): allowed.reshape(frames * tile_size * tile_size, frames * rim_span * rim_s...]
    dot_general x36 -> x0, matrix products: 27.1 us -> none  [the longest x12 14.7 us: contract_last(): lax.dot_general(left_rows, right_rows, (((1,), (1,)), ((), ())), preferre...]
    slice x9 -> x12, local copies, waits for them, and re-layouts: 18.6 us -> 0.13 us  [the longest x3 0.04 us: swapped(): theirs = jnp.stack([g[i] for g in returned])]
    pallas_call x0 -> x4, Pallas kernels: none -> 18.3 us  [the longest x3 16.4 us: head_grads(): pl.pallas_call(head_kernel, out_shape=(jax.ShapeDtypeStruct((tokens, widt...]
    dynamic_update_slice x6 -> x0, other arithmetic: 7.52 us -> none  [local(): lax.map(head_returned, (queries, out_grad, pair_rims))]
    broadcast_in_dim x12 -> x0, local copies, waits for them, and re-layouts: 6.03 us -> none  [the longest x6 6.02 us: window_mask(): jnp.broadcast_to(cell_pairs[None, :, :, None], (frames, tile_size, tile_s...]
    unnamed x7 -> x43, local copies, waits for them, and re-layouts: 0.09 us -> 5.98 us
  transfers between devices with their start and end apart: 8 -> 18, of which waited for: 8 -> 5; matrix products, arithmetic and copies ran while one was open for 0% -> 6% of each run, Pallas kernels for 0% -> 25%
where the time goes in v1:
time: 74.7 us; the launch traced here: 74.1 us
  starting transfers between devices  28.7 us (38%)
  Pallas kernels  18.3 us (24%)
  waiting for transfers between devices  12.6 us (17%)
  local copies, waits for them, and re-layouts  8.12 us (11%)
  other arithmetic  5.29 us (7%)
  between operations  1.1 us (1%)
    pallas_call x3, Pallas kernels, head_grads(): pl.pallas_call(head_kernel, out_shape=(jax.ShapeDtypeStruct((tokens, widt...  16.4 us
    ppermute x3, starting transfers between devices, swapped(): odd = lax.ppermute(halo, 'sy', odd_pairs)  12.2 us
    ppermute x3, starting transfers between devices, swapped(): odd_back = lax.ppermute(odd_part, 'sy', odd_pairs)  9.37 us
    ppermute x3, waiting for transfers between devices, swapped(): returned.append(lax.ppermute(outgoing, 'sx', swap))  7.11 us
    unnamed x43, local copies, waits for them, and re-layouts  5.98 us
    ppermute x3, waiting for transfers between devices, swapped(): lax.ppermute(one_head((1 - column) * half + h), 'sx', swap)  4.34 us
    ppermute x3, starting transfers between devices, swapped(): lax.ppermute(one_head((1 - column) * half + h), 'sx', swap)  3.72 us
    ppermute x3, starting transfers between devices, swapped(): returned.append(lax.ppermute(outgoing, 'sx', swap))  2.92 us
  transfers between devices with their start and end apart: 18, of which 5 were waited for; matrix products, arithmetic and copies ran while one was open for 6% of the time, Pallas kernels for 25%

profile of v1, /device:TPU:1, one launch (start us, length us, event | category | flops | bytes accessed | tf_op | source)
XLA Modules:
  0.0 74.1 jit_solution(4067383661819807542)
XLA Ops:
  0.7 1.3 %constant_dynamic-slice_fusion.16 = (bf16[1,256,128]{2,1,0:T(8,128)(2,1)S(1)}, bf16[1,256,128]{2,1,0:T(8,128)(2,1)S(1)}, bf16[1,256,128]{2,1,0:T(8,128)(2,1)S(1)...) fusion(bf16[6,256,128]{2,1,0:T(8,128)(2,1)} %bitcast.30, ...), kind=kLoop, calls=%fused_computation.49 | loop fusion | bytes 1572888 | tf_op jit(solution)/shard_map/dynamic_slice | solution.py:282
  1.9 0.0 copy-done.3
  2.0 0.1 copy-done.4
  2.1 0.1 constant_dynamic-slice_fusion.18
  2.2 2.1 %collective-permute-start.3 = (bf16[4,256,128]{2,1,0:T(8,128)(2,1)S(1)}, bf16[4,256,128]{2,1,0:T(8,128)(2,1)S(1)}, u32[]{:S(2)}, u32[]{:S(2)}) collective-permute-start(bf16[4,256,128]{2,1,0:T(8,128)(2,1)S(1)} %pad_maximum_fusion.9), channel_id=1, source_target_pairs={{0,1},{1,0},{2,3},{3,2},{4,5},{5,4},{6,7},{7,6},{8,9},{9,8},{10,11... | collective-permute-start | bytes 786440 | tf_op jit(solution)/shard_map/ppermute | solution.py:288
  4.4 0.1 collective-permute-start.6
  4.5 1.5 %collective-permute-start = (bf16[4,256,128]{2,1,0:T(8,128)(2,1)S(1)}, bf16[4,256,128]{2,1,0:T(8,128)(2,1)S(1)}, u32[]{:S(2)}, u32[]{:S(2)}) collective-permute-start(bf16[4,256,128]{2,1,0:T(8,128)(2,1)S(1)} %pad_maximum_fusion.5), channel_id=1, source_target_pairs={{0,1},{1,0},{2,3},{3,2},{4,5},{5,4},{6,7},{7,6},{8,9},{9,8},{10,11... | collective-permute-start | bytes 786440 | tf_op jit(solution)/shard_map/ppermute | solution.py:288
  6.0 4.3 %collective-permute-done.3.partner_ref = bf16[4,256,128]{2,1,0:T(8,128)(2,1)S(1)} collective-permute-done((bf16[4,256,128]{2,1,0:T(8,128)(2,1)S(1)}, bf16[4,256,128]{2,1,0:T(8,128)(2,1)S(1)}, u32[]{:S(2)}, u32[]{:S(2)}) %collective-permute-start.3) | collective-permute-done | bytes 262176 | tf_op jit(solution)/shard_map/ppermute | solution.py:288
  10.3 0.8 %pad_maximum_fusion.10 = (bf16[4,256,128]{2,1,0:T(8,128)(2,1)S(1)}, bf16[4,256,128]{2,1,0:T(8,128)(2,1)}) fusion(bf16[2,256,128]{2,1,0:T(8,128)(2,1)S(1)} %slice.100, bf16[1,256,128]{2,1,0:T(8,128)(2,1)S(1)} %get-tuple-element.49, bf16[1,256,128]{2,1,0:T(8,128)(2,1)S(1)} %get-tuple-element.91, bf16[1,256,128]{2,1,0:T(8,128)(2,1)S(1)} %get-tuple-element.61, ...), kind=kLoop, calls=%fused_computation.13 | loop fusion | flops 524288 | bytes 917504 | tf_op jit(solution)/shard_map/concatenate | solution.py:293
  11.1 5.6 %collective-permute-start.5 = (bf16[4,256,128]{2,1,0:T(8,128)(2,1)S(1)}, bf16[4,256,128]{2,1,0:T(8,128)(2,1)S(1)}, u32[]{:S(2)}, u32[]{:S(2)}) collective-permute-start(bf16[4,256,128]{2,1,0:T(8,128)(2,1)S(1)} %get-tuple-element.80), channel_id=1, source_target_pairs={{2,4},{4,2},{3,5},{5,3},{10,12},{12,10},{11,13},{13,11},{18,20},{2... | collective-permute-start | bytes 786440 | tf_op jit(solution)/shard_map/ppermute | solution.py:295
  16.7 0.1 collective-permute-start.4
  16.8 0.0 copy-start.6
  16.9 0.8 %pad_maximum_fusion.14 = (bf16[4,256,128]{2,1,0:T(8,128)(2,1)S(1)}, bf16[4,256,128]{2,1,0:T(8,128)(2,1)}) fusion(bf16[2,256,128]{2,1,0:T(8,128)(2,1)S(1)} %slice.101, bf16[1,256,128]{2,1,0:T(8,128)(2,1)S(1)} %get-tuple-element.47, bf16[1,256,128]{2,1,0:T(8,128)(2,1)S(1)} %get-tuple-element.93, bf16[1,256,128]{2,1,0:T(8,128)(2,1)S(1)} %get-tuple-element.59, ...), kind=kLoop, calls=%fused_computation.17 | loop fusion | flops 524288 | bytes 917504 | tf_op jit(solution)/shard_map/concatenate | solution.py:293
  17.6 4.7 %collective-permute-start.8 = (bf16[4,256,128]{2,1,0:T(8,128)(2,1)S(1)}, bf16[4,256,128]{2,1,0:T(8,128)(2,1)S(1)}, u32[]{:S(2)}, u32[]{:S(2)}) collective-permute-start(bf16[4,256,128]{2,1,0:T(8,128)(2,1)S(1)} %get-tuple-element.82), channel_id=1, source_target_pairs={{2,4},{4,2},{3,5},{5,3},{10,12},{12,10},{11,13},{13,11},{18,20},{2... | collective-permute-start | bytes 786440 | tf_op jit(solution)/shard_map/ppermute | solution.py:295
  22.3 0.0 copy-start.14
  22.4 0.7 copy-done.14
  23.0 0.7 copy.8.valid_ref
  23.7 0.7 stack.77.place_ref
  24.4 0.0 collective-permute-start.7
  24.4 0.0 collective-permute-done.partner_ref
  24.4 0.8 %pad_maximum_fusion.6 = (bf16[4,256,128]{2,1,0:T(8,128)(2,1)S(1)}, bf16[4,256,128]{2,1,0:T(8,128)(2,1)}) fusion(bf16[2,256,128]{2,1,0:T(8,128)(2,1)S(1)} %slice.99, bf16[1,256,128]{2,1,0:T(8,128)(2,1)S(1)} %get-tuple-element.50, bf16[1,256,128]{2,1,0:T(8,128)(2,1)S(1)} %get-tuple-element.90, bf16[1,256,128]{2,1,0:T(8,128)(2,1)S(1)} %get-tuple-element.62, ...), kind=kLoop, calls=%fused_computation.9 | loop fusion | flops 524288 | bytes 917504 | tf_op jit(solution)/shard_map/concatenate | solution.py:293
  25.2 1.9 %collective-permute-start.2 = (bf16[4,256,128]{2,1,0:T(8,128)(2,1)S(1)}, bf16[4,256,128]{2,1,0:T(8,128)(2,1)S(1)}, u32[]{:S(2)}, u32[]{:S(2)}) collective-permute-start(bf16[4,256,128]{2,1,0:T(8,128)(2,1)S(1)} %get-tuple-element.78), channel_id=1, source_target_pairs={{2,4},{4,2},{3,5},{5,3},{10,12},{12,10},{11,13},{13,11},{18,20},{2... | collective-permute-start | bytes 786440 | tf_op jit(solution)/shard_map/ppermute | solution.py:295
  27.1 1.8 %window_bias.1.bias_ref = f32[2,6,64,128]{3,2,1,0:T(8,128)} custom-call(s32[5]{0:T(128)} %stack.77.place_ref, s32[32,16]{1,0:T(8,128)} %copy.8.valid_ref), custom_call_target="tpu_custom_call" | custom-call | tf_op jit(solution)/shard_map/window_bias/pallas_call | solution.py:175
  29.0 0.0 collective-permute-done.4.even_ref
  29.0 0.7 copy-done.16
  29.6 0.1 copy-done.17
  29.7 5.5 %head_grads.4 = (bf16[256,128]{1,0:T(8,128)(2,1)}, bf16[256,128]{1,0:T(8,128)(2,1)}, f32[4,256,128]{2,1,0:T(8,128)}, bf16[4,256,128]{2,1,0:T(8,128)(2,1)}, bf16[4,256,128]{2,1,0:T(8,128)(2,1)}) custom-call(bf16[4,256,128]{2,1,0:T(8,128)(2,1)} %get-tuple-element.81.own_ref, bf16[4,256,128]{2,1,0:T(8,128)(2,1)} %copy-done.7, bf16[4,256,128]{2,1,0:T(8,128)(2,1)} %copy-done.17, ...), custom_call_target="tpu_custom_call" | custom-call | flops 1006632960 | bytes 1310720 | tf_op jit(solution)/shard_map/head_grads/pallas_call | solution.py:246
  35.2 0.4 collective-permute-start.12
  35.6 0.0 collective-permute-done.8.odd_ref
  35.6 3.6 %collective-permute-start.13 = (bf16[4,256,128]{2,1,0:T(8,128)(2,1)}, bf16[4,256,128]{2,1,0:T(8,128)(2,1)S(1)}, u32[]{:S(2)}, u32[]{:S(2)}) collective-permute-start(bf16[4,256,128]{2,1,0:T(8,128)(2,1)} %get-tuple-element.28), channel_id=1, source_target_pairs={{2,4},{4,2},{3,5},{5,3},{10,12},{12,10},{11,13},{13,11},{18,20},{2... | collective-permute-start | bytes 786440 | tf_op jit(solution)/shard_map/ppermute | solution.py:300
  39.3 0.7 copy-done.19
  40.0 5.5 %head_grads.5 = (bf16[256,128]{1,0:T(8,128)(2,1)}, bf16[256,128]{1,0:T(8,128)(2,1)}, f32[4,256,128]{2,1,0:T(8,128)}, bf16[4,256,128]{2,1,0:T(8,128)(2,1)}, bf16[4,256,128]{2,1,0:T(8,128)(2,1)}) custom-call(bf16[4,256,128]{2,1,0:T(8,128)(2,1)} %get-tuple-element.83.own_ref, bf16[4,256,128]{2,1,0:T(8,128)(2,1)} %copy-done.6, bf16[4,256,128]{2,1,0:T(8,128)(2,1)} %copy-done.19, ...), custom_call_target="tpu_custom_call" | custom-call | flops 1006632960 | bytes 1310720 | tf_op jit(solution)/shard_map/head_grads/pallas_call | solution.py:246
  45.4 0.0 collective-permute-start.15
  45.4 0.0 collective-permute-done.2.odd_ref
  45.5 0.0 copy-start.18
  45.5 2.1 %collective-permute-start.16 = (bf16[4,256,128]{2,1,0:T(8,128)(2,1)}, bf16[4,256,128]{2,1,0:T(8,128)(2,1)S(1)}, u32[]{:S(2)}, u32[]{:S(2)}) collective-permute-start(bf16[4,256,128]{2,1,0:T(8,128)(2,1)} %get-tuple-element.32), channel_id=1, source_target_pairs={{2,4},{4,2},{3,5},{5,3},{10,12},{12,10},{11,13},{13,11},{18,20},{2... | collective-permute-start | bytes 786440 | tf_op jit(solution)/shard_map/ppermute | solution.py:300
  47.6 0.0 collective-permute-done.1.even_ref
  47.6 0.0 copy-start.20
  47.6 0.7 copy-done.20
  48.3 5.5 %head_grads.3 = (bf16[256,128]{1,0:T(8,128)(2,1)}, bf16[256,128]{1,0:T(8,128)(2,1)}, f32[4,256,128]{2,1,0:T(8,128)}, bf16[4,256,128]{2,1,0:T(8,128)(2,1)}, bf16[4,256,128]{2,1,0:T(8,128)(2,1)}) custom-call(bf16[4,256,128]{2,1,0:T(8,128)(2,1)} %get-tuple-element.79.own_ref, bf16[4,256,128]{2,1,0:T(8,128)(2,1)} %copy-done.5, bf16[4,256,128]{2,1,0:T(8,128)(2,1)} %copy-done.20, ...), custom_call_target="tpu_custom_call" | custom-call | flops 1006632960 | bytes 1310720 | tf_op jit(solution)/shard_map/head_grads/pallas_call | solution.py:246
  53.8 0.0 collective-permute-start.9
  53.8 0.0 collective-permute-done.12
  53.8 3.6 %collective-permute-start.10 = (bf16[4,256,128]{2,1,0:T(8,128)(2,1)}, bf16[4,256,128]{2,1,0:T(8,128)(2,1)S(1)}, u32[]{:S(2)}, u32[]{:S(2)}) collective-permute-start(bf16[4,256,128]{2,1,0:T(8,128)(2,1)} %get-tuple-element.24), channel_id=1, source_target_pairs={{2,4},{4,2},{3,5},{5,3},{10,12},{12,10},{11,13},{13,11},{18,20},{2... | collective-permute-start | bytes 786440 | tf_op jit(solution)/shard_map/ppermute | solution.py:300
  57.5 0.1 add_convert_fusion.1
  57.6 0.7 copy-done.8
  58.3 1.3 %collective-permute-start.14 = (bf16[3,256,128]{2,1,0:T(8,128)(2,1)S(1)}, bf16[3,256,128]{2,1,0:T(8,128)(2,1)S(1)}, u32[]{:S(2)}, u32[]{:S(2)}) collective-permute-start(bf16[3,256,128]{2,1,0:T(8,128)(2,1)S(1)} %pad_maximum_fusion.17), channel_id=1, source_target_pairs={{0,1},{1,0},{2,3},{3,2},{4,5},{5,4},{6,7},{7,6},{8,9},{9,8},{10,11... | collective-permute-start | bytes 589832 | tf_op jit(solution)/shard_map/ppermute | solution.py:305
  59.7 0.1 add_convert_fusion
  59.9 0.7 copy-done.9
  60.6 0.3 collective-permute-start.17
  60.9 1.1 %collective-permute-done.10 = bf16[4,256,128]{2,1,0:T(8,128)(2,1)S(1)} collective-permute-done((bf16[4,256,128]{2,1,0:T(8,128)(2,1)}, bf16[4,256,128]{2,1,0:T(8,128)(2,1)S(1)}, u32[]{:S(2)}, u32[]{:S(2)}) %collective-permute-start.10) | collective-permute-done | bytes 262176 | tf_op jit(solution)/shard_map/ppermute | solution.py:300
  62.0 0.1 add_convert_fusion.2
  62.2 0.8 %copy-done.10 = bf16[256,128]{1,0:T(8,128)(2,1)S(1)} copy-done((bf16[256,128]{1,0:T(8,128)(2,1)S(1)}, bf16[256,128]{1,0:T(8,128)(2,1)}, u32[]{:S(2)}) %copy-start.10) | copy-done | bytes 65560
  63.0 1.3 %collective-permute-start.11 = (bf16[3,256,128]{2,1,0:T(8,128)(2,1)S(1)}, bf16[3,256,128]{2,1,0:T(8,128)(2,1)S(1)}, u32[]{:S(2)}, u32[]{:S(2)}) collective-permute-start(bf16[3,256,128]{2,1,0:T(8,128)(2,1)S(1)} %pad_maximum_fusion.16), channel_id=1, source_target_pairs={{0,1},{1,0},{2,3},{3,2},{4,5},{5,4},{6,7},{7,6},{8,9},{9,8},{10,11... | collective-permute-start | bytes 589832 | tf_op jit(solution)/shard_map/ppermute | solution.py:305
  64.3 0.7 collective-permute-done.14
  65.1 4.2 %collective-permute-done.17 = bf16[3,256,128]{2,1,0:T(8,128)(2,1)S(1)} collective-permute-done((bf16[3,256,128]{2,1,0:T(8,128)(2,1)S(1)}, bf16[3,256,128]{2,1,0:T(8,128)(2,1)S(1)}, u32[]{:S(2)}, u32[]{:S(2)}) %collective-permute-start.17) | collective-permute-done | bytes 196640 | tf_op jit(solution)/shard_map/ppermute | solution.py:305
  69.3 2.2 %collective-permute-done.11 = bf16[3,256,128]{2,1,0:T(8,128)(2,1)S(1)} collective-permute-done((bf16[3,256,128]{2,1,0:T(8,128)(2,1)S(1)}, bf16[3,256,128]{2,1,0:T(8,128)(2,1)S(1)}, u32[]{:S(2)}, u32[]{:S(2)}) %collective-permute-start.11) | collective-permute-done | bytes 196640 | tf_op jit(solution)/shard_map/ppermute | solution.py:305
  71.5 0.1 broadcast_select_fusion.3
  71.6 0.8 %pad_maximum_fusion.1 = bf16[6,4,8,8,128]{4,3,2,1,0:T(8,128)(2,1)} fusion(bf16[3,4,8,8,128]{4,3,2,1,0:T(8,128)(2,1)S(1)} %get-tuple-element.36, bf16[3,4,8,8,128]{4,3,2,1,0:T(8,128)(2,1)S(1)} %get-tuple-element.35), kind=kLoop, calls=%fused_computation.4 | loop fusion | flops 196608 | bytes 786432 | tf_op jit(solution)/shard_map/concatenate | solution.py:311
  72.4 0.0 copy-done.11
  72.4 0.0 copy-done.12
  72.4 0.1 copy-done.13
  72.5 0.8 %pad_maximum_fusion = bf16[6,4,8,8,128]{4,3,2,1,0:T(8,128)(2,1)} fusion(bf16[3,4,8,8,128]{4,3,2,1,0:T(8,128)(2,1)S(1)} %get-tuple-element.38, bf16[3,4,8,8,128]{4,3,2,1,0:T(8,128)(2,1)S(1)} %get-tuple-element.37), kind=kLoop, calls=%fused_computation.3 | loop fusion | flops 196608 | bytes 786432 | tf_op jit(solution)/shard_map/concatenate | solution.py:311
  73.3 0.1 broadcast_select_fusion.1
  73.4 0.8 %pad_maximum_fusion.2 = bf16[6,4,8,8,128]{4,3,2,1,0:T(8,128)(2,1)} fusion(bf16[3,4,8,8,128]{4,3,2,1,0:T(8,128)(2,1)S(1)} %get-tuple-element.34, bf16[3,4,8,8,128]{4,3,2,1,0:T(8,128)(2,1)S(1)} %get-tuple-element.33), kind=kLoop, calls=%fused_computation.5 | loop fusion | flops 196608 | bytes 786432 | tf_op jit(solution)/shard_map/concatenate | solution.py:311
  (52 shorter events, 0.4 us)
Async XLA Ops:
  0.6 1.3 %copy-start.3 = (bf16[6,4,8,8,128]{4,3,2,1,0:T(8,128)(2,1)S(1)}, bf16[6,4,8,8,128]{4,3,2,1,0:T(8,128)(2,1)}, u32[]{:S(2)}) copy-start(bf16[6,4,8,8,128]{4,3,2,1,0:T(8,128)(2,1)} %param.7) | copy-start | bytes 1179652
  0.7 1.4 %copy-start.4 = (bf16[6,4,8,8,128]{4,3,2,1,0:T(8,128)(2,1)S(1)}, bf16[6,4,8,8,128]{4,3,2,1,0:T(8,128)(2,1)}, u32[]{:S(2)}) copy-start(bf16[6,4,8,8,128]{4,3,2,1,0:T(8,128)(2,1)} %param.6) | copy-start | bytes 1179652
  2.2 8.1 %collective-permute-start.3 = (bf16[4,256,128]{2,1,0:T(8,128)(2,1)S(1)}, bf16[4,256,128]{2,1,0:T(8,128)(2,1)S(1)}, u32[]{:S(2)}, u32[]{:S(2)}) collective-permute-start(bf16[4,256,128]{2,1,0:T(8,128)(2,1)S(1)} %pad_maximum_fusion.9), channel_id=1, source_target_pairs={{0,1},{1,0},{2,3},{3,2},{4,5},{5,4},{6,7},{7,6},{8,9},{9,8},{10,11... | collective-permute-start | bytes 786440 | tf_op jit(solution)/shard_map/ppermute | solution.py:288
  4.4 12.5 %collective-permute-start.6 = (bf16[4,256,128]{2,1,0:T(8,128)(2,1)S(1)}, bf16[4,256,128]{2,1,0:T(8,128)(2,1)S(1)}, u32[]{:S(2)}, u32[]{:S(2)}) collective-permute-start(bf16[4,256,128]{2,1,0:T(8,128)(2,1)S(1)} %pad_maximum_fusion.13), channel_id=1, source_target_pairs={{0,1},{1,0},{2,3},{3,2},{4,5},{5,4},{6,7},{7,6},{8,9},{9,8},{10,11... | collective-permute-start | bytes 786440 | tf_op jit(solution)/shard_map/ppermute | solution.py:288
  4.5 19.9 %collective-permute-start = (bf16[4,256,128]{2,1,0:T(8,128)(2,1)S(1)}, bf16[4,256,128]{2,1,0:T(8,128)(2,1)S(1)}, u32[]{:S(2)}, u32[]{:S(2)}) collective-permute-start(bf16[4,256,128]{2,1,0:T(8,128)(2,1)S(1)} %pad_maximum_fusion.5), channel_id=1, source_target_pairs={{0,1},{1,0},{2,3},{3,2},{4,5},{5,4},{6,7},{7,6},{8,9},{9,8},{10,11... | collective-permute-start | bytes 786440 | tf_op jit(solution)/shard_map/ppermute | solution.py:288
  10.3 0.8 %copy-start.7 = (bf16[4,256,128]{2,1,0:T(8,128)(2,1)}, bf16[4,256,128]{2,1,0:T(8,128)(2,1)S(1)}, u32[]{:S(2)}) copy-start(bf16[4,256,128]{2,1,0:T(8,128)(2,1)S(1)} %collective-permute-done.3.partner_ref) | copy-start | bytes 786436
  11.1 17.8 %collective-permute-start.5 = (bf16[4,256,128]{2,1,0:T(8,128)(2,1)S(1)}, bf16[4,256,128]{2,1,0:T(8,128)(2,1)S(1)}, u32[]{:S(2)}, u32[]{:S(2)}) collective-permute-start(bf16[4,256,128]{2,1,0:T(8,128)(2,1)S(1)} %get-tuple-element.80), channel_id=1, source_target_pairs={{2,4},{4,2},{3,5},{5,3},{10,12},{12,10},{11,13},{13,11},{18,20},{2... | collective-permute-start | bytes 786440 | tf_op jit(solution)/shard_map/ppermute | solution.py:295
  16.7 12.2 %collective-permute-start.4 = (bf16[4,256,128]{2,1,0:T(8,128)(2,1)S(1)}, bf16[4,256,128]{2,1,0:T(8,128)(2,1)S(1)}, u32[]{:S(2)}, u32[]{:S(2)}) collective-permute-start(bf16[4,256,128]{2,1,0:T(8,128)(2,1)S(1)} %get-tuple-element.80), channel_id=1, source_target_pairs={{0,2},{4,6},{2,0},{6,4},{1,3},{5,7},{3,1},{7,5},{8,10},{12,14},{10... | collective-permute-start | bytes 786440 | tf_op jit(solution)/shard_map/ppermute | solution.py:294
  16.8 0.8 %copy-start.6 = (bf16[4,256,128]{2,1,0:T(8,128)(2,1)}, bf16[4,256,128]{2,1,0:T(8,128)(2,1)S(1)}, u32[]{:S(2)}) copy-start(bf16[4,256,128]{2,1,0:T(8,128)(2,1)S(1)} %collective-permute-done.6.partner_ref) | copy-start | bytes 786436
  17.6 18.0 %collective-permute-start.8 = (bf16[4,256,128]{2,1,0:T(8,128)(2,1)S(1)}, bf16[4,256,128]{2,1,0:T(8,128)(2,1)S(1)}, u32[]{:S(2)}, u32[]{:S(2)}) collective-permute-start(bf16[4,256,128]{2,1,0:T(8,128)(2,1)S(1)} %get-tuple-element.82), channel_id=1, source_target_pairs={{2,4},{4,2},{3,5},{5,3},{10,12},{12,10},{11,13},{13,11},{18,20},{2... | collective-permute-start | bytes 786440 | tf_op jit(solution)/shard_map/ppermute | solution.py:295
  22.3 0.7 copy-start.14
  24.4 14.9 %collective-permute-start.7 = (bf16[4,256,128]{2,1,0:T(8,128)(2,1)S(1)}, bf16[4,256,128]{2,1,0:T(8,128)(2,1)S(1)}, u32[]{:S(2)}, u32[]{:S(2)}) collective-permute-start(bf16[4,256,128]{2,1,0:T(8,128)(2,1)S(1)} %get-tuple-element.82), channel_id=1, source_target_pairs={{0,2},{4,6},{2,0},{6,4},{1,3},{5,7},{3,1},{7,5},{8,10},{12,14},{10... | collective-permute-start | bytes 786440 | tf_op jit(solution)/shard_map/ppermute | solution.py:294
  24.4 0.8 %copy-start.5 = (bf16[4,256,128]{2,1,0:T(8,128)(2,1)}, bf16[4,256,128]{2,1,0:T(8,128)(2,1)S(1)}, u32[]{:S(2)}) copy-start(bf16[4,256,128]{2,1,0:T(8,128)(2,1)S(1)} %collective-permute-done.partner_ref) | copy-start | bytes 786436
  25.2 20.3 %collective-permute-start.2 = (bf16[4,256,128]{2,1,0:T(8,128)(2,1)S(1)}, bf16[4,256,128]{2,1,0:T(8,128)(2,1)S(1)}, u32[]{:S(2)}, u32[]{:S(2)}) collective-permute-start(bf16[4,256,128]{2,1,0:T(8,128)(2,1)S(1)} %get-tuple-element.78), channel_id=1, source_target_pairs={{2,4},{4,2},{3,5},{5,3},{10,12},{12,10},{11,13},{13,11},{18,20},{2... | collective-permute-start | bytes 786440 | tf_op jit(solution)/shard_map/ppermute | solution.py:295
  28.9 0.7 copy-start.16
  28.9 18.6 %collective-permute-start.1 = (bf16[4,256,128]{2,1,0:T(8,128)(2,1)S(1)}, bf16[4,256,128]{2,1,0:T(8,128)(2,1)S(1)}, u32[]{:S(2)}, u32[]{:S(2)}) collective-permute-start(bf16[4,256,128]{2,1,0:T(8,128)(2,1)S(1)} %get-tuple-element.78), channel_id=1, source_target_pairs={{0,2},{4,6},{2,0},{6,4},{1,3},{5,7},{3,1},{7,5},{8,10},{12,14},{10... | collective-permute-start | bytes 786440 | tf_op jit(solution)/shard_map/ppermute | solution.py:294
  29.0 0.8 %copy-start.17 = (bf16[4,256,128]{2,1,0:T(8,128)(2,1)}, bf16[4,256,128]{2,1,0:T(8,128)(2,1)S(1)}, u32[]{:S(2)}) copy-start(bf16[4,256,128]{2,1,0:T(8,128)(2,1)S(1)} %collective-permute-done.4.even_ref) | copy-start | bytes 786436
  35.2 18.6 %collective-permute-start.12 = (bf16[4,256,128]{2,1,0:T(8,128)(2,1)}, bf16[4,256,128]{2,1,0:T(8,128)(2,1)S(1)}, u32[]{:S(2)}, u32[]{:S(2)}) collective-permute-start(bf16[4,256,128]{2,1,0:T(8,128)(2,1)} %get-tuple-element.27), channel_id=1, source_target_pairs={{0,2},{4,6},{2,0},{6,4},{1,3},{5,7},{3,1},{7,5},{8,10},{12,14},{10... | collective-permute-start | bytes 786440 | tf_op jit(solution)/shard_map/ppermute | solution.py:299
  35.6 3.7 %copy-start.15 = (bf16[4,256,128]{2,1,0:T(8,128)(2,1)}, bf16[4,256,128]{2,1,0:T(8,128)(2,1)S(1)}, u32[]{:S(2)}) copy-start(bf16[4,256,128]{2,1,0:T(8,128)(2,1)S(1)} %collective-permute-done.8.odd_ref) | copy-start | bytes 786436
  35.6 21.8 %collective-permute-start.13 = (bf16[4,256,128]{2,1,0:T(8,128)(2,1)}, bf16[4,256,128]{2,1,0:T(8,128)(2,1)S(1)}, u32[]{:S(2)}, u32[]{:S(2)}) collective-permute-start(bf16[4,256,128]{2,1,0:T(8,128)(2,1)} %get-tuple-element.28), channel_id=1, source_target_pairs={{2,4},{4,2},{3,5},{5,3},{10,12},{12,10},{11,13},{13,11},{18,20},{2... | collective-permute-start | bytes 786440 | tf_op jit(solution)/shard_map/ppermute | solution.py:300
  39.3 0.7 copy-start.19
  45.4 14.3 %collective-permute-start.15 = (bf16[4,256,128]{2,1,0:T(8,128)(2,1)}, bf16[4,256,128]{2,1,0:T(8,128)(2,1)S(1)}, u32[]{:S(2)}, u32[]{:S(2)}) collective-permute-start(bf16[4,256,128]{2,1,0:T(8,128)(2,1)} %get-tuple-element.31), channel_id=1, source_target_pairs={{0,2},{4,6},{2,0},{6,4},{1,3},{5,7},{3,1},{7,5},{8,10},{12,14},{10... | collective-permute-start | bytes 786440 | tf_op jit(solution)/shard_map/ppermute | solution.py:299
  45.5 2.2 %copy-start.18 = (bf16[4,256,128]{2,1,0:T(8,128)(2,1)}, bf16[4,256,128]{2,1,0:T(8,128)(2,1)S(1)}, u32[]{:S(2)}) copy-start(bf16[4,256,128]{2,1,0:T(8,128)(2,1)S(1)} %collective-permute-done.2.odd_ref) | copy-start | bytes 786436
  45.5 14.2 %collective-permute-start.16 = (bf16[4,256,128]{2,1,0:T(8,128)(2,1)}, bf16[4,256,128]{2,1,0:T(8,128)(2,1)S(1)}, u32[]{:S(2)}, u32[]{:S(2)}) collective-permute-start(bf16[4,256,128]{2,1,0:T(8,128)(2,1)} %get-tuple-element.32), channel_id=1, source_target_pairs={{2,4},{4,2},{3,5},{5,3},{10,12},{12,10},{11,13},{13,11},{18,20},{2... | collective-permute-start | bytes 786440 | tf_op jit(solution)/shard_map/ppermute | solution.py:300
  47.6 0.7 copy-start.20
  48.3 9.2 %copy-start = (f32[4,256,128]{2,1,0:T(8,128)S(1)}, f32[4,256,128]{2,1,0:T(8,128)}, u32[]{:S(2)}) copy-start(f32[4,256,128]{2,1,0:T(8,128)} %get-tuple-element.26) | copy-start | bytes 1572868
  53.8 7.1 %collective-permute-start.9 = (bf16[4,256,128]{2,1,0:T(8,128)(2,1)}, bf16[4,256,128]{2,1,0:T(8,128)(2,1)S(1)}, u32[]{:S(2)}, u32[]{:S(2)}) collective-permute-start(bf16[4,256,128]{2,1,0:T(8,128)(2,1)} %get-tuple-element.23), channel_id=1, source_target_pairs={{0,2},{4,6},{2,0},{6,4},{1,3},{5,7},{3,1},{7,5},{8,10},{12,14},{10... | collective-permute-start | bytes 786440 | tf_op jit(solution)/shard_map/ppermute | solution.py:299
  53.8 8.2 %collective-permute-start.10 = (bf16[4,256,128]{2,1,0:T(8,128)(2,1)}, bf16[4,256,128]{2,1,0:T(8,128)(2,1)S(1)}, u32[]{:S(2)}, u32[]{:S(2)}) collective-permute-start(bf16[4,256,128]{2,1,0:T(8,128)(2,1)} %get-tuple-element.24), channel_id=1, source_target_pairs={{2,4},{4,2},{3,5},{5,3},{10,12},{12,10},{11,13},{13,11},{18,20},{2... | collective-permute-start | bytes 786440 | tf_op jit(solution)/shard_map/ppermute | solution.py:300
  57.5 0.8 %copy-start.8 = (bf16[256,128]{1,0:T(8,128)(2,1)S(1)}, bf16[256,128]{1,0:T(8,128)(2,1)}, u32[]{:S(2)}) copy-start(bf16[256,128]{1,0:T(8,128)(2,1)} %get-tuple-element.25) | copy-start | bytes 196612
  57.6 2.1 %copy-start.1 = (f32[4,256,128]{2,1,0:T(8,128)S(1)}, f32[4,256,128]{2,1,0:T(8,128)}, u32[]{:S(2)}) copy-start(f32[4,256,128]{2,1,0:T(8,128)} %get-tuple-element.30) | copy-start | bytes 1572868
  58.3 6.7 %collective-permute-start.14 = (bf16[3,256,128]{2,1,0:T(8,128)(2,1)S(1)}, bf16[3,256,128]{2,1,0:T(8,128)(2,1)S(1)}, u32[]{:S(2)}, u32[]{:S(2)}) collective-permute-start(bf16[3,256,128]{2,1,0:T(8,128)(2,1)S(1)} %pad_maximum_fusion.17), channel_id=1, source_target_pairs={{0,1},{1,0},{2,3},{3,2},{4,5},{5,4},{6,7},{7,6},{8,9},{9,8},{10,11... | collective-permute-start | bytes 589832 | tf_op jit(solution)/shard_map/ppermute | solution.py:305
  59.7 0.8 %copy-start.9 = (bf16[256,128]{1,0:T(8,128)(2,1)S(1)}, bf16[256,128]{1,0:T(8,128)(2,1)}, u32[]{:S(2)}) copy-start(bf16[256,128]{1,0:T(8,128)(2,1)} %get-tuple-element.29) | copy-start | bytes 196612
  59.8 2.2 %copy-start.2 = (f32[4,256,128]{2,1,0:T(8,128)S(1)}, f32[4,256,128]{2,1,0:T(8,128)}, u32[]{:S(2)}) copy-start(f32[4,256,128]{2,1,0:T(8,128)} %get-tuple-element.22) | copy-start | bytes 1572868
  60.6 8.7 %collective-permute-start.17 = (bf16[3,256,128]{2,1,0:T(8,128)(2,1)S(1)}, bf16[3,256,128]{2,1,0:T(8,128)(2,1)S(1)}, u32[]{:S(2)}, u32[]{:S(2)}) collective-permute-start(bf16[3,256,128]{2,1,0:T(8,128)(2,1)S(1)} %pad_maximum_fusion.18), channel_id=1, source_target_pairs={{0,1},{1,0},{2,3},{3,2},{4,5},{5,4},{6,7},{7,6},{8,9},{9,8},{10,11... | collective-permute-start | bytes 589832 | tf_op jit(solution)/shard_map/ppermute | solution.py:305
  62.1 0.8 %copy-start.10 = (bf16[256,128]{1,0:T(8,128)(2,1)S(1)}, bf16[256,128]{1,0:T(8,128)(2,1)}, u32[]{:S(2)}) copy-start(bf16[256,128]{1,0:T(8,128)(2,1)} %get-tuple-element.21) | copy-start | bytes 196612
  63.0 8.5 %collective-permute-start.11 = (bf16[3,256,128]{2,1,0:T(8,128)(2,1)S(1)}, bf16[3,256,128]{2,1,0:T(8,128)(2,1)S(1)}, u32[]{:S(2)}, u32[]{:S(2)}) collective-permute-start(bf16[3,256,128]{2,1,0:T(8,128)(2,1)S(1)} %pad_maximum_fusion.16), channel_id=1, source_target_pairs={{0,1},{1,0},{2,3},{3,2},{4,5},{5,4},{6,7},{7,6},{8,9},{9,8},{10,11... | collective-permute-start | bytes 589832 | tf_op jit(solution)/shard_map/ppermute | solution.py:305
  71.5 0.8 %copy-start.11 = (bf16[256,128]{1,0:T(8,128)(2,1)S(1)}, bf16[256,128]{1,0:T(8,128)(2,1)}, u32[]{:S(2)}) copy-start(bf16[256,128]{1,0:T(8,128)(2,1)} %get-tuple-element.19) | copy-start | bytes 196612
  71.6 0.9 %copy-start.12 = (bf16[256,128]{1,0:T(8,128)(2,1)S(1)}, bf16[256,128]{1,0:T(8,128)(2,1)}, u32[]{:S(2)}) copy-start(bf16[256,128]{1,0:T(8,128)(2,1)} %get-tuple-element.20) | copy-start | bytes 196612
  71.6 0.9 %copy-start.13 = (bf16[256,128]{1,0:T(8,128)(2,1)S(1)}, bf16[256,128]{1,0:T(8,128)(2,1)}, u32[]{:S(2)}) copy-start(bf16[256,128]{1,0:T(8,128)(2,1)} %get-tuple-element.18) | copy-start | bytes 196612

commit v2 on v1

--- a/solution.py
+++ b/solution.py
@@ -10,6 +10,11 @@
 
 MASKED = -1e30
 VMEM_SPEC = pl.BlockSpec(memory_space=pltpu.VMEM)
+SMALL_GRANT = pltpu.CompilerParams(vmem_limit_bytes=16 * 2**20)
+
+
+def on_chip(*arrays):
+    return [pltpu.with_memory_space_constraint(a, pltpu.VMEM) for a in arrays]
 
 
 def extended(block, sides, width):
@@ -97,7 +102,7 @@
         query_head, grad_head, pair_rim = inputs
         query_rows = query_head.reshape(-1, width)
         grad_rows = grad_head.reshape(-1, width)
-        probs_low, dscores_low, query_part, row_max, row_total, row_delta = query_pass(
+        probs_low, dscores_low, query_part, _, _, _ = query_pass(
             query_rows,
             grad_rows,
             pair_rim[0].reshape(-1, width),
@@ -138,7 +143,49 @@
     return [(i, i + 1) for i in low] + [(i + 1, i) for i in low]
 
 
-def bias_kernel(tile_size, place_ref, valid_ref, bias_ref):
+def neighbour_rows(row):
+    return row + 1 - 2 * lax.rem(row, 2), row - 1 + 2 * lax.rem(row, 2)
+
+
+def copy_all(copies):
+    for copy in copies:
+        copy.start()
+    for copy in copies:
+        copy.wait()
+
+
+def pack_kernel(picks, *refs):
+    arrays, outs, sems = refs[:4], refs[4:-1], refs[-1]
+    half = arrays[0].shape[0] // 2
+    column = lax.axis_index("sx")
+    copies = []
+    for out, rows in zip(outs, picks):
+        for slot, (array, h, mine) in enumerate(rows):
+            head = (column if mine else 1 - column) * half + h
+            copies.append(
+                pltpu.make_async_copy(
+                    arrays[array].at[head], out.at[slot], sems.at[len(copies)]
+                )
+            )
+    copy_all(copies)
+
+
+def packed(arrays, picks):
+    tokens, width = arrays[0].shape[1:]
+    return pl.pallas_call(
+        functools.partial(pack_kernel, picks),
+        out_shape=tuple(pltpu.VMEM((len(rows), tokens, width), jnp.bfloat16) for rows in picks),
+        in_specs=[pl.BlockSpec(memory_space=pltpu.HBM)] * 4,
+        out_specs=tuple(VMEM_SPEC for _ in picks),
+        scratch_shapes=[pltpu.SemaphoreType.DMA((sum(map(len, picks)),))],
+        compiler_params=SMALL_GRANT,
+    )(*[pltpu.with_memory_space_constraint(a, pltpu.HBM) for a in arrays])
+
+
+def bias_kernel(tile_size, valid_ref, bias_ref):
+    row, column = lax.axis_index("sy"), lax.axis_index("sx")
+    tile_rows = (row, *neighbour_rows(row))
+    tile_columns = (column, 1 - column)
     valid = valid_ref[...] == 1
     rows = lax.broadcasted_iota(jnp.int32, valid.shape, 0)
     columns = lax.broadcasted_iota(jnp.int32, valid.shape, 1)
@@ -153,16 +200,16 @@
     key_row, key_column = key_cell // tile_size, key_cell % tile_size
     query_row, query_column = query_cell // tile_size, query_cell % tile_size
 
-    def inside(row, column):
-        return (row >= top) & (row <= bottom) & (column >= left) & (column <= right)
+    def inside(r, c):
+        return (r >= top) & (r <= bottom) & (c >= left) & (c <= right)
 
     for b in range(2):
-        q_row = query_row + place_ref[0] * tile_size
-        q_column = query_column + place_ref[3 + b] * tile_size
+        q_row = query_row + row * tile_size
+        q_column = query_column + tile_columns[b] * tile_size
         q_ok = inside(q_row, q_column)
         for t in range(6):
-            k_row = key_row + place_ref[t // 2] * tile_size
-            k_column = key_column + place_ref[3 + t % 2] * tile_size
+            k_row = key_row + tile_rows[t // 2] * tile_size
+            k_column = key_column + tile_columns[t % 2] * tile_size
             near = (jnp.abs(k_row - q_row) <= tile_size) & (
                 jnp.abs(k_column - q_column) <= tile_size
             )
@@ -170,32 +217,41 @@
             bias_ref[b, t] = jnp.where(ok, 0.0, MASKED)
 
 
-def window_bias(places, cell_valid, tile_size):
+def window_bias(cell_valid, tile_size):
     cells = tile_size * tile_size
     return pl.pallas_call(
         functools.partial(bias_kernel, tile_size),
-        out_shape=jax.ShapeDtypeStruct((2, 6, cells, 2 * cells), jnp.float32),
-        in_specs=[pl.BlockSpec(memory_space=pltpu.SMEM), VMEM_SPEC],
+        out_shape=pltpu.VMEM((2, 6, cells, 2 * cells), jnp.float32),
+        in_specs=[VMEM_SPEC],
         out_specs=VMEM_SPEC,
+        compiler_params=SMALL_GRANT,
         name="window_bias",
-    )(places, cell_valid)
+    )(cell_valid)
 
 
 def head_kernel(
-    own_ref, partner_ref, even_ref, odd_ref, bias_ref,
+    h, place,
+    own_kv_ref, own_qg_ref, kv_ref, qg_ref, even_own_ref, even_ref, odd_own_ref, odd_ref, bias_ref,
     own_dq_ref, partner_dq_ref, middle_ref, even_part_ref, odd_part_ref,
     score_ref, dprob_ref, key_sum_ref, value_sum_ref,
 ):
-    tokens, width = own_ref.shape[1:]
+    tokens, width = own_kv_ref.shape[1:]
     score_scale = 1.0 / math.sqrt(width)
     exponent_scale = math.log2(math.e) / math.sqrt(width)
-    keys = [own_ref.at[0], partner_ref.at[0], even_ref.at[0], even_ref.at[2], odd_ref.at[0], odd_ref.at[2]]
-    values = [own_ref.at[1], partner_ref.at[1], even_ref.at[1], even_ref.at[3], odd_ref.at[1], odd_ref.at[3]]
-    key_parts = [middle_ref.at[0], middle_ref.at[2], even_part_ref.at[0], even_part_ref.at[2], odd_part_ref.at[0], odd_part_ref.at[2]]
-    value_parts = [middle_ref.at[1], middle_ref.at[3], even_part_ref.at[1], even_part_ref.at[3], odd_part_ref.at[1], odd_part_ref.at[3]]
-    for b, (side, dq_ref) in enumerate(((own_ref, own_dq_ref), (partner_ref, partner_dq_ref))):
-        query_rows = side[2]
-        grad_rows = side[3]
+    sides = ((own_kv_ref, kv_ref), (even_own_ref, even_ref), (odd_own_ref, odd_ref))
+    keys, values = [
+        [ref.at[first + i] for side in sides for ref, first in zip(side, (2 * h, place))]
+        for i in range(2)
+    ]
+    key_parts, value_parts = [
+        [part.at[2 * c + i] for part in (middle_ref, even_part_ref, odd_part_ref) for c in range(2)]
+        for i in range(2)
+    ]
+    blocks = (
+        (own_qg_ref[2 * h], own_qg_ref[2 * h + 1], own_dq_ref),
+        (qg_ref[place], qg_ref[place + 1], partner_dq_ref),
+    )
+    for b, (query_rows, grad_rows, dq_ref) in enumerate(blocks):
         row_max = None
         for t in range(6):
             bias = bias_ref[b, t]
@@ -231,28 +287,28 @@
                 value_sum_ref[t] = value_part
             else:
                 key_total = (key_sum_ref[t] + key_part) * score_scale
-                key_parts[t][...] = key_total.astype(middle_ref.dtype if t < 2 else jnp.bfloat16)
+                key_parts[t][...] = key_total.astype(key_parts[t].dtype)
                 value_total = value_sum_ref[t] + value_part
-                value_parts[t][...] = value_total.astype(middle_ref.dtype if t < 2 else jnp.bfloat16)
+                value_parts[t][...] = value_total.astype(value_parts[t].dtype)
             query_part = contract_first(dscores_low, keys[t][...])
             query_grad = query_part if query_grad is None else query_grad + query_part
         dq_ref[...] = (query_grad * score_scale).astype(jnp.bfloat16)
 
 
-def head_grads(own, partner, even, odd, bias):
-    tokens, width = own.shape[1:]
+def head_grads(h, place, arrays, bias):
+    tokens, width = arrays[0].shape[1:]
     low = jnp.bfloat16
     pairs = 2 * 6 * tokens * tokens
     return pl.pallas_call(
-        head_kernel,
+        functools.partial(head_kernel, h, place),
         out_shape=(
-            jax.ShapeDtypeStruct((tokens, width), low),
-            jax.ShapeDtypeStruct((tokens, width), low),
-            jax.ShapeDtypeStruct((4, tokens, width), jnp.float32),
-            jax.ShapeDtypeStruct((4, tokens, width), low),
-            jax.ShapeDtypeStruct((4, tokens, width), low),
+            pltpu.VMEM((tokens, width), low),
+            pltpu.VMEM((tokens, width), low),
+            pltpu.VMEM((4, tokens, width), jnp.float32),
+            pltpu.VMEM((4, tokens, width), low),
+            pltpu.VMEM((4, tokens, width), low),
         ),
-        in_specs=[VMEM_SPEC] * 5,
+        in_specs=[VMEM_SPEC] * 9,
         out_specs=[VMEM_SPEC] * 5,
         scratch_shapes=[
             pltpu.VMEM((6, tokens, tokens), jnp.float32),
@@ -260,11 +316,47 @@
             pltpu.VMEM((6, tokens, width), jnp.float32),
             pltpu.VMEM((6, tokens, width), jnp.float32),
         ],
+        compiler_params=SMALL_GRANT,
         cost_estimate=pl.CostEstimate(
             flops=10 * pairs * width, transcendentals=pairs, bytes_accessed=20 * tokens * width * 2
         ),
         name="head_grads",
-    )(own, partner, even, odd, bias)
+    )(*on_chip(*arrays, bias))
+
+
+def query_slots(half):
+    return [(0, 2)] + [(h - 1, 2 + (h == 1)) for h in range(1, half)]
+
+
+def collect_kernel(count, *refs):
+    mine, theirs, outs, sems = refs[:count], refs[count:-4], refs[-4:-1], refs[-1]
+    half = outs[0].shape[0] // 2
+    column = lax.axis_index("sx")
+    copies = []
+
+    def send(source, out, head):
+        copies.append(pltpu.make_async_copy(source, out.at[head], sems.at[len(copies)]))
+
+    for h, (ref, slot) in enumerate(query_slots(half)):
+        send(mine[2 * h], outs[0], column * half + h)
+        send(theirs[ref].at[slot], outs[0], (1 - column) * half + h)
+        for i in range(2):
+            send(mine[2 * h + 1].at[i], outs[1 + i], column * half + h)
+            send(theirs[h].at[i], outs[1 + i], (1 - column) * half + h)
+    copy_all(copies)
+
+
+def collected(mine, theirs, shape):
+    heads = shape[0]
+    return pl.pallas_call(
+        functools.partial(collect_kernel, len(mine)),
+        out_shape=(pltpu.HBM(shape, jnp.bfloat16),) * 3,
+        in_specs=[VMEM_SPEC] * (len(mine) + len(theirs)),
+        out_specs=(pl.BlockSpec(memory_space=pltpu.HBM),) * 3,
+        scratch_shapes=[pltpu.SemaphoreType.DMA((3 * heads,))],
+        compiler_params=SMALL_GRANT,
+        name="collected",
+    )(*on_chip(*mine, *theirs))
 
 
 def swapped(queries, key_vectors, value_vectors, out_grad, cell_valid):
@@ -272,70 +364,73 @@
     tokens = frames * tile_size * tile_size
     half = heads // 2
     rows = lax.axis_size("sy")
-    row, column = lax.axis_index("sy"), lax.axis_index("sx")
     swap = [(0, 1), (1, 0)]
     even_pairs, odd_pairs = pairs_of(rows, 0), pairs_of(rows, 1)
     arrays = [a.reshape(heads, tokens, width) for a in (key_vectors, value_vectors, queries, out_grad)]
-
-    def one_head(index):
-        return jnp.concatenate(
-            [lax.dynamic_slice_in_dim(a, index, 1, axis=0) for a in arrays], axis=0
+    later = range(1, half)
+
+    def rows_sent(even_block, odd_block):
+        return (
+            lax.ppermute(even_block, "sy", even_pairs), lax.ppermute(odd_block, "sy", odd_pairs)
         )
 
-    even_row = row + 1 - 2 * (row % 2)
-    odd_row = row - 1 + 2 * (row % 2)
-    places = jnp.stack([row, even_row, odd_row, column, 1 - column]).astype(jnp.int32)
-    received = [lax.ppermute(one_head((1 - column) * half + h), "sx", swap) for h in range(half)]
-    bias = window_bias(places, cell_valid, tile_size)
-    local_grads, returned = [], []
+    key_value, query_grad_pair = (0, 1), (2, 3)
+    first_kv, = packed(arrays, [[(a, 0, False) for a in key_value]])
+    own_kv, first_qg = packed(
+        arrays,
+        [[(a, h, True) for h in range(half) for a in key_value]]
+        + [[(a, 0, False) for a in query_grad_pair]],
+    )
+    later_kv, later_qg, own_qg = packed(
+        arrays,
+        [[(a, h, False) for h in later for a in side] for side in (key_value, query_grad_pair)]
+        + [[(a, h, True) for h in range(half) for a in query_grad_pair]],
+    )
+    kv_first = lax.ppermute(first_kv, "sx", swap)
+    qg_first = lax.ppermute(first_qg, "sx", swap)
+    kv_later = lax.ppermute(later_kv, "sx", swap)
+    qg_later = lax.ppermute(later_qg, "sx", swap)
+    even_own, odd_own = rows_sent(own_kv, own_kv)
+    bias = window_bias(cell_valid, tile_size)
+    even_first, odd_first = rows_sent(kv_first, kv_first)
+    even_later, odd_later = rows_sent(kv_later, kv_later)
+
+    own_dq, partner_dq, backs = [], [], []
     for h in range(half):
-        own = one_head(column * half + h)
-        halo = jnp.concatenate([own[:2], received[h][:2]], axis=0)
-        even = lax.ppermute(halo, "sy", even_pairs)
-        odd = lax.ppermute(halo, "sy", odd_pairs)
-        own_dq, partner_dq, middle, even_part, odd_part = head_grads(
-            own, received[h], even, odd, bias
+        kv, qg, even, odd = (
+            (kv_later, qg_later, even_later, odd_later)
+            if h
+            else (kv_first, qg_first, even_first, odd_first)
         )
-        even_back = lax.ppermute(even_part, "sy", even_pairs)
-        odd_back = lax.ppermute(odd_part, "sy", odd_pairs)
+        sides = (own_kv, own_qg, kv, qg, even_own, even, odd_own, odd)
+        grads = head_grads(h, max(2 * h - 2, 0), sides, bias)
+        own_dq.append(grads[0])
+        partner_dq.append(grads[1])
+        backs.append((grads[2], rows_sent(grads[3], grads[4])))
+    mine, theirs = [], []
+    for h, (middle, (even_back, odd_back)) in enumerate(backs):
         total = middle + even_back.astype(jnp.float32) + odd_back.astype(jnp.float32)
         total = total.astype(jnp.bfloat16)
-        local_grads.append(jnp.concatenate([own_dq[None], total[:2]], axis=0))
-        outgoing = jnp.concatenate([partner_dq[None], total[2:]], axis=0)
-        returned.append(lax.ppermute(outgoing, "sx", swap))
-    first = column == 0
-    outs = []
-    for i in range(3):
-        mine = jnp.stack([g[i] for g in local_grads])
-        theirs = jnp.stack([g[i] for g in returned])
-        out = jnp.concatenate(
-            [jnp.where(first, mine, theirs), jnp.where(first, theirs, mine)], axis=0
-        )
-        outs.append(out.reshape(queries.shape))
-    return tuple(outs)
+        mine += [own_dq[h], total[:2]]
+        queries_out = [partner_dq[j] for j, (ref, _) in enumerate(query_slots(half)) if ref == h]
+        outgoing = jnp.concatenate([total[2:]] + [q[None] for q in queries_out], axis=0)
+        theirs.append(lax.ppermute(outgoing, "sx", swap))
+    outs = collected(mine, theirs, (heads, tokens, width))
+    return tuple(out.reshape(queries.shape) for out in outs)
 
 
 def local(queries, *rest):
-    if lax.axis_size("sx") == 2 and queries.shape[0] % 2 == 0:
+    if lax.axis_size("sx") == 2 and queries.shape[0] % 2 == 0 and queries.shape[0] > 2:
         return swapped(queries, *rest)
     return general(queries, *rest)
 
 
 def solution(mesh):
+    spec = P("tp", None, "sy", "sx", None)
     return jax.shard_map(
         local,
         mesh=mesh,
-        in_specs=(
-            P("tp", None, "sy", "sx", None),
-            P("tp", None, "sy", "sx", None),
-            P("tp", None, "sy", "sx", None),
-            P("tp", None, "sy", "sx", None),
-            P(),
-        ),
-        out_specs=(
-            P("tp", None, "sy", "sx", None),
-            P("tp", None, "sy", "sx", None),
-            P("tp", None, "sy", "sx", None),
-        ),
+        in_specs=(spec, spec, spec, spec, P()),
+        out_specs=(spec, spec, spec),
         check_vma=False,
     )

time: 74.7 us -> 65.3 us (0.87)
  the two profiles are of different devices: /device:TPU:1 before, /device:TPU:0 now
where the time goes in v2:
time: 65.3 us; the launch traced here: 64.9 us
  starting transfers between devices  30.3 us (46%)
  waiting for transfers between devices  18.5 us (28%)
  Pallas kernels  14.8 us (23%)
  between operations  0.83 us (1%)
    ppermute x6, starting transfers between devices, rows_sent(): lax.ppermute(even_block, 'sy', even_pairs)  17.8 us
    ppermute x3, waiting for transfers between devices, swapped(): theirs.append(lax.ppermute(outgoing, 'sx', swap))  11.8 us
    pallas_call x3, Pallas kernels, head_grads(): pl.pallas_call(functools.partial(head_kernel, h, place), out_shape=(pltpu...  9.99 us
    ppermute x1, waiting for transfers between devices, swapped(): qg_first = lax.ppermute(first_qg, 'sx', swap)  6.63 us
    ppermute x6, starting transfers between devices, rows_sent(): lax.ppermute(odd_block, 'sy', odd_pairs)  4.03 us
    pallas_call x3, Pallas kernels, packed(): pl.pallas_call(functools.partial(pack_kernel, picks), out_shape=tuple((pl...  3.36 us
    ppermute x3, starting transfers between devices, swapped(): theirs.append(lax.ppermute(outgoing, 'sx', swap))  3.21 us
    ppermute x1, starting transfers between devices, swapped(): kv_first = lax.ppermute(first_kv, 'sx', swap)  2.59 us
  transfers between devices with their start and end apart: 19, of which 2 were waited for; matrix products, arithmetic and copies ran while one was open for 1% of the time, Pallas kernels for 19%

profile of v2, /device:TPU:0, one launch (start us, length us, event | category | flops | bytes accessed | tf_op | source)
XLA Modules:
  0.0 64.9 jit_solution(17451281965873510931)
XLA Ops:
  0.6 1.1 %shard_map.76 = (bf16[6,256,128]{2,1,0:T(8,128)(2,1)S(1)}, bf16[2,256,128]{2,1,0:T(8,128)(2,1)S(1)}) custom-call(bf16[6,256,128]{2,1,0:T(8,128)(2,1)} %bitcast.13, bf16[6,256,128]{2,1,0:T(8,128)(2,1)} %bitcast.16, bf16[6,256,128]{2,1,0:T(8,128)(2,1)} %bitcast.19, bf16[6,256,128]{2,1,0:T(8,128)(2,1)} %bitcast.22), custom_call_target="tpu_custom_call" | custom-call | tf_op jit(solution)/shard_map/pallas_call | solution.py:175
  1.8 0.6 collective-permute-start.2
  2.3 0.7 %collective-permute-start.4 = (bf16[6,256,128]{2,1,0:T(8,128)(2,1)S(1)}, bf16[6,256,128]{2,1,0:T(8,128)(2,1)S(1)}, u32[]{:S(2)}, u32[]{:S(2)}) collective-permute-start(bf16[6,256,128]{2,1,0:T(8,128)(2,1)S(1)} %get-tuple-element.26.own_kv_ref), channel_id=1, source_target_pairs={{2,4},{4,2},{3,5},{5,3},{10,12},{12,10},{11,13},{13,11},{18,20},{2... | collective-permute-start | bytes 1179656 | tf_op jit(solution)/shard_map/ppermute | solution.py:374
  3.0 0.9 %shard_map.78 = bf16[2,256,128]{2,1,0:T(8,128)(2,1)S(1)} custom-call(bf16[6,256,128]{2,1,0:T(8,128)(2,1)} %bitcast.14, bf16[6,256,128]{2,1,0:T(8,128)(2,1)} %bitcast.17, bf16[6,256,128]{2,1,0:T(8,128)(2,1)} %bitcast.20, bf16[6,256,128]{2,1,0:T(8,128)(2,1)} %bitcast.23), custom_call_target="tpu_custom_call" | custom-call | tf_op jit(solution)/shard_map/pallas_call | solution.py:175
  3.9 2.6 %collective-permute-start = (bf16[2,256,128]{2,1,0:T(8,128)(2,1)S(1)}, bf16[2,256,128]{2,1,0:T(8,128)(2,1)S(1)}, u32[]{:S(2)}, u32[]{:S(2)}) collective-permute-start(bf16[2,256,128]{2,1,0:T(8,128)(2,1)S(1)} %shard_map.78), channel_id=1, source_target_pairs={{0,1},{1,0},{2,3},{3,2},{4,5},{5,4},{6,7},{7,6},{8,9},{9,8},{10,11... | collective-permute-start | bytes 393224 | tf_op jit(solution)/shard_map/ppermute | solution.py:389
  6.5 0.0 copy-start
  6.5 1.3 %shard_map.77 = (bf16[4,256,128]{2,1,0:T(8,128)(2,1)S(1)}, bf16[4,256,128]{2,1,0:T(8,128)(2,1)S(1)}, bf16[6,256,128]{2,1,0:T(8,128)(2,1)S(1)}) custom-call(bf16[6,256,128]{2,1,0:T(8,128)(2,1)} %bitcast.15, bf16[6,256,128]{2,1,0:T(8,128)(2,1)} %bitcast.18, bf16[6,256,128]{2,1,0:T(8,128)(2,1)} %bitcast.21, bf16[6,256,128]{2,1,0:T(8,128)(2,1)} %bitcast.24), custom_call_target="tpu_custom_call" | custom-call | tf_op jit(solution)/shard_map/pallas_call | solution.py:175
  7.9 0.1 collective-permute-start.8
  7.9 2.0 %collective-permute-start.1 = (bf16[2,256,128]{2,1,0:T(8,128)(2,1)S(1)}, bf16[2,256,128]{2,1,0:T(8,128)(2,1)S(1)}, u32[]{:S(2)}, u32[]{:S(2)}) collective-permute-start(bf16[2,256,128]{2,1,0:T(8,128)(2,1)S(1)} %get-tuple-element.28), channel_id=1, source_target_pairs={{0,1},{1,0},{2,3},{3,2},{4,5},{5,4},{6,7},{7,6},{8,9},{9,8},{10,11... | collective-permute-start | bytes 393224 | tf_op jit(solution)/shard_map/ppermute | solution.py:390
  9.9 0.0 collective-permute-done.kv_ref
  9.9 2.4 %collective-permute-start.3 = (bf16[2,256,128]{2,1,0:T(8,128)(2,1)S(1)}, bf16[2,256,128]{2,1,0:T(8,128)(2,1)S(1)}, u32[]{:S(2)}, u32[]{:S(2)}) collective-permute-start(bf16[2,256,128]{2,1,0:T(8,128)(2,1)S(1)} %collective-permute-done.kv_ref), channel_id=1, source_target_pairs={{0,2},{4,6},{2,0},{6,4},{1,3},{5,7},{3,1},{7,5},{8,10},{12,14},{10... | collective-permute-start | bytes 393224 | tf_op jit(solution)/shard_map/ppermute | solution.py:374
  12.4 6.6 %collective-permute-done.1.qg_ref = bf16[2,256,128]{2,1,0:T(8,128)(2,1)S(1)} collective-permute-done((bf16[2,256,128]{2,1,0:T(8,128)(2,1)S(1)}, bf16[2,256,128]{2,1,0:T(8,128)(2,1)S(1)}, u32[]{:S(2)}, u32[]{:S(2)}) %collective-permute-start.1) | collective-permute-done | bytes 131104 | tf_op jit(solution)/shard_map/ppermute | solution.py:390
  19.0 0.7 %collective-permute-start.5 = (bf16[2,256,128]{2,1,0:T(8,128)(2,1)S(1)}, bf16[2,256,128]{2,1,0:T(8,128)(2,1)S(1)}, u32[]{:S(2)}, u32[]{:S(2)}) collective-permute-start(bf16[2,256,128]{2,1,0:T(8,128)(2,1)S(1)} %collective-permute-done.kv_ref), channel_id=1, source_target_pairs={{2,4},{4,2},{3,5},{5,3},{10,12},{12,10},{11,13},{13,11},{18,20},{2... | collective-permute-start | bytes 393224 | tf_op jit(solution)/shard_map/ppermute | solution.py:374
  19.7 0.0 collective-permute-done.3.even_ref
  19.7 0.6 collective-permute-start.9
  20.2 0.0 collective-permute-done.8.kv_ref
  20.2 4.1 %collective-permute-start.10 = (bf16[4,256,128]{2,1,0:T(8,128)(2,1)S(1)}, bf16[4,256,128]{2,1,0:T(8,128)(2,1)S(1)}, u32[]{:S(2)}, u32[]{:S(2)}) collective-permute-start(bf16[4,256,128]{2,1,0:T(8,128)(2,1)S(1)} %collective-permute-done.8.kv_ref), channel_id=1, source_target_pairs={{0,2},{4,6},{2,0},{6,4},{1,3},{5,7},{3,1},{7,5},{8,10},{12,14},{10... | collective-permute-start | bytes 786440 | tf_op jit(solution)/shard_map/ppermute | solution.py:374
  24.4 0.0 collective-permute-done.5.odd_ref
  24.4 0.7 %collective-permute-start.11 = (bf16[4,256,128]{2,1,0:T(8,128)(2,1)S(1)}, bf16[4,256,128]{2,1,0:T(8,128)(2,1)S(1)}, u32[]{:S(2)}, u32[]{:S(2)}) collective-permute-start(bf16[4,256,128]{2,1,0:T(8,128)(2,1)S(1)} %collective-permute-done.8.kv_ref), channel_id=1, source_target_pairs={{2,4},{4,2},{3,5},{5,3},{10,12},{12,10},{11,13},{13,11},{18,20},{2... | collective-permute-start | bytes 786440 | tf_op jit(solution)/shard_map/ppermute | solution.py:374
  25.0 0.0 copy-done
  25.1 0.1 copy.8.valid_ref
  25.1 0.3 window_bias.1.bias_ref
  25.5 0.0 collective-permute-done.2.even_own_ref
  25.5 0.0 collective-permute-done.4.odd_own_ref
  25.5 3.3 %head_grads.3 = (bf16[256,128]{1,0:T(8,128)(2,1)S(1)}, bf16[256,128]{1,0:T(8,128)(2,1)S(1)}, f32[4,256,128]{2,1,0:T(8,128)S(1)}, bf16[4,256,128]{2,1,0:T(8,128)(2,1)S(1)}, bf16[4,256,128]{2,1,0:T(8,128)(2,1)S(1)}) custom-call(bf16[6,256,128]{2,1,0:T(8,128)(2,1)S(1)} %get-tuple-element.26.own_kv_ref, bf16[6,256,128]{2,1,0:T(8,128)(2,1)S(1)} %get-tuple-element.27.own_qg_ref, ...), custom_call_target="tpu_custom_call" | custom-call | flops 1006632960 | bytes 1310720 | tf_op jit(solution)/shard_map/head_grads/pallas_call | solution.py:302
  28.8 0.7 %collective-permute-start.7 = (bf16[4,256,128]{2,1,0:T(8,128)(2,1)S(1)}, bf16[4,256,128]{2,1,0:T(8,128)(2,1)S(1)}, u32[]{:S(2)}, u32[]{:S(2)}) collective-permute-start(bf16[4,256,128]{2,1,0:T(8,128)(2,1)S(1)} %get-tuple-element.32), channel_id=1, source_target_pairs={{2,4},{4,2},{3,5},{5,3},{10,12},{12,10},{11,13},{13,11},{18,20},{2... | collective-permute-start | bytes 786440 | tf_op jit(solution)/shard_map/ppermute | solution.py:374
  29.5 6.3 %collective-permute-start.6 = (bf16[4,256,128]{2,1,0:T(8,128)(2,1)S(1)}, bf16[4,256,128]{2,1,0:T(8,128)(2,1)S(1)}, u32[]{:S(2)}, u32[]{:S(2)}) collective-permute-start(bf16[4,256,128]{2,1,0:T(8,128)(2,1)S(1)} %get-tuple-element.31), channel_id=1, source_target_pairs={{0,2},{4,6},{2,0},{6,4},{1,3},{5,7},{3,1},{7,5},{8,10},{12,14},{10... | collective-permute-start | bytes 786440 | tf_op jit(solution)/shard_map/ppermute | solution.py:374
  35.8 0.0 collective-permute-done.9.qg_ref
  35.9 0.0 collective-permute-done.10.even_ref
  35.9 0.0 collective-permute-done.11.odd_ref
  35.9 3.3 %head_grads.4 = (bf16[256,128]{1,0:T(8,128)(2,1)S(1)}, bf16[256,128]{1,0:T(8,128)(2,1)S(1)}, f32[4,256,128]{2,1,0:T(8,128)S(1)}, bf16[4,256,128]{2,1,0:T(8,128)(2,1)S(1)}, bf16[4,256,128]{2,1,0:T(8,128)(2,1)S(1)}) custom-call(bf16[6,256,128]{2,1,0:T(8,128)(2,1)S(1)} %get-tuple-element.26.own_kv_ref, bf16[6,256,128]{2,1,0:T(8,128)(2,1)S(1)} %get-tuple-element.27.own_qg_ref, ...), custom_call_target="tpu_custom_call" | custom-call | flops 1006632960 | bytes 1310720 | tf_op jit(solution)/shard_map/head_grads/pallas_call | solution.py:302
  39.2 0.7 %collective-permute-start.13 = (bf16[4,256,128]{2,1,0:T(8,128)(2,1)S(1)}, bf16[4,256,128]{2,1,0:T(8,128)(2,1)S(1)}, u32[]{:S(2)}, u32[]{:S(2)}) collective-permute-start(bf16[4,256,128]{2,1,0:T(8,128)(2,1)S(1)} %get-tuple-element.38), channel_id=1, source_target_pairs={{2,4},{4,2},{3,5},{5,3},{10,12},{12,10},{11,13},{13,11},{18,20},{2... | collective-permute-start | bytes 786440 | tf_op jit(solution)/shard_map/ppermute | solution.py:374
  39.9 2.5 %collective-permute-start.12 = (bf16[4,256,128]{2,1,0:T(8,128)(2,1)S(1)}, bf16[4,256,128]{2,1,0:T(8,128)(2,1)S(1)}, u32[]{:S(2)}, u32[]{:S(2)}) collective-permute-start(bf16[4,256,128]{2,1,0:T(8,128)(2,1)S(1)} %get-tuple-element.37), channel_id=1, source_target_pairs={{0,2},{4,6},{2,0},{6,4},{1,3},{5,7},{3,1},{7,5},{8,10},{12,14},{10... | collective-permute-start | bytes 786440 | tf_op jit(solution)/shard_map/ppermute | solution.py:374
  42.4 3.3 %head_grads.5 = (bf16[256,128]{1,0:T(8,128)(2,1)S(1)}, bf16[256,128]{1,0:T(8,128)(2,1)S(1)}, f32[4,256,128]{2,1,0:T(8,128)S(1)}, bf16[4,256,128]{2,1,0:T(8,128)(2,1)S(1)}, bf16[4,256,128]{2,1,0:T(8,128)(2,1)S(1)}) custom-call(bf16[6,256,128]{2,1,0:T(8,128)(2,1)S(1)} %get-tuple-element.26.own_kv_ref, bf16[6,256,128]{2,1,0:T(8,128)(2,1)S(1)} %get-tuple-element.27.own_qg_ref, ...), custom_call_target="tpu_custom_call" | custom-call | flops 1006632960 | bytes 1310720 | tf_op jit(solution)/shard_map/head_grads/pallas_call | solution.py:302
  45.7 0.7 %collective-permute-start.15 = (bf16[4,256,128]{2,1,0:T(8,128)(2,1)S(1)}, bf16[4,256,128]{2,1,0:T(8,128)(2,1)S(1)}, u32[]{:S(2)}, u32[]{:S(2)}) collective-permute-start(bf16[4,256,128]{2,1,0:T(8,128)(2,1)S(1)} %get-tuple-element.42), channel_id=1, source_target_pairs={{2,4},{4,2},{3,5},{5,3},{10,12},{12,10},{11,13},{13,11},{18,20},{2... | collective-permute-start | bytes 786440 | tf_op jit(solution)/shard_map/ppermute | solution.py:374
  46.4 0.0 collective-permute-done.7
  46.4 1.9 %collective-permute-start.14 = (bf16[4,256,128]{2,1,0:T(8,128)(2,1)S(1)}, bf16[4,256,128]{2,1,0:T(8,128)(2,1)S(1)}, u32[]{:S(2)}, u32[]{:S(2)}) collective-permute-start(bf16[4,256,128]{2,1,0:T(8,128)(2,1)S(1)} %get-tuple-element.41), channel_id=1, source_target_pairs={{0,2},{4,6},{2,0},{6,4},{1,3},{5,7},{3,1},{7,5},{8,10},{12,14},{10... | collective-permute-start | bytes 786440 | tf_op jit(solution)/shard_map/ppermute | solution.py:374
  48.3 0.0 collective-permute-done.6
  48.3 0.1 add_convert_fusion.2
  48.5 1.1 %collective-permute-start.16 = (bf16[4,256,128]{2,1,0:T(8,128)(2,1)S(1)}, bf16[4,256,128]{2,1,0:T(8,128)(2,1)S(1)}, u32[]{:S(2)}, u32[]{:S(2)}) collective-permute-start(bf16[4,256,128]{2,1,0:T(8,128)(2,1)S(1)} %pad_maximum_fusion), channel_id=1, source_target_pairs={{0,1},{1,0},{2,3},{3,2},{4,5},{5,4},{6,7},{7,6},{8,9},{9,8},{10,11... | collective-permute-start | bytes 786440 | tf_op jit(solution)/shard_map/ppermute | solution.py:417
  49.5 0.0 collective-permute-done.13
  49.5 0.0 collective-permute-done.12
  49.5 0.1 add_convert_fusion.1
  49.7 1.1 %collective-permute-start.17 = (bf16[3,256,128]{2,1,0:T(8,128)(2,1)S(1)}, bf16[3,256,128]{2,1,0:T(8,128)(2,1)S(1)}, u32[]{:S(2)}, u32[]{:S(2)}) collective-permute-start(bf16[3,256,128]{2,1,0:T(8,128)(2,1)S(1)} %pad_maximum_fusion.1), channel_id=1, source_target_pairs={{0,1},{1,0},{2,3},{3,2},{4,5},{5,4},{6,7},{7,6},{8,9},{9,8},{10,11... | collective-permute-start | bytes 589832 | tf_op jit(solution)/shard_map/ppermute | solution.py:417
  50.8 0.0 collective-permute-done.15
  50.8 0.0 collective-permute-done.14
  50.8 0.1 add_convert_fusion
  50.9 1.1 %collective-permute-start.18 = (bf16[2,256,128]{2,1,0:T(8,128)(2,1)S(1)}, bf16[2,256,128]{2,1,0:T(8,128)(2,1)S(1)}, u32[]{:S(2)}, u32[]{:S(2)}) collective-permute-start(bf16[2,256,128]{2,1,0:T(8,128)(2,1)S(1)} %get-tuple-element.49), channel_id=1, source_target_pairs={{0,1},{1,0},{2,3},{3,2},{4,5},{5,4},{6,7},{7,6},{8,9},{9,8},{10,11... | collective-permute-start | bytes 393224 | tf_op jit(solution)/shard_map/ppermute | solution.py:417
  52.0 11.8 %collective-permute-done.18.refs_8_ = bf16[2,256,128]{2,1,0:T(8,128)(2,1)S(1)} collective-permute-done((bf16[2,256,128]{2,1,0:T(8,128)(2,1)S(1)}, bf16[2,256,128]{2,1,0:T(8,128)(2,1)S(1)}, u32[]{:S(2)}, u32[]{:S(2)}) %collective-permute-start.18) | collective-permute-done | bytes 131104 | tf_op jit(solution)/shard_map/ppermute | solution.py:417
  63.8 0.0 collective-permute-done.16.refs_6_
  63.8 0.0 collective-permute-done.17.refs_7_
  63.8 1.1 %collected.1 = (bf16[6,256,128]{2,1,0:T(8,128)(2,1)}, bf16[6,256,128]{2,1,0:T(8,128)(2,1)}, bf16[6,256,128]{2,1,0:T(8,128)(2,1)}) custom-call(bf16[256,128]{1,0:T(8,128)(2,1)S(1)} %get-tuple-element.29.refs_0_, bf16[2,256,128]{2,1,0:T(8,128)(2,1)S(1)} %get-tuple-element.54.refs_1_, bf16[256,128]{1,0:T(8,128)(2,1)S(1)} %get-tuple-element.35.refs_2_, ...), custom_call_target="tpu_custom_call" | custom-call | tf_op jit(solution)/shard_map/collected/pallas_call | solution.py:351
  (5 shorter events, 0.1 us)
Async XLA Ops:
  1.8 23.7 %collective-permute-start.2 = (bf16[6,256,128]{2,1,0:T(8,128)(2,1)S(1)}, bf16[6,256,128]{2,1,0:T(8,128)(2,1)S(1)}, u32[]{:S(2)}, u32[]{:S(2)}) collective-permute-start(bf16[6,256,128]{2,1,0:T(8,128)(2,1)S(1)} %get-tuple-element.26.own_kv_ref), channel_id=1, source_target_pairs={{0,2},{4,6},{2,0},{6,4},{1,3},{5,7},{3,1},{7,5},{8,10},{12,14},{10... | collective-permute-start | bytes 1179656 | tf_op jit(solution)/shard_map/ppermute | solution.py:374
  2.3 23.1 %collective-permute-start.4 = (bf16[6,256,128]{2,1,0:T(8,128)(2,1)S(1)}, bf16[6,256,128]{2,1,0:T(8,128)(2,1)S(1)}, u32[]{:S(2)}, u32[]{:S(2)}) collective-permute-start(bf16[6,256,128]{2,1,0:T(8,128)(2,1)S(1)} %get-tuple-element.26.own_kv_ref), channel_id=1, source_target_pairs={{2,4},{4,2},{3,5},{5,3},{10,12},{12,10},{11,13},{13,11},{18,20},{2... | collective-permute-start | bytes 1179656 | tf_op jit(solution)/shard_map/ppermute | solution.py:374
  3.9 6.0 %collective-permute-start = (bf16[2,256,128]{2,1,0:T(8,128)(2,1)S(1)}, bf16[2,256,128]{2,1,0:T(8,128)(2,1)S(1)}, u32[]{:S(2)}, u32[]{:S(2)}) collective-permute-start(bf16[2,256,128]{2,1,0:T(8,128)(2,1)S(1)} %shard_map.78), channel_id=1, source_target_pairs={{0,1},{1,0},{2,3},{3,2},{4,5},{5,4},{6,7},{7,6},{8,9},{9,8},{10,11... | collective-permute-start | bytes 393224 | tf_op jit(solution)/shard_map/ppermute | solution.py:389
  6.5 18.5 %copy-start = (s32[32,16]{0,1:T(8,128)S(1)}, s32[32,16]{0,1:T(8,128)}, u32[]{:S(2)}) copy-start(s32[32,16]{0,1:T(8,128)} %param.9) | copy-start | bytes 6148
  7.9 12.4 %collective-permute-start.8 = (bf16[4,256,128]{2,1,0:T(8,128)(2,1)S(1)}, bf16[4,256,128]{2,1,0:T(8,128)(2,1)S(1)}, u32[]{:S(2)}, u32[]{:S(2)}) collective-permute-start(bf16[4,256,128]{2,1,0:T(8,128)(2,1)S(1)} %get-tuple-element.33), channel_id=1, source_target_pairs={{0,1},{1,0},{2,3},{3,2},{4,5},{5,4},{6,7},{7,6},{8,9},{9,8},{10,11... | collective-permute-start | bytes 786440 | tf_op jit(solution)/shard_map/ppermute | solution.py:391
  7.9 11.1 %collective-permute-start.1 = (bf16[2,256,128]{2,1,0:T(8,128)(2,1)S(1)}, bf16[2,256,128]{2,1,0:T(8,128)(2,1)S(1)}, u32[]{:S(2)}, u32[]{:S(2)}) collective-permute-start(bf16[2,256,128]{2,1,0:T(8,128)(2,1)S(1)} %get-tuple-element.28), channel_id=1, source_target_pairs={{0,1},{1,0},{2,3},{3,2},{4,5},{5,4},{6,7},{7,6},{8,9},{9,8},{10,11... | collective-permute-start | bytes 393224 | tf_op jit(solution)/shard_map/ppermute | solution.py:390
  9.9 9.7 %collective-permute-start.3 = (bf16[2,256,128]{2,1,0:T(8,128)(2,1)S(1)}, bf16[2,256,128]{2,1,0:T(8,128)(2,1)S(1)}, u32[]{:S(2)}, u32[]{:S(2)}) collective-permute-start(bf16[2,256,128]{2,1,0:T(8,128)(2,1)S(1)} %collective-permute-done.kv_ref), channel_id=1, source_target_pairs={{0,2},{4,6},{2,0},{6,4},{1,3},{5,7},{3,1},{7,5},{8,10},{12,14},{10... | collective-permute-start | bytes 393224 | tf_op jit(solution)/shard_map/ppermute | solution.py:374
  19.0 5.4 %collective-permute-start.5 = (bf16[2,256,128]{2,1,0:T(8,128)(2,1)S(1)}, bf16[2,256,128]{2,1,0:T(8,128)(2,1)S(1)}, u32[]{:S(2)}, u32[]{:S(2)}) collective-permute-start(bf16[2,256,128]{2,1,0:T(8,128)(2,1)S(1)} %collective-permute-done.kv_ref), channel_id=1, source_target_pairs={{2,4},{4,2},{3,5},{5,3},{10,12},{12,10},{11,13},{13,11},{18,20},{2... | collective-permute-start | bytes 393224 | tf_op jit(solution)/shard_map/ppermute | solution.py:374
  19.7 16.2 %collective-permute-start.9 = (bf16[4,256,128]{2,1,0:T(8,128)(2,1)S(1)}, bf16[4,256,128]{2,1,0:T(8,128)(2,1)S(1)}, u32[]{:S(2)}, u32[]{:S(2)}) collective-permute-start(bf16[4,256,128]{2,1,0:T(8,128)(2,1)S(1)} %get-tuple-element.34), channel_id=1, source_target_pairs={{0,1},{1,0},{2,3},{3,2},{4,5},{5,4},{6,7},{7,6},{8,9},{9,8},{10,11... | collective-permute-start | bytes 786440 | tf_op jit(solution)/shard_map/ppermute | solution.py:392
  20.2 15.6 %collective-permute-start.10 = (bf16[4,256,128]{2,1,0:T(8,128)(2,1)S(1)}, bf16[4,256,128]{2,1,0:T(8,128)(2,1)S(1)}, u32[]{:S(2)}, u32[]{:S(2)}) collective-permute-start(bf16[4,256,128]{2,1,0:T(8,128)(2,1)S(1)} %collective-permute-done.8.kv_ref), channel_id=1, source_target_pairs={{0,2},{4,6},{2,0},{6,4},{1,3},{5,7},{3,1},{7,5},{8,10},{12,14},{10... | collective-permute-start | bytes 786440 | tf_op jit(solution)/shard_map/ppermute | solution.py:374
  24.4 11.5 %collective-permute-start.11 = (bf16[4,256,128]{2,1,0:T(8,128)(2,1)S(1)}, bf16[4,256,128]{2,1,0:T(8,128)(2,1)S(1)}, u32[]{:S(2)}, u32[]{:S(2)}) collective-permute-start(bf16[4,256,128]{2,1,0:T(8,128)(2,1)S(1)} %collective-permute-done.8.kv_ref), channel_id=1, source_target_pairs={{2,4},{4,2},{3,5},{5,3},{10,12},{12,10},{11,13},{13,11},{18,20},{2... | collective-permute-start | bytes 786440 | tf_op jit(solution)/shard_map/ppermute | solution.py:374
  28.8 17.6 %collective-permute-start.7 = (bf16[4,256,128]{2,1,0:T(8,128)(2,1)S(1)}, bf16[4,256,128]{2,1,0:T(8,128)(2,1)S(1)}, u32[]{:S(2)}, u32[]{:S(2)}) collective-permute-start(bf16[4,256,128]{2,1,0:T(8,128)(2,1)S(1)} %get-tuple-element.32), channel_id=1, source_target_pairs={{2,4},{4,2},{3,5},{5,3},{10,12},{12,10},{11,13},{13,11},{18,20},{2... | collective-permute-start | bytes 786440 | tf_op jit(solution)/shard_map/ppermute | solution.py:374
  29.5 18.8 %collective-permute-start.6 = (bf16[4,256,128]{2,1,0:T(8,128)(2,1)S(1)}, bf16[4,256,128]{2,1,0:T(8,128)(2,1)S(1)}, u32[]{:S(2)}, u32[]{:S(2)}) collective-permute-start(bf16[4,256,128]{2,1,0:T(8,128)(2,1)S(1)} %get-tuple-element.31), channel_id=1, source_target_pairs={{0,2},{4,6},{2,0},{6,4},{1,3},{5,7},{3,1},{7,5},{8,10},{12,14},{10... | collective-permute-start | bytes 786440 | tf_op jit(solution)/shard_map/ppermute | solution.py:374
  39.2 10.3 %collective-permute-start.13 = (bf16[4,256,128]{2,1,0:T(8,128)(2,1)S(1)}, bf16[4,256,128]{2,1,0:T(8,128)(2,1)S(1)}, u32[]{:S(2)}, u32[]{:S(2)}) collective-permute-start(bf16[4,256,128]{2,1,0:T(8,128)(2,1)S(1)} %get-tuple-element.38), channel_id=1, source_target_pairs={{2,4},{4,2},{3,5},{5,3},{10,12},{12,10},{11,13},{13,11},{18,20},{2... | collective-permute-start | bytes 786440 | tf_op jit(solution)/shard_map/ppermute | solution.py:374
  39.9 9.6 %collective-permute-start.12 = (bf16[4,256,128]{2,1,0:T(8,128)(2,1)S(1)}, bf16[4,256,128]{2,1,0:T(8,128)(2,1)S(1)}, u32[]{:S(2)}, u32[]{:S(2)}) collective-permute-start(bf16[4,256,128]{2,1,0:T(8,128)(2,1)S(1)} %get-tuple-element.37), channel_id=1, source_target_pairs={{0,2},{4,6},{2,0},{6,4},{1,3},{5,7},{3,1},{7,5},{8,10},{12,14},{10... | collective-permute-start | bytes 786440 | tf_op jit(solution)/shard_map/ppermute | solution.py:374
  45.7 5.0 %collective-permute-start.15 = (bf16[4,256,128]{2,1,0:T(8,128)(2,1)S(1)}, bf16[4,256,128]{2,1,0:T(8,128)(2,1)S(1)}, u32[]{:S(2)}, u32[]{:S(2)}) collective-permute-start(bf16[4,256,128]{2,1,0:T(8,128)(2,1)S(1)} %get-tuple-element.42), channel_id=1, source_target_pairs={{2,4},{4,2},{3,5},{5,3},{10,12},{12,10},{11,13},{13,11},{18,20},{2... | collective-permute-start | bytes 786440 | tf_op jit(solution)/shard_map/ppermute | solution.py:374
  46.4 4.4 %collective-permute-start.14 = (bf16[4,256,128]{2,1,0:T(8,128)(2,1)S(1)}, bf16[4,256,128]{2,1,0:T(8,128)(2,1)S(1)}, u32[]{:S(2)}, u32[]{:S(2)}) collective-permute-start(bf16[4,256,128]{2,1,0:T(8,128)(2,1)S(1)} %get-tuple-element.41), channel_id=1, source_target_pairs={{0,2},{4,6},{2,0},{6,4},{1,3},{5,7},{3,1},{7,5},{8,10},{12,14},{10... | collective-permute-start | bytes 786440 | tf_op jit(solution)/shard_map/ppermute | solution.py:374
  48.5 15.3 %collective-permute-start.16 = (bf16[4,256,128]{2,1,0:T(8,128)(2,1)S(1)}, bf16[4,256,128]{2,1,0:T(8,128)(2,1)S(1)}, u32[]{:S(2)}, u32[]{:S(2)}) collective-permute-start(bf16[4,256,128]{2,1,0:T(8,128)(2,1)S(1)} %pad_maximum_fusion), channel_id=1, source_target_pairs={{0,1},{1,0},{2,3},{3,2},{4,5},{5,4},{6,7},{7,6},{8,9},{9,8},{10,11... | collective-permute-start | bytes 786440 | tf_op jit(solution)/shard_map/ppermute | solution.py:417
  49.7 14.1 %collective-permute-start.17 = (bf16[3,256,128]{2,1,0:T(8,128)(2,1)S(1)}, bf16[3,256,128]{2,1,0:T(8,128)(2,1)S(1)}, u32[]{:S(2)}, u32[]{:S(2)}) collective-permute-start(bf16[3,256,128]{2,1,0:T(8,128)(2,1)S(1)} %pad_maximum_fusion.1), channel_id=1, source_target_pairs={{0,1},{1,0},{2,3},{3,2},{4,5},{5,4},{6,7},{7,6},{8,9},{9,8},{10,11... | collective-permute-start | bytes 589832 | tf_op jit(solution)/shard_map/ppermute | solution.py:417
  50.9 12.9 %collective-permute-start.18 = (bf16[2,256,128]{2,1,0:T(8,128)(2,1)S(1)}, bf16[2,256,128]{2,1,0:T(8,128)(2,1)S(1)}, u32[]{:S(2)}, u32[]{:S(2)}) collective-permute-start(bf16[2,256,128]{2,1,0:T(8,128)(2,1)S(1)} %get-tuple-element.49), channel_id=1, source_target_pairs={{0,1},{1,0},{2,3},{3,2},{4,5},{5,4},{6,7},{7,6},{8,9},{9,8},{10,11... | collective-permute-start | bytes 393224 | tf_op jit(solution)/shard_map/ppermute | solution.py:417

commit v3 on v2

--- a/solution.py
+++ b/solution.py
@@ -138,9 +138,16 @@
     return (query_grad, key_grad, value_grad)
 
 
-def pairs_of(count, first):
-    low = range(first, count - 1, 2)
-    return [(i, i + 1) for i in low] + [(i + 1, i) for i in low]
+def pairs_of(count, first, groups):
+    route = []
+    for group in range(groups):
+        for row in range(count):
+            other = row + 1 if (row - first) % 2 == 0 else row - 1
+            if 0 <= other < count:
+                route.append((group * count + row, group * count + other))
+            elif groups % 2 == 0:
+                route.append((group * count + row, (group ^ 1) * count + row))
+    return route
 
 
 def neighbour_rows(row):
@@ -365,13 +372,14 @@
     half = heads // 2
     rows = lax.axis_size("sy")
     swap = [(0, 1), (1, 0)]
-    even_pairs, odd_pairs = pairs_of(rows, 0), pairs_of(rows, 1)
+    even_pairs, odd_pairs = [pairs_of(rows, first, lax.axis_size("tp")) for first in range(2)]
     arrays = [a.reshape(heads, tokens, width) for a in (key_vectors, value_vectors, queries, out_grad)]
     later = range(1, half)
 
     def rows_sent(even_block, odd_block):
         return (
-            lax.ppermute(even_block, "sy", even_pairs), lax.ppermute(odd_block, "sy", odd_pairs)
+            lax.ppermute(even_block, ("tp", "sy"), even_pairs),
+            lax.ppermute(odd_block, ("tp", "sy"), odd_pairs),
         )
 
     key_value, query_grad_pair = (0, 1), (2, 3)

time: 65.3 us -> 57.4 us (0.88)
  the two profiles are of different devices: /device:TPU:0 before, /device:TPU:1 now
where the time goes in v3:
time: 57.4 us; the launch traced here: 56.2 us
  waiting for transfers between devices  20.6 us (36%)
  starting transfers between devices  19.6 us (34%)
  Pallas kernels  14.8 us (26%)
  between operations  0.78 us (1%)
    pallas_call x3, Pallas kernels, head_grads(): pl.pallas_call(functools.partial(head_kernel, h, place), out_shape=(pltpu...  9.99 us
    ppermute x3, waiting for transfers between devices, swapped(): theirs.append(lax.ppermute(outgoing, 'sx', swap))  8.44 us
    ppermute x6, starting transfers between devices, rows_sent(): lax.ppermute(odd_block, ('tp', 'sy'), odd_pairs)  7.47 us
    ppermute x1, waiting for transfers between devices, swapped(): qg_first = lax.ppermute(first_qg, 'sx', swap)  6.81 us
    ppermute x6, starting transfers between devices, rows_sent(): lax.ppermute(even_block, ('tp', 'sy'), even_pairs)  5.6 us
    ppermute x6, waiting for transfers between devices, rows_sent(): lax.ppermute(odd_block, ('tp', 'sy'), odd_pairs)  4.82 us
    pallas_call x3, Pallas kernels, packed(): pl.pallas_call(functools.partial(pack_kernel, picks), out_shape=tuple((pl...  3.35 us
    ppermute x3, starting transfers between devices, swapped(): theirs.append(lax.ppermute(outgoing, 'sx', swap))  2.68 us
  transfers between devices with their start and end apart: 19, of which 5 were waited for; matrix products, arithmetic and copies ran while one was open for 1% of the time, Pallas kernels for 22%

profile of v3, /device:TPU:1, one launch (start us, length us, event | category | flops | bytes accessed | tf_op | source)
XLA Modules:
  0.0 56.2 jit_solution(17927230507220762099)
XLA Ops:
  0.6 1.1 %shard_map.76 = (bf16[6,256,128]{2,1,0:T(8,128)(2,1)S(1)}, bf16[2,256,128]{2,1,0:T(8,128)(2,1)S(1)}) custom-call(bf16[6,256,128]{2,1,0:T(8,128)(2,1)} %bitcast.13, bf16[6,256,128]{2,1,0:T(8,128)(2,1)} %bitcast.16, bf16[6,256,128]{2,1,0:T(8,128)(2,1)} %bitcast.19, bf16[6,256,128]{2,1,0:T(8,128)(2,1)} %bitcast.22), custom_call_target="tpu_custom_call" | custom-call | tf_op jit(solution)/shard_map/pallas_call | solution.py:182
  1.8 0.1 collective-permute-start.2
  1.9 2.7 %collective-permute-start.4 = (bf16[6,256,128]{2,1,0:T(8,128)(2,1)S(1)}, bf16[6,256,128]{2,1,0:T(8,128)(2,1)S(1)}, u32[]{:S(2)}, u32[]{:S(2)}) collective-permute-start(bf16[6,256,128]{2,1,0:T(8,128)(2,1)S(1)} %get-tuple-element.26.own_kv_ref), channel_id=1, source_target_pairs={{0,8},{2,4},{4,2},{6,14},{8,0},{10,12},{12,10},{14,6},{16,24},{18,... | collective-permute-start | bytes 1179656 | tf_op jit(solution)/shard_map/ppermute | solution.py:382
  4.5 0.9 %shard_map.78 = bf16[2,256,128]{2,1,0:T(8,128)(2,1)S(1)} custom-call(bf16[6,256,128]{2,1,0:T(8,128)(2,1)} %bitcast.14, bf16[6,256,128]{2,1,0:T(8,128)(2,1)} %bitcast.17, bf16[6,256,128]{2,1,0:T(8,128)(2,1)} %bitcast.20, bf16[6,256,128]{2,1,0:T(8,128)(2,1)} %bitcast.23), custom_call_target="tpu_custom_call" | custom-call | tf_op jit(solution)/shard_map/pallas_call | solution.py:182
  5.4 1.3 %collective-permute-start = (bf16[2,256,128]{2,1,0:T(8,128)(2,1)S(1)}, bf16[2,256,128]{2,1,0:T(8,128)(2,1)S(1)}, u32[]{:S(2)}, u32[]{:S(2)}) collective-permute-start(bf16[2,256,128]{2,1,0:T(8,128)(2,1)S(1)} %shard_map.78), channel_id=1, source_target_pairs={{0,1},{1,0},{2,3},{3,2},{4,5},{5,4},{6,7},{7,6},{8,9},{9,8},{10,11... | collective-permute-start | bytes 393224 | tf_op jit(solution)/shard_map/ppermute | solution.py:397
  6.7 0.0 copy-start
  6.7 1.3 %shard_map.77 = (bf16[4,256,128]{2,1,0:T(8,128)(2,1)S(1)}, bf16[4,256,128]{2,1,0:T(8,128)(2,1)S(1)}, bf16[6,256,128]{2,1,0:T(8,128)(2,1)S(1)}) custom-call(bf16[6,256,128]{2,1,0:T(8,128)(2,1)} %bitcast.15, bf16[6,256,128]{2,1,0:T(8,128)(2,1)} %bitcast.18, bf16[6,256,128]{2,1,0:T(8,128)(2,1)} %bitcast.21, bf16[6,256,128]{2,1,0:T(8,128)(2,1)} %bitcast.24), custom_call_target="tpu_custom_call" | custom-call | tf_op jit(solution)/shard_map/pallas_call | solution.py:182
  8.0 0.3 collective-permute-start.8
  8.3 1.2 %collective-permute-start.1 = (bf16[2,256,128]{2,1,0:T(8,128)(2,1)S(1)}, bf16[2,256,128]{2,1,0:T(8,128)(2,1)S(1)}, u32[]{:S(2)}, u32[]{:S(2)}) collective-permute-start(bf16[2,256,128]{2,1,0:T(8,128)(2,1)S(1)} %get-tuple-element.28), channel_id=1, source_target_pairs={{0,1},{1,0},{2,3},{3,2},{4,5},{5,4},{6,7},{7,6},{8,9},{9,8},{10,11... | collective-permute-start | bytes 393224 | tf_op jit(solution)/shard_map/ppermute | solution.py:398
  9.6 0.5 collective-permute-done.kv_ref
  10.0 1.5 %collective-permute-start.3 = (bf16[2,256,128]{2,1,0:T(8,128)(2,1)S(1)}, bf16[2,256,128]{2,1,0:T(8,128)(2,1)S(1)}, u32[]{:S(2)}, u32[]{:S(2)}) collective-permute-start(bf16[2,256,128]{2,1,0:T(8,128)(2,1)S(1)} %collective-permute-done.kv_ref), channel_id=1, source_target_pairs={{0,2},{2,0},{4,6},{6,4},{8,10},{10,8},{12,14},{14,12},{16,18},{18,... | collective-permute-start | bytes 393224 | tf_op jit(solution)/shard_map/ppermute | solution.py:381
  11.5 6.8 %collective-permute-done.1.qg_ref = bf16[2,256,128]{2,1,0:T(8,128)(2,1)S(1)} collective-permute-done((bf16[2,256,128]{2,1,0:T(8,128)(2,1)S(1)}, bf16[2,256,128]{2,1,0:T(8,128)(2,1)S(1)}, u32[]{:S(2)}, u32[]{:S(2)}) %collective-permute-start.1) | collective-permute-done | bytes 131104 | tf_op jit(solution)/shard_map/ppermute | solution.py:398
  18.4 2.5 %collective-permute-start.5 = (bf16[2,256,128]{2,1,0:T(8,128)(2,1)S(1)}, bf16[2,256,128]{2,1,0:T(8,128)(2,1)S(1)}, u32[]{:S(2)}, u32[]{:S(2)}) collective-permute-start(bf16[2,256,128]{2,1,0:T(8,128)(2,1)S(1)} %collective-permute-done.kv_ref), channel_id=1, source_target_pairs={{0,8},{2,4},{4,2},{6,14},{8,0},{10,12},{12,10},{14,6},{16,24},{18,... | collective-permute-start | bytes 393224 | tf_op jit(solution)/shard_map/ppermute | solution.py:382
  20.9 0.0 collective-permute-done.3.even_ref
  20.9 1.0 %collective-permute-start.9 = (bf16[4,256,128]{2,1,0:T(8,128)(2,1)S(1)}, bf16[4,256,128]{2,1,0:T(8,128)(2,1)S(1)}, u32[]{:S(2)}, u32[]{:S(2)}) collective-permute-start(bf16[4,256,128]{2,1,0:T(8,128)(2,1)S(1)} %get-tuple-element.34), channel_id=1, source_target_pairs={{0,1},{1,0},{2,3},{3,2},{4,5},{5,4},{6,7},{7,6},{8,9},{9,8},{10,11... | collective-permute-start | bytes 786440 | tf_op jit(solution)/shard_map/ppermute | solution.py:400
  21.9 0.0 collective-permute-done.8.kv_ref
  21.9 0.6 %collective-permute-start.10 = (bf16[4,256,128]{2,1,0:T(8,128)(2,1)S(1)}, bf16[4,256,128]{2,1,0:T(8,128)(2,1)S(1)}, u32[]{:S(2)}, u32[]{:S(2)}) collective-permute-start(bf16[4,256,128]{2,1,0:T(8,128)(2,1)S(1)} %collective-permute-done.8.kv_ref), channel_id=1, source_target_pairs={{0,2},{2,0},{4,6},{6,4},{8,10},{10,8},{12,14},{14,12},{16,18},{18,... | collective-permute-start | bytes 786440 | tf_op jit(solution)/shard_map/ppermute | solution.py:381
  22.5 1.3 %collective-permute-done.5.odd_ref = bf16[2,256,128]{2,1,0:T(8,128)(2,1)S(1)} collective-permute-done((bf16[2,256,128]{2,1,0:T(8,128)(2,1)S(1)}, bf16[2,256,128]{2,1,0:T(8,128)(2,1)S(1)}, u32[]{:S(2)}, u32[]{:S(2)}) %collective-permute-start.5) | collective-permute-done | bytes 131104 | tf_op jit(solution)/shard_map/ppermute | solution.py:382
  23.8 1.4 %collective-permute-start.11 = (bf16[4,256,128]{2,1,0:T(8,128)(2,1)S(1)}, bf16[4,256,128]{2,1,0:T(8,128)(2,1)S(1)}, u32[]{:S(2)}, u32[]{:S(2)}) collective-permute-start(bf16[4,256,128]{2,1,0:T(8,128)(2,1)S(1)} %collective-permute-done.8.kv_ref), channel_id=1, source_target_pairs={{0,8},{2,4},{4,2},{6,14},{8,0},{10,12},{12,10},{14,6},{16,24},{18,... | collective-permute-start | bytes 786440 | tf_op jit(solution)/shard_map/ppermute | solution.py:382
  25.3 0.0 copy-done
  25.3 0.1 copy.8.valid_ref
  25.3 0.3 window_bias.1.bias_ref
  25.7 0.0 collective-permute-done.2.even_own_ref
  25.7 0.0 collective-permute-done.4.odd_own_ref
  25.7 3.3 %head_grads.3 = (bf16[256,128]{1,0:T(8,128)(2,1)S(1)}, bf16[256,128]{1,0:T(8,128)(2,1)S(1)}, f32[4,256,128]{2,1,0:T(8,128)S(1)}, bf16[4,256,128]{2,1,0:T(8,128)(2,1)S(1)}, bf16[4,256,128]{2,1,0:T(8,128)(2,1)S(1)}) custom-call(bf16[6,256,128]{2,1,0:T(8,128)(2,1)S(1)} %get-tuple-element.26.own_kv_ref, bf16[6,256,128]{2,1,0:T(8,128)(2,1)S(1)} %get-tuple-element.27.own_qg_ref, ...), custom_call_target="tpu_custom_call" | custom-call | flops 1006632960 | bytes 1310720 | tf_op jit(solution)/shard_map/head_grads/pallas_call | solution.py:309
  29.0 0.4 collective-permute-start.7
  29.4 1.3 %collective-permute-start.6 = (bf16[4,256,128]{2,1,0:T(8,128)(2,1)S(1)}, bf16[4,256,128]{2,1,0:T(8,128)(2,1)S(1)}, u32[]{:S(2)}, u32[]{:S(2)}) collective-permute-start(bf16[4,256,128]{2,1,0:T(8,128)(2,1)S(1)} %get-tuple-element.31), channel_id=1, source_target_pairs={{0,2},{2,0},{4,6},{6,4},{8,10},{10,8},{12,14},{14,12},{16,18},{18,... | collective-permute-start | bytes 786440 | tf_op jit(solution)/shard_map/ppermute | solution.py:381
  30.6 0.0 collective-permute-done.9.qg_ref
  30.6 0.0 collective-permute-done.10.even_ref
  30.6 0.0 collective-permute-done.11.odd_ref
  30.7 3.3 %head_grads.4 = (bf16[256,128]{1,0:T(8,128)(2,1)S(1)}, bf16[256,128]{1,0:T(8,128)(2,1)S(1)}, f32[4,256,128]{2,1,0:T(8,128)S(1)}, bf16[4,256,128]{2,1,0:T(8,128)(2,1)S(1)}, bf16[4,256,128]{2,1,0:T(8,128)(2,1)S(1)}) custom-call(bf16[6,256,128]{2,1,0:T(8,128)(2,1)S(1)} %get-tuple-element.26.own_kv_ref, bf16[6,256,128]{2,1,0:T(8,128)(2,1)S(1)} %get-tuple-element.27.own_qg_ref, ...), custom_call_target="tpu_custom_call" | custom-call | flops 1006632960 | bytes 1310720 | tf_op jit(solution)/shard_map/head_grads/pallas_call | solution.py:309
  34.0 0.5 collective-permute-start.13
  34.4 1.5 %collective-permute-start.12 = (bf16[4,256,128]{2,1,0:T(8,128)(2,1)S(1)}, bf16[4,256,128]{2,1,0:T(8,128)(2,1)S(1)}, u32[]{:S(2)}, u32[]{:S(2)}) collective-permute-start(bf16[4,256,128]{2,1,0:T(8,128)(2,1)S(1)} %get-tuple-element.37), channel_id=1, source_target_pairs={{0,2},{2,0},{4,6},{6,4},{8,10},{10,8},{12,14},{14,12},{16,18},{18,... | collective-permute-start | bytes 786440 | tf_op jit(solution)/shard_map/ppermute | solution.py:381
  36.0 3.3 %head_grads.5 = (bf16[256,128]{1,0:T(8,128)(2,1)S(1)}, bf16[256,128]{1,0:T(8,128)(2,1)S(1)}, f32[4,256,128]{2,1,0:T(8,128)S(1)}, bf16[4,256,128]{2,1,0:T(8,128)(2,1)S(1)}, bf16[4,256,128]{2,1,0:T(8,128)(2,1)S(1)}) custom-call(bf16[6,256,128]{2,1,0:T(8,128)(2,1)S(1)} %get-tuple-element.26.own_kv_ref, bf16[6,256,128]{2,1,0:T(8,128)(2,1)S(1)} %get-tuple-element.27.own_qg_ref, ...), custom_call_target="tpu_custom_call" | custom-call | flops 1006632960 | bytes 1310720 | tf_op jit(solution)/shard_map/head_grads/pallas_call | solution.py:309
  39.3 0.1 collective-permute-start.15
  39.4 0.0 collective-permute-done.7
  39.4 0.6 %collective-permute-start.14 = (bf16[4,256,128]{2,1,0:T(8,128)(2,1)S(1)}, bf16[4,256,128]{2,1,0:T(8,128)(2,1)S(1)}, u32[]{:S(2)}, u32[]{:S(2)}) collective-permute-start(bf16[4,256,128]{2,1,0:T(8,128)(2,1)S(1)} %get-tuple-element.41), channel_id=1, source_target_pairs={{0,2},{2,0},{4,6},{6,4},{8,10},{10,8},{12,14},{14,12},{16,18},{18,... | collective-permute-start | bytes 786440 | tf_op jit(solution)/shard_map/ppermute | solution.py:381
  40.0 0.0 collective-permute-done.6
  40.0 0.1 add_convert_fusion.2
  40.1 1.3 %collective-permute-start.16 = (bf16[4,256,128]{2,1,0:T(8,128)(2,1)S(1)}, bf16[4,256,128]{2,1,0:T(8,128)(2,1)S(1)}, u32[]{:S(2)}, u32[]{:S(2)}) collective-permute-start(bf16[4,256,128]{2,1,0:T(8,128)(2,1)S(1)} %pad_maximum_fusion), channel_id=1, source_target_pairs={{0,1},{1,0},{2,3},{3,2},{4,5},{5,4},{6,7},{7,6},{8,9},{9,8},{10,11... | collective-permute-start | bytes 786440 | tf_op jit(solution)/shard_map/ppermute | solution.py:425
  41.4 0.0 collective-permute-done.13
  41.4 0.0 collective-permute-done.12
  41.4 0.1 add_convert_fusion.1
  41.6 0.3 collective-permute-start.17
  41.9 3.5 %collective-permute-done.15 = bf16[4,256,128]{2,1,0:T(8,128)(2,1)S(1)} collective-permute-done((bf16[4,256,128]{2,1,0:T(8,128)(2,1)S(1)}, bf16[4,256,128]{2,1,0:T(8,128)(2,1)S(1)}, u32[]{:S(2)}, u32[]{:S(2)}) %collective-permute-start.15) | collective-permute-done | bytes 262176 | tf_op jit(solution)/shard_map/ppermute | solution.py:382
  45.4 0.0 collective-permute-done.14
  45.4 0.1 add_convert_fusion
  45.6 1.1 %collective-permute-start.18 = (bf16[2,256,128]{2,1,0:T(8,128)(2,1)S(1)}, bf16[2,256,128]{2,1,0:T(8,128)(2,1)S(1)}, u32[]{:S(2)}, u32[]{:S(2)}) collective-permute-start(bf16[2,256,128]{2,1,0:T(8,128)(2,1)S(1)} %get-tuple-element.49), channel_id=1, source_target_pairs={{0,1},{1,0},{2,3},{3,2},{4,5},{5,4},{6,7},{7,6},{8,9},{9,8},{10,11... | collective-permute-start | bytes 393224 | tf_op jit(solution)/shard_map/ppermute | solution.py:425
  46.7 8.4 %collective-permute-done.18.refs_8_ = bf16[2,256,128]{2,1,0:T(8,128)(2,1)S(1)} collective-permute-done((bf16[2,256,128]{2,1,0:T(8,128)(2,1)S(1)}, bf16[2,256,128]{2,1,0:T(8,128)(2,1)S(1)}, u32[]{:S(2)}, u32[]{:S(2)}) %collective-permute-start.18) | collective-permute-done | bytes 131104 | tf_op jit(solution)/shard_map/ppermute | solution.py:425
  55.1 0.0 collective-permute-done.16.refs_6_
  55.1 0.0 collective-permute-done.17.refs_7_
  55.1 1.1 %collected.1 = (bf16[6,256,128]{2,1,0:T(8,128)(2,1)}, bf16[6,256,128]{2,1,0:T(8,128)(2,1)}, bf16[6,256,128]{2,1,0:T(8,128)(2,1)}) custom-call(bf16[256,128]{1,0:T(8,128)(2,1)S(1)} %get-tuple-element.29.refs_0_, bf16[2,256,128]{2,1,0:T(8,128)(2,1)S(1)} %get-tuple-element.54.refs_1_, bf16[256,128]{1,0:T(8,128)(2,1)S(1)} %get-tuple-element.35.refs_2_, ...), custom_call_target="tpu_custom_call" | custom-call | tf_op jit(solution)/shard_map/collected/pallas_call | solution.py:358
  (5 shorter events, 0.1 us)
Async XLA Ops:
  1.8 23.9 %collective-permute-start.2 = (bf16[6,256,128]{2,1,0:T(8,128)(2,1)S(1)}, bf16[6,256,128]{2,1,0:T(8,128)(2,1)S(1)}, u32[]{:S(2)}, u32[]{:S(2)}) collective-permute-start(bf16[6,256,128]{2,1,0:T(8,128)(2,1)S(1)} %get-tuple-element.26.own_kv_ref), channel_id=1, source_target_pairs={{0,2},{2,0},{4,6},{6,4},{8,10},{10,8},{12,14},{14,12},{16,18},{18,... | collective-permute-start | bytes 1179656 | tf_op jit(solution)/shard_map/ppermute | solution.py:381
  1.9 23.8 %collective-permute-start.4 = (bf16[6,256,128]{2,1,0:T(8,128)(2,1)S(1)}, bf16[6,256,128]{2,1,0:T(8,128)(2,1)S(1)}, u32[]{:S(2)}, u32[]{:S(2)}) collective-permute-start(bf16[6,256,128]{2,1,0:T(8,128)(2,1)S(1)} %get-tuple-element.26.own_kv_ref), channel_id=1, source_target_pairs={{0,8},{2,4},{4,2},{6,14},{8,0},{10,12},{12,10},{14,6},{16,24},{18,... | collective-permute-start | bytes 1179656 | tf_op jit(solution)/shard_map/ppermute | solution.py:382
  5.4 4.6 %collective-permute-start = (bf16[2,256,128]{2,1,0:T(8,128)(2,1)S(1)}, bf16[2,256,128]{2,1,0:T(8,128)(2,1)S(1)}, u32[]{:S(2)}, u32[]{:S(2)}) collective-permute-start(bf16[2,256,128]{2,1,0:T(8,128)(2,1)S(1)} %shard_map.78), channel_id=1, source_target_pairs={{0,1},{1,0},{2,3},{3,2},{4,5},{5,4},{6,7},{7,6},{8,9},{9,8},{10,11... | collective-permute-start | bytes 393224 | tf_op jit(solution)/shard_map/ppermute | solution.py:397
  6.7 18.5 %copy-start = (s32[32,16]{0,1:T(8,128)S(1)}, s32[32,16]{0,1:T(8,128)}, u32[]{:S(2)}) copy-start(s32[32,16]{0,1:T(8,128)} %param.9) | copy-start | bytes 6148
  8.0 13.9 %collective-permute-start.8 = (bf16[4,256,128]{2,1,0:T(8,128)(2,1)S(1)}, bf16[4,256,128]{2,1,0:T(8,128)(2,1)S(1)}, u32[]{:S(2)}, u32[]{:S(2)}) collective-permute-start(bf16[4,256,128]{2,1,0:T(8,128)(2,1)S(1)} %get-tuple-element.33), channel_id=1, source_target_pairs={{0,1},{1,0},{2,3},{3,2},{4,5},{5,4},{6,7},{7,6},{8,9},{9,8},{10,11... | collective-permute-start | bytes 786440 | tf_op jit(solution)/shard_map/ppermute | solution.py:399
  8.3 10.0 %collective-permute-start.1 = (bf16[2,256,128]{2,1,0:T(8,128)(2,1)S(1)}, bf16[2,256,128]{2,1,0:T(8,128)(2,1)S(1)}, u32[]{:S(2)}, u32[]{:S(2)}) collective-permute-start(bf16[2,256,128]{2,1,0:T(8,128)(2,1)S(1)} %get-tuple-element.28), channel_id=1, source_target_pairs={{0,1},{1,0},{2,3},{3,2},{4,5},{5,4},{6,7},{7,6},{8,9},{9,8},{10,11... | collective-permute-start | bytes 393224 | tf_op jit(solution)/shard_map/ppermute | solution.py:398
  10.0 10.8 %collective-permute-start.3 = (bf16[2,256,128]{2,1,0:T(8,128)(2,1)S(1)}, bf16[2,256,128]{2,1,0:T(8,128)(2,1)S(1)}, u32[]{:S(2)}, u32[]{:S(2)}) collective-permute-start(bf16[2,256,128]{2,1,0:T(8,128)(2,1)S(1)} %collective-permute-done.kv_ref), channel_id=1, source_target_pairs={{0,2},{2,0},{4,6},{6,4},{8,10},{10,8},{12,14},{14,12},{16,18},{18,... | collective-permute-start | bytes 393224 | tf_op jit(solution)/shard_map/ppermute | solution.py:381
  18.4 5.4 %collective-permute-start.5 = (bf16[2,256,128]{2,1,0:T(8,128)(2,1)S(1)}, bf16[2,256,128]{2,1,0:T(8,128)(2,1)S(1)}, u32[]{:S(2)}, u32[]{:S(2)}) collective-permute-start(bf16[2,256,128]{2,1,0:T(8,128)(2,1)S(1)} %collective-permute-done.kv_ref), channel_id=1, source_target_pairs={{0,8},{2,4},{4,2},{6,14},{8,0},{10,12},{12,10},{14,6},{16,24},{18,... | collective-permute-start | bytes 393224 | tf_op jit(solution)/shard_map/ppermute | solution.py:382
  20.9 9.8 %collective-permute-start.9 = (bf16[4,256,128]{2,1,0:T(8,128)(2,1)S(1)}, bf16[4,256,128]{2,1,0:T(8,128)(2,1)S(1)}, u32[]{:S(2)}, u32[]{:S(2)}) collective-permute-start(bf16[4,256,128]{2,1,0:T(8,128)(2,1)S(1)} %get-tuple-element.34), channel_id=1, source_target_pairs={{0,1},{1,0},{2,3},{3,2},{4,5},{5,4},{6,7},{7,6},{8,9},{9,8},{10,11... | collective-permute-start | bytes 786440 | tf_op jit(solution)/shard_map/ppermute | solution.py:400
  21.9 8.8 %collective-permute-start.10 = (bf16[4,256,128]{2,1,0:T(8,128)(2,1)S(1)}, bf16[4,256,128]{2,1,0:T(8,128)(2,1)S(1)}, u32[]{:S(2)}, u32[]{:S(2)}) collective-permute-start(bf16[4,256,128]{2,1,0:T(8,128)(2,1)S(1)} %collective-permute-done.8.kv_ref), channel_id=1, source_target_pairs={{0,2},{2,0},{4,6},{6,4},{8,10},{10,8},{12,14},{14,12},{16,18},{18,... | collective-permute-start | bytes 786440 | tf_op jit(solution)/shard_map/ppermute | solution.py:381
  23.8 6.8 %collective-permute-start.11 = (bf16[4,256,128]{2,1,0:T(8,128)(2,1)S(1)}, bf16[4,256,128]{2,1,0:T(8,128)(2,1)S(1)}, u32[]{:S(2)}, u32[]{:S(2)}) collective-permute-start(bf16[4,256,128]{2,1,0:T(8,128)(2,1)S(1)} %collective-permute-done.8.kv_ref), channel_id=1, source_target_pairs={{0,8},{2,4},{4,2},{6,14},{8,0},{10,12},{12,10},{14,6},{16,24},{18,... | collective-permute-start | bytes 786440 | tf_op jit(solution)/shard_map/ppermute | solution.py:382
  29.0 10.3 %collective-permute-start.7 = (bf16[4,256,128]{2,1,0:T(8,128)(2,1)S(1)}, bf16[4,256,128]{2,1,0:T(8,128)(2,1)S(1)}, u32[]{:S(2)}, u32[]{:S(2)}) collective-permute-start(bf16[4,256,128]{2,1,0:T(8,128)(2,1)S(1)} %get-tuple-element.32), channel_id=1, source_target_pairs={{0,8},{2,4},{4,2},{6,14},{8,0},{10,12},{12,10},{14,6},{16,24},{18,... | collective-permute-start | bytes 786440 | tf_op jit(solution)/shard_map/ppermute | solution.py:382
  29.4 10.6 %collective-permute-start.6 = (bf16[4,256,128]{2,1,0:T(8,128)(2,1)S(1)}, bf16[4,256,128]{2,1,0:T(8,128)(2,1)S(1)}, u32[]{:S(2)}, u32[]{:S(2)}) collective-permute-start(bf16[4,256,128]{2,1,0:T(8,128)(2,1)S(1)} %get-tuple-element.31), channel_id=1, source_target_pairs={{0,2},{2,0},{4,6},{6,4},{8,10},{10,8},{12,14},{14,12},{16,18},{18,... | collective-permute-start | bytes 786440 | tf_op jit(solution)/shard_map/ppermute | solution.py:381
  34.0 7.4 %collective-permute-start.13 = (bf16[4,256,128]{2,1,0:T(8,128)(2,1)S(1)}, bf16[4,256,128]{2,1,0:T(8,128)(2,1)S(1)}, u32[]{:S(2)}, u32[]{:S(2)}) collective-permute-start(bf16[4,256,128]{2,1,0:T(8,128)(2,1)S(1)} %get-tuple-element.38), channel_id=1, source_target_pairs={{0,8},{2,4},{4,2},{6,14},{8,0},{10,12},{12,10},{14,6},{16,24},{18,... | collective-permute-start | bytes 786440 | tf_op jit(solution)/shard_map/ppermute | solution.py:382
  34.4 7.0 %collective-permute-start.12 = (bf16[4,256,128]{2,1,0:T(8,128)(2,1)S(1)}, bf16[4,256,128]{2,1,0:T(8,128)(2,1)S(1)}, u32[]{:S(2)}, u32[]{:S(2)}) collective-permute-start(bf16[4,256,128]{2,1,0:T(8,128)(2,1)S(1)} %get-tuple-element.37), channel_id=1, source_target_pairs={{0,2},{2,0},{4,6},{6,4},{8,10},{10,8},{12,14},{14,12},{16,18},{18,... | collective-permute-start | bytes 786440 | tf_op jit(solution)/shard_map/ppermute | solution.py:381
  39.3 6.2 %collective-permute-start.15 = (bf16[4,256,128]{2,1,0:T(8,128)(2,1)S(1)}, bf16[4,256,128]{2,1,0:T(8,128)(2,1)S(1)}, u32[]{:S(2)}, u32[]{:S(2)}) collective-permute-start(bf16[4,256,128]{2,1,0:T(8,128)(2,1)S(1)} %get-tuple-element.42), channel_id=1, source_target_pairs={{0,8},{2,4},{4,2},{6,14},{8,0},{10,12},{12,10},{14,6},{16,24},{18,... | collective-permute-start | bytes 786440 | tf_op jit(solution)/shard_map/ppermute | solution.py:382
  39.4 6.1 %collective-permute-start.14 = (bf16[4,256,128]{2,1,0:T(8,128)(2,1)S(1)}, bf16[4,256,128]{2,1,0:T(8,128)(2,1)S(1)}, u32[]{:S(2)}, u32[]{:S(2)}) collective-permute-start(bf16[4,256,128]{2,1,0:T(8,128)(2,1)S(1)} %get-tuple-element.41), channel_id=1, source_target_pairs={{0,2},{2,0},{4,6},{6,4},{8,10},{10,8},{12,14},{14,12},{16,18},{18,... | collective-permute-start | bytes 786440 | tf_op jit(solution)/shard_map/ppermute | solution.py:381
  40.1 14.9 %collective-permute-start.16 = (bf16[4,256,128]{2,1,0:T(8,128)(2,1)S(1)}, bf16[4,256,128]{2,1,0:T(8,128)(2,1)S(1)}, u32[]{:S(2)}, u32[]{:S(2)}) collective-permute-start(bf16[4,256,128]{2,1,0:T(8,128)(2,1)S(1)} %pad_maximum_fusion), channel_id=1, source_target_pairs={{0,1},{1,0},{2,3},{3,2},{4,5},{5,4},{6,7},{7,6},{8,9},{9,8},{10,11... | collective-permute-start | bytes 786440 | tf_op jit(solution)/shard_map/ppermute | solution.py:425
  41.6 13.5 %collective-permute-start.17 = (bf16[3,256,128]{2,1,0:T(8,128)(2,1)S(1)}, bf16[3,256,128]{2,1,0:T(8,128)(2,1)S(1)}, u32[]{:S(2)}, u32[]{:S(2)}) collective-permute-start(bf16[3,256,128]{2,1,0:T(8,128)(2,1)S(1)} %pad_maximum_fusion.1), channel_id=1, source_target_pairs={{0,1},{1,0},{2,3},{3,2},{4,5},{5,4},{6,7},{7,6},{8,9},{9,8},{10,11... | collective-permute-start | bytes 589832 | tf_op jit(solution)/shard_map/ppermute | solution.py:425
  45.6 9.5 %collective-permute-start.18 = (bf16[2,256,128]{2,1,0:T(8,128)(2,1)S(1)}, bf16[2,256,128]{2,1,0:T(8,128)(2,1)S(1)}, u32[]{:S(2)}, u32[]{:S(2)}) collective-permute-start(bf16[2,256,128]{2,1,0:T(8,128)(2,1)S(1)} %get-tuple-element.49), channel_id=1, source_target_pairs={{0,1},{1,0},{2,3},{3,2},{4,5},{5,4},{6,7},{7,6},{8,9},{9,8},{10,11... | collective-permute-start | bytes 393224 | tf_op jit(solution)/shard_map/ppermute | solution.py:425

commit v4 on v3

--- a/solution.py
+++ b/solution.py
@@ -237,7 +237,7 @@
 
 
 def head_kernel(
-    h, place,
+    h,
     own_kv_ref, own_qg_ref, kv_ref, qg_ref, even_own_ref, even_ref, odd_own_ref, odd_ref, bias_ref,
     own_dq_ref, partner_dq_ref, middle_ref, even_part_ref, odd_part_ref,
     score_ref, dprob_ref, key_sum_ref, value_sum_ref,
@@ -247,7 +247,7 @@
     exponent_scale = math.log2(math.e) / math.sqrt(width)
     sides = ((own_kv_ref, kv_ref), (even_own_ref, even_ref), (odd_own_ref, odd_ref))
     keys, values = [
-        [ref.at[first + i] for side in sides for ref, first in zip(side, (2 * h, place))]
+        [ref.at[first + i] for side in sides for ref, first in zip(side, (2 * h, 0))]
         for i in range(2)
     ]
     key_parts, value_parts = [
@@ -256,7 +256,7 @@
     ]
     blocks = (
         (own_qg_ref[2 * h], own_qg_ref[2 * h + 1], own_dq_ref),
-        (qg_ref[place], qg_ref[place + 1], partner_dq_ref),
+        (qg_ref[0], qg_ref[1], partner_dq_ref),
     )
     for b, (query_rows, grad_rows, dq_ref) in enumerate(blocks):
         row_max = None
@@ -302,12 +302,12 @@
         dq_ref[...] = (query_grad * score_scale).astype(jnp.bfloat16)
 
 
-def head_grads(h, place, arrays, bias):
+def head_grads(h, arrays, bias):
     tokens, width = arrays[0].shape[1:]
     low = jnp.bfloat16
     pairs = 2 * 6 * tokens * tokens
     return pl.pallas_call(
-        functools.partial(head_kernel, h, place),
+        functools.partial(head_kernel, h),
         out_shape=(
             pltpu.VMEM((tokens, width), low),
             pltpu.VMEM((tokens, width), low),
@@ -382,36 +382,31 @@
             lax.ppermute(odd_block, ("tp", "sy"), odd_pairs),
         )
 
-    key_value, query_grad_pair = (0, 1), (2, 3)
-    first_kv, = packed(arrays, [[(a, 0, False) for a in key_value]])
-    own_kv, first_qg = packed(
+    key_value, query_and_grad = (0, 1), (2, 3)
+
+    def picks(head_range, side, mine):
+        return [(a, h, mine) for h in head_range for a in side]
+
+    kv_out, qg_out = [None] * half, [None] * half
+    kv_out[0], = packed(arrays, [picks([0], key_value, False)])
+    own_kv, qg_out[0] = packed(
+        arrays, [picks(range(half), key_value, True), picks([0], query_and_grad, False)]
+    )
+    own_qg, *rest = packed(
         arrays,
-        [[(a, h, True) for h in range(half) for a in key_value]]
-        + [[(a, 0, False) for a in query_grad_pair]],
-    )
-    later_kv, later_qg, own_qg = packed(
-        arrays,
-        [[(a, h, False) for h in later for a in side] for side in (key_value, query_grad_pair)]
-        + [[(a, h, True) for h in range(half) for a in query_grad_pair]],
-    )
-    kv_first = lax.ppermute(first_kv, "sx", swap)
-    qg_first = lax.ppermute(first_qg, "sx", swap)
-    kv_later = lax.ppermute(later_kv, "sx", swap)
-    qg_later = lax.ppermute(later_qg, "sx", swap)
+        [picks(range(half), query_and_grad, True)]
+        + [picks([h], side, False) for side in (key_value, query_and_grad) for h in later],
+    )
+    kv_out[1:], qg_out[1:] = rest[: half - 1], rest[half - 1 :]
+    kv = [lax.ppermute(kv_out[h], "sx", swap) for h in range(half)]
+    qg = [lax.ppermute(qg_out[h], "sx", swap) for h in range(half)]
     even_own, odd_own = rows_sent(own_kv, own_kv)
     bias = window_bias(cell_valid, tile_size)
-    even_first, odd_first = rows_sent(kv_first, kv_first)
-    even_later, odd_later = rows_sent(kv_later, kv_later)
 
     own_dq, partner_dq, backs = [], [], []
     for h in range(half):
-        kv, qg, even, odd = (
-            (kv_later, qg_later, even_later, odd_later)
-            if h
-            else (kv_first, qg_first, even_first, odd_first)
-        )
-        sides = (own_kv, own_qg, kv, qg, even_own, even, odd_own, odd)
-        grads = head_grads(h, max(2 * h - 2, 0), sides, bias)
+        even, odd = rows_sent(kv[h], kv[h])
+        grads = head_grads(h, (own_kv, own_qg, kv[h], qg[h], even_own, even, odd_own, odd), bias)
         own_dq.append(grads[0])
         partner_dq.append(grads[1])
         backs.append((grads[2], rows_sent(grads[3], grads[4])))
@@ -427,18 +422,27 @@
     return tuple(out.reshape(queries.shape) for out in outs)
 
 
-def local(queries, *rest):
-    if lax.axis_size("sx") == 2 and queries.shape[0] % 2 == 0 and queries.shape[0] > 2:
-        return swapped(queries, *rest)
-    return general(queries, *rest)
+def swaps_heads(mesh, queries):
+    half, rest = divmod(queries.shape[0], 2 * mesh.shape["tp"])
+    return mesh.shape["sx"] == 2 and rest == 0 and half > 1
 
 
 def solution(mesh):
     spec = P("tp", None, "sy", "sx", None)
-    return jax.shard_map(
-        local,
-        mesh=mesh,
-        in_specs=(spec, spec, spec, spec, P()),
-        out_specs=(spec, spec, spec),
-        check_vma=False,
-    )
+
+    def mapped(body):
+        return jax.shard_map(
+            body,
+            mesh=mesh,
+            in_specs=(spec, spec, spec, spec, P()),
+            out_specs=(spec, spec, spec),
+            check_vma=False,
+        )
+
+    def step(queries, key_vectors, value_vectors, out_grad, cell_valid):
+        arrays = (queries, key_vectors, value_vectors, out_grad, cell_valid)
+        if not swaps_heads(mesh, queries):
+            return mapped(general)(*arrays)
+        return mapped(swapped)(*arrays)
+
+    return step

time: 57.4 us -> 54.7 us (0.953)
  the two profiles are of different devices: /device:TPU:1 before, /device:TPU:0 now
where the time goes in v4:
time: 54.7 us; the launch traced here: 54.4 us
  waiting for transfers between devices  20.3 us (37%)
  starting transfers between devices  18.2 us (33%)
  Pallas kernels  14.8 us (27%)
  between operations  0.77 us (1%)
    pallas_call x3, Pallas kernels, head_grads(): pl.pallas_call(functools.partial(head_kernel, h), out_shape=(pltpu.VMEM((...  9.96 us
    ppermute x3, waiting for transfers between devices, swapped(): theirs.append(lax.ppermute(outgoing, 'sx', swap))  9.46 us
    ppermute x7, starting transfers between devices, rows_sent(): lax.ppermute(odd_block, ('tp', 'sy'), odd_pairs)  7.09 us
    ppermute x7, waiting for transfers between devices, rows_sent(): lax.ppermute(odd_block, ('tp', 'sy'), odd_pairs)  4.24 us
    ppermute x3, starting transfers between devices, swapped(): kv = [lax.ppermute(kv_out[h], 'sx', swap) for h in range(half)]  3.68 us
    ppermute x3, starting transfers between devices, swapped(): qg = [lax.ppermute(qg_out[h], 'sx', swap) for h in range(half)]  3.54 us
    pallas_call x3, Pallas kernels, packed(): pl.pallas_call(functools.partial(pack_kernel, picks), out_shape=tuple((pl...  3.35 us
    ppermute x3, waiting for transfers between devices, swapped(): kv = [lax.ppermute(kv_out[h], 'sx', swap) for h in range(half)]  3.29 us
  transfers between devices with their start and end apart: 23, of which 7 were waited for; matrix products, arithmetic and copies ran while one was open for 1% of the time, Pallas kernels for 23%

profile of v4, /device:TPU:0, one launch (start us, length us, event | category | flops | bytes accessed | tf_op | source)
XLA Modules:
  0.0 54.4 jit_solution(16502821060266995605)
XLA Ops:
  0.6 1.1 %shard_map.76 = (bf16[6,256,128]{2,1,0:T(8,128)(2,1)S(1)}, bf16[2,256,128]{2,1,0:T(8,128)(2,1)S(1)}) custom-call(bf16[6,256,128]{2,1,0:T(8,128)(2,1)} %bitcast.13, bf16[6,256,128]{2,1,0:T(8,128)(2,1)} %bitcast.16, bf16[6,256,128]{2,1,0:T(8,128)(2,1)} %bitcast.19, bf16[6,256,128]{2,1,0:T(8,128)(2,1)} %bitcast.22), custom_call_target="tpu_custom_call" | custom-call | tf_op jit(solution)/shard_map/pallas_call | solution.py:182
  1.8 0.6 %collective-permute-start.2 = (bf16[6,256,128]{2,1,0:T(8,128)(2,1)S(1)}, bf16[6,256,128]{2,1,0:T(8,128)(2,1)S(1)}, u32[]{:S(2)}, u32[]{:S(2)}) collective-permute-start(bf16[6,256,128]{2,1,0:T(8,128)(2,1)S(1)} %get-tuple-element.28.own_kv_ref), channel_id=1, source_target_pairs={{0,2},{2,0},{4,6},{6,4},{8,10},{10,8},{12,14},{14,12},{16,18},{18,... | collective-permute-start | bytes 1179656 | tf_op jit(solution)/shard_map/ppermute | solution.py:381
  2.3 2.6 %collective-permute-start.4 = (bf16[6,256,128]{2,1,0:T(8,128)(2,1)S(1)}, bf16[6,256,128]{2,1,0:T(8,128)(2,1)S(1)}, u32[]{:S(2)}, u32[]{:S(2)}) collective-permute-start(bf16[6,256,128]{2,1,0:T(8,128)(2,1)S(1)} %get-tuple-element.28.own_kv_ref), channel_id=1, source_target_pairs={{0,8},{2,4},{4,2},{6,14},{8,0},{10,12},{12,10},{14,6},{16,24},{18,... | collective-permute-start | bytes 1179656 | tf_op jit(solution)/shard_map/ppermute | solution.py:382
  5.0 0.9 %shard_map.78 = bf16[2,256,128]{2,1,0:T(8,128)(2,1)S(1)} custom-call(bf16[6,256,128]{2,1,0:T(8,128)(2,1)} %bitcast.14, bf16[6,256,128]{2,1,0:T(8,128)(2,1)} %bitcast.17, bf16[6,256,128]{2,1,0:T(8,128)(2,1)} %bitcast.20, bf16[6,256,128]{2,1,0:T(8,128)(2,1)} %bitcast.23), custom_call_target="tpu_custom_call" | custom-call | tf_op jit(solution)/shard_map/pallas_call | solution.py:182
  5.9 1.6 %collective-permute-start = (bf16[2,256,128]{2,1,0:T(8,128)(2,1)S(1)}, bf16[2,256,128]{2,1,0:T(8,128)(2,1)S(1)}, u32[]{:S(2)}, u32[]{:S(2)}) collective-permute-start(bf16[2,256,128]{2,1,0:T(8,128)(2,1)S(1)} %shard_map.78), channel_id=1, source_target_pairs={{0,1},{1,0},{2,3},{3,2},{4,5},{5,4},{6,7},{7,6},{8,9},{9,8},{10,11... | collective-permute-start | bytes 393224 | tf_op jit(solution)/shard_map/ppermute | solution.py:401
  7.5 0.5 collective-permute-start.1
  8.0 0.0 copy-start
  8.0 1.3 %shard_map.77 = (bf16[6,256,128]{2,1,0:T(8,128)(2,1)S(1)}, bf16[2,256,128]{2,1,0:T(8,128)(2,1)S(1)}, bf16[2,256,128]{2,1,0:T(8,128)(2,1)S(1)}, bf16[2,256,128]{2,1,0:T(8,128)(2,1)S(1)}, bf16[2,256,128]{2,1,0:T(8,128)(2,1)S(1)}) custom-call(bf16[6,256,128]{2,1,0:T(8,128)(2,1)} %bitcast.15, bf16[6,256,128]{2,1,0:T(8,128)(2,1)} %bitcast.18, ...), custom_call_target="tpu_custom_call" | custom-call | tf_op jit(solution)/shard_map/pallas_call | solution.py:182
  9.3 1.6 %collective-permute-start.8 = (bf16[2,256,128]{2,1,0:T(8,128)(2,1)S(1)}, bf16[2,256,128]{2,1,0:T(8,128)(2,1)S(1)}, u32[]{:S(2)}, u32[]{:S(2)}) collective-permute-start(bf16[2,256,128]{2,1,0:T(8,128)(2,1)S(1)} %get-tuple-element.35), channel_id=1, source_target_pairs={{0,1},{1,0},{2,3},{3,2},{4,5},{5,4},{6,7},{7,6},{8,9},{9,8},{10,11... | collective-permute-start | bytes 393224 | tf_op jit(solution)/shard_map/ppermute | solution.py:401
  10.9 1.4 %collective-permute-done.kv_ref = bf16[2,256,128]{2,1,0:T(8,128)(2,1)S(1)} collective-permute-done((bf16[2,256,128]{2,1,0:T(8,128)(2,1)S(1)}, bf16[2,256,128]{2,1,0:T(8,128)(2,1)S(1)}, u32[]{:S(2)}, u32[]{:S(2)}) %collective-permute-start) | collective-permute-done | bytes 131104 | tf_op jit(solution)/shard_map/ppermute | solution.py:401
  12.3 0.0 collective-permute-start.3
  12.3 2.8 %collective-permute-done.1.qg_ref = bf16[2,256,128]{2,1,0:T(8,128)(2,1)S(1)} collective-permute-done((bf16[2,256,128]{2,1,0:T(8,128)(2,1)S(1)}, bf16[2,256,128]{2,1,0:T(8,128)(2,1)S(1)}, u32[]{:S(2)}, u32[]{:S(2)}) %collective-permute-start.1) | collective-permute-done | bytes 131104 | tf_op jit(solution)/shard_map/ppermute | solution.py:402
  15.1 0.0 collective-permute-start.5
  15.1 1.9 %collective-permute-done.8.kv_ref = bf16[2,256,128]{2,1,0:T(8,128)(2,1)S(1)} collective-permute-done((bf16[2,256,128]{2,1,0:T(8,128)(2,1)S(1)}, bf16[2,256,128]{2,1,0:T(8,128)(2,1)S(1)}, u32[]{:S(2)}, u32[]{:S(2)}) %collective-permute-start.8) | collective-permute-done | bytes 131104 | tf_op jit(solution)/shard_map/ppermute | solution.py:401
  17.0 1.5 %collective-permute-start.9 = (bf16[2,256,128]{2,1,0:T(8,128)(2,1)S(1)}, bf16[2,256,128]{2,1,0:T(8,128)(2,1)S(1)}, u32[]{:S(2)}, u32[]{:S(2)}) collective-permute-start(bf16[2,256,128]{2,1,0:T(8,128)(2,1)S(1)} %get-tuple-element.36), channel_id=1, source_target_pairs={{0,1},{1,0},{2,3},{3,2},{4,5},{5,4},{6,7},{7,6},{8,9},{9,8},{10,11... | collective-permute-start | bytes 393224 | tf_op jit(solution)/shard_map/ppermute | solution.py:402
  18.5 0.0 collective-permute-done.3.even_ref
  18.5 0.5 collective-permute-start.14
  19.0 1.1 %collective-permute-done.5.odd_ref = bf16[2,256,128]{2,1,0:T(8,128)(2,1)S(1)} collective-permute-done((bf16[2,256,128]{2,1,0:T(8,128)(2,1)S(1)}, bf16[2,256,128]{2,1,0:T(8,128)(2,1)S(1)}, u32[]{:S(2)}, u32[]{:S(2)}) %collective-permute-start.5) | collective-permute-done | bytes 131104 | tf_op jit(solution)/shard_map/ppermute | solution.py:382
  20.1 0.0 collective-permute-start.10
  20.1 0.0 copy-done
  20.1 0.1 copy.8.valid_ref
  20.2 0.0 collective-permute-done.2.even_own_ref
  20.2 0.2 collective-permute-start.11
  20.3 0.3 window_bias.1.bias_ref
  20.7 0.0 collective-permute-done.4.odd_own_ref
  20.7 3.3 %head_grads.3 = (bf16[256,128]{1,0:T(8,128)(2,1)S(1)}, bf16[256,128]{1,0:T(8,128)(2,1)S(1)}, f32[4,256,128]{2,1,0:T(8,128)S(1)}, bf16[4,256,128]{2,1,0:T(8,128)(2,1)S(1)}, bf16[4,256,128]{2,1,0:T(8,128)(2,1)S(1)}) custom-call(bf16[6,256,128]{2,1,0:T(8,128)(2,1)S(1)} %get-tuple-element.28.own_kv_ref, bf16[6,256,128]{2,1,0:T(8,128)(2,1)S(1)} %get-tuple-element.29.own_qg_ref, ...), custom_call_target="tpu_custom_call" | custom-call | flops 1006632960 | bytes 1310720 | tf_op jit(solution)/shard_map/head_grads/pallas_call | solution.py:309
  24.0 1.9 %collective-permute-start.7 = (bf16[4,256,128]{2,1,0:T(8,128)(2,1)S(1)}, bf16[4,256,128]{2,1,0:T(8,128)(2,1)S(1)}, u32[]{:S(2)}, u32[]{:S(2)}) collective-permute-start(bf16[4,256,128]{2,1,0:T(8,128)(2,1)S(1)} %get-tuple-element.34), channel_id=1, source_target_pairs={{0,8},{2,4},{4,2},{6,14},{8,0},{10,12},{12,10},{14,6},{16,24},{18,... | collective-permute-start | bytes 786440 | tf_op jit(solution)/shard_map/ppermute | solution.py:382
  25.9 0.0 collective-permute-done.9.qg_ref
  25.9 0.2 collective-permute-start.6
  26.2 0.0 collective-permute-done.14.kv_ref
  26.2 1.5 %collective-permute-start.15 = (bf16[2,256,128]{2,1,0:T(8,128)(2,1)S(1)}, bf16[2,256,128]{2,1,0:T(8,128)(2,1)S(1)}, u32[]{:S(2)}, u32[]{:S(2)}) collective-permute-start(bf16[2,256,128]{2,1,0:T(8,128)(2,1)S(1)} %get-tuple-element.42), channel_id=1, source_target_pairs={{0,1},{1,0},{2,3},{3,2},{4,5},{5,4},{6,7},{7,6},{8,9},{9,8},{10,11... | collective-permute-start | bytes 393224 | tf_op jit(solution)/shard_map/ppermute | solution.py:402
  27.7 0.0 collective-permute-done.10.even_ref
  27.7 0.0 collective-permute-start.16
  27.7 0.0 collective-permute-done.11.odd_ref
  27.7 0.4 collective-permute-start.17
  28.1 3.3 %head_grads.4 = (bf16[256,128]{1,0:T(8,128)(2,1)S(1)}, bf16[256,128]{1,0:T(8,128)(2,1)S(1)}, f32[4,256,128]{2,1,0:T(8,128)S(1)}, bf16[4,256,128]{2,1,0:T(8,128)(2,1)S(1)}, bf16[4,256,128]{2,1,0:T(8,128)(2,1)S(1)}) custom-call(bf16[6,256,128]{2,1,0:T(8,128)(2,1)S(1)} %get-tuple-element.28.own_kv_ref, bf16[6,256,128]{2,1,0:T(8,128)(2,1)S(1)} %get-tuple-element.29.own_qg_ref, ...), custom_call_target="tpu_custom_call" | custom-call | flops 1006632960 | bytes 1310720 | tf_op jit(solution)/shard_map/head_grads/pallas_call | solution.py:309
  31.4 0.4 collective-permute-done.15.qg_ref
  31.9 1.3 %collective-permute-start.13 = (bf16[4,256,128]{2,1,0:T(8,128)(2,1)S(1)}, bf16[4,256,128]{2,1,0:T(8,128)(2,1)S(1)}, u32[]{:S(2)}, u32[]{:S(2)}) collective-permute-start(bf16[4,256,128]{2,1,0:T(8,128)(2,1)S(1)} %get-tuple-element.40), channel_id=1, source_target_pairs={{0,8},{2,4},{4,2},{6,14},{8,0},{10,12},{12,10},{14,6},{16,24},{18,... | collective-permute-start | bytes 786440 | tf_op jit(solution)/shard_map/ppermute | solution.py:382
  33.2 0.0 collective-permute-done.16.even_ref
  33.2 0.2 collective-permute-start.12
  33.4 0.0 collective-permute-done.17.odd_ref
  33.4 3.3 %head_grads.5 = (bf16[256,128]{1,0:T(8,128)(2,1)S(1)}, bf16[256,128]{1,0:T(8,128)(2,1)S(1)}, f32[4,256,128]{2,1,0:T(8,128)S(1)}, bf16[4,256,128]{2,1,0:T(8,128)(2,1)S(1)}, bf16[4,256,128]{2,1,0:T(8,128)(2,1)S(1)}) custom-call(bf16[6,256,128]{2,1,0:T(8,128)(2,1)S(1)} %get-tuple-element.28.own_kv_ref, bf16[6,256,128]{2,1,0:T(8,128)(2,1)S(1)} %get-tuple-element.29.own_qg_ref, ...), custom_call_target="tpu_custom_call" | custom-call | flops 1006632960 | bytes 1310720 | tf_op jit(solution)/shard_map/head_grads/pallas_call | solution.py:309
  36.7 0.6 %collective-permute-start.19 = (bf16[4,256,128]{2,1,0:T(8,128)(2,1)S(1)}, bf16[4,256,128]{2,1,0:T(8,128)(2,1)S(1)}, u32[]{:S(2)}, u32[]{:S(2)}) collective-permute-start(bf16[4,256,128]{2,1,0:T(8,128)(2,1)S(1)} %get-tuple-element.46), channel_id=1, source_target_pairs={{0,8},{2,4},{4,2},{6,14},{8,0},{10,12},{12,10},{14,6},{16,24},{18,... | collective-permute-start | bytes 786440 | tf_op jit(solution)/shard_map/ppermute | solution.py:382
  37.3 0.0 collective-permute-done.7
  37.3 0.0 collective-permute-start.18
  37.3 0.0 collective-permute-done.6
  37.3 0.1 add_convert_fusion.2
  37.5 1.6 %collective-permute-start.20 = (bf16[4,256,128]{2,1,0:T(8,128)(2,1)S(1)}, bf16[4,256,128]{2,1,0:T(8,128)(2,1)S(1)}, u32[]{:S(2)}, u32[]{:S(2)}) collective-permute-start(bf16[4,256,128]{2,1,0:T(8,128)(2,1)S(1)} %pad_maximum_fusion), channel_id=1, source_target_pairs={{0,1},{1,0},{2,3},{3,2},{4,5},{5,4},{6,7},{7,6},{8,9},{9,8},{10,11... | collective-permute-start | bytes 786440 | tf_op jit(solution)/shard_map/ppermute | solution.py:420
  39.1 0.0 collective-permute-done.13
  39.1 0.0 collective-permute-done.12
  39.1 0.1 add_convert_fusion.1
  39.2 0.8 %collective-permute-start.21 = (bf16[3,256,128]{2,1,0:T(8,128)(2,1)S(1)}, bf16[3,256,128]{2,1,0:T(8,128)(2,1)S(1)}, u32[]{:S(2)}, u32[]{:S(2)}) collective-permute-start(bf16[3,256,128]{2,1,0:T(8,128)(2,1)S(1)} %pad_maximum_fusion.1), channel_id=1, source_target_pairs={{0,1},{1,0},{2,3},{3,2},{4,5},{5,4},{6,7},{7,6},{8,9},{9,8},{10,11... | collective-permute-start | bytes 589832 | tf_op jit(solution)/shard_map/ppermute | solution.py:420
  40.0 3.2 %collective-permute-done.19 = bf16[4,256,128]{2,1,0:T(8,128)(2,1)S(1)} collective-permute-done((bf16[4,256,128]{2,1,0:T(8,128)(2,1)S(1)}, bf16[4,256,128]{2,1,0:T(8,128)(2,1)S(1)}, u32[]{:S(2)}, u32[]{:S(2)}) %collective-permute-start.19) | collective-permute-done | bytes 262176 | tf_op jit(solution)/shard_map/ppermute | solution.py:382
  43.1 0.0 collective-permute-done.18
  43.1 0.1 add_convert_fusion
  43.3 0.6 %collective-permute-start.22 = (bf16[2,256,128]{2,1,0:T(8,128)(2,1)S(1)}, bf16[2,256,128]{2,1,0:T(8,128)(2,1)S(1)}, u32[]{:S(2)}, u32[]{:S(2)}) collective-permute-start(bf16[2,256,128]{2,1,0:T(8,128)(2,1)S(1)} %get-tuple-element.53), channel_id=1, source_target_pairs={{0,1},{1,0},{2,3},{3,2},{4,5},{5,4},{6,7},{7,6},{8,9},{9,8},{10,11... | collective-permute-start | bytes 393224 | tf_op jit(solution)/shard_map/ppermute | solution.py:420
  43.8 9.5 %collective-permute-done.22.refs_8_ = bf16[2,256,128]{2,1,0:T(8,128)(2,1)S(1)} collective-permute-done((bf16[2,256,128]{2,1,0:T(8,128)(2,1)S(1)}, bf16[2,256,128]{2,1,0:T(8,128)(2,1)S(1)}, u32[]{:S(2)}, u32[]{:S(2)}) %collective-permute-start.22) | collective-permute-done | bytes 131104 | tf_op jit(solution)/shard_map/ppermute | solution.py:420
  53.3 0.0 collective-permute-done.21.refs_7_
  53.3 0.0 collective-permute-done.20.refs_6_
  53.3 1.1 %collected.1 = (bf16[6,256,128]{2,1,0:T(8,128)(2,1)}, bf16[6,256,128]{2,1,0:T(8,128)(2,1)}, bf16[6,256,128]{2,1,0:T(8,128)(2,1)}) custom-call(bf16[256,128]{1,0:T(8,128)(2,1)S(1)} %get-tuple-element.31.refs_0_, bf16[2,256,128]{2,1,0:T(8,128)(2,1)S(1)} %get-tuple-element.58.refs_1_, bf16[256,128]{1,0:T(8,128)(2,1)S(1)} %get-tuple-element.37.refs_2_, ...), custom_call_target="tpu_custom_call" | custom-call | tf_op jit(solution)/shard_map/collected/pallas_call | solution.py:358
  (5 shorter events, 0.1 us)
Async XLA Ops:
  1.8 18.4 %collective-permute-start.2 = (bf16[6,256,128]{2,1,0:T(8,128)(2,1)S(1)}, bf16[6,256,128]{2,1,0:T(8,128)(2,1)S(1)}, u32[]{:S(2)}, u32[]{:S(2)}) collective-permute-start(bf16[6,256,128]{2,1,0:T(8,128)(2,1)S(1)} %get-tuple-element.28.own_kv_ref), channel_id=1, source_target_pairs={{0,2},{2,0},{4,6},{6,4},{8,10},{10,8},{12,14},{14,12},{16,18},{18,... | collective-permute-start | bytes 1179656 | tf_op jit(solution)/shard_map/ppermute | solution.py:381
  2.3 18.3 %collective-permute-start.4 = (bf16[6,256,128]{2,1,0:T(8,128)(2,1)S(1)}, bf16[6,256,128]{2,1,0:T(8,128)(2,1)S(1)}, u32[]{:S(2)}, u32[]{:S(2)}) collective-permute-start(bf16[6,256,128]{2,1,0:T(8,128)(2,1)S(1)} %get-tuple-element.28.own_kv_ref), channel_id=1, source_target_pairs={{0,8},{2,4},{4,2},{6,14},{8,0},{10,12},{12,10},{14,6},{16,24},{18,... | collective-permute-start | bytes 1179656 | tf_op jit(solution)/shard_map/ppermute | solution.py:382
  5.9 6.4 %collective-permute-start = (bf16[2,256,128]{2,1,0:T(8,128)(2,1)S(1)}, bf16[2,256,128]{2,1,0:T(8,128)(2,1)S(1)}, u32[]{:S(2)}, u32[]{:S(2)}) collective-permute-start(bf16[2,256,128]{2,1,0:T(8,128)(2,1)S(1)} %shard_map.78), channel_id=1, source_target_pairs={{0,1},{1,0},{2,3},{3,2},{4,5},{5,4},{6,7},{7,6},{8,9},{9,8},{10,11... | collective-permute-start | bytes 393224 | tf_op jit(solution)/shard_map/ppermute | solution.py:401
  7.5 7.7 %collective-permute-start.1 = (bf16[2,256,128]{2,1,0:T(8,128)(2,1)S(1)}, bf16[2,256,128]{2,1,0:T(8,128)(2,1)S(1)}, u32[]{:S(2)}, u32[]{:S(2)}) collective-permute-start(bf16[2,256,128]{2,1,0:T(8,128)(2,1)S(1)} %get-tuple-element.30), channel_id=1, source_target_pairs={{0,1},{1,0},{2,3},{3,2},{4,5},{5,4},{6,7},{7,6},{8,9},{9,8},{10,11... | collective-permute-start | bytes 393224 | tf_op jit(solution)/shard_map/ppermute | solution.py:402
  8.0 12.1 %copy-start = (s32[32,16]{0,1:T(8,128)S(1)}, s32[32,16]{0,1:T(8,128)}, u32[]{:S(2)}) copy-start(s32[32,16]{0,1:T(8,128)} %param.9) | copy-start | bytes 6148
  9.3 7.7 %collective-permute-start.8 = (bf16[2,256,128]{2,1,0:T(8,128)(2,1)S(1)}, bf16[2,256,128]{2,1,0:T(8,128)(2,1)S(1)}, u32[]{:S(2)}, u32[]{:S(2)}) collective-permute-start(bf16[2,256,128]{2,1,0:T(8,128)(2,1)S(1)} %get-tuple-element.35), channel_id=1, source_target_pairs={{0,1},{1,0},{2,3},{3,2},{4,5},{5,4},{6,7},{7,6},{8,9},{9,8},{10,11... | collective-permute-start | bytes 393224 | tf_op jit(solution)/shard_map/ppermute | solution.py:401
  12.3 6.2 %collective-permute-start.3 = (bf16[2,256,128]{2,1,0:T(8,128)(2,1)S(1)}, bf16[2,256,128]{2,1,0:T(8,128)(2,1)S(1)}, u32[]{:S(2)}, u32[]{:S(2)}) collective-permute-start(bf16[2,256,128]{2,1,0:T(8,128)(2,1)S(1)} %collective-permute-done.kv_ref), channel_id=1, source_target_pairs={{0,2},{2,0},{4,6},{6,4},{8,10},{10,8},{12,14},{14,12},{16,18},{18,... | collective-permute-start | bytes 393224 | tf_op jit(solution)/shard_map/ppermute | solution.py:381
  15.1 5.0 %collective-permute-start.5 = (bf16[2,256,128]{2,1,0:T(8,128)(2,1)S(1)}, bf16[2,256,128]{2,1,0:T(8,128)(2,1)S(1)}, u32[]{:S(2)}, u32[]{:S(2)}) collective-permute-start(bf16[2,256,128]{2,1,0:T(8,128)(2,1)S(1)} %collective-permute-done.kv_ref), channel_id=1, source_target_pairs={{0,8},{2,4},{4,2},{6,14},{8,0},{10,12},{12,10},{14,6},{16,24},{18,... | collective-permute-start | bytes 393224 | tf_op jit(solution)/shard_map/ppermute | solution.py:382
  17.0 9.0 %collective-permute-start.9 = (bf16[2,256,128]{2,1,0:T(8,128)(2,1)S(1)}, bf16[2,256,128]{2,1,0:T(8,128)(2,1)S(1)}, u32[]{:S(2)}, u32[]{:S(2)}) collective-permute-start(bf16[2,256,128]{2,1,0:T(8,128)(2,1)S(1)} %get-tuple-element.36), channel_id=1, source_target_pairs={{0,1},{1,0},{2,3},{3,2},{4,5},{5,4},{6,7},{7,6},{8,9},{9,8},{10,11... | collective-permute-start | bytes 393224 | tf_op jit(solution)/shard_map/ppermute | solution.py:402
  18.5 7.7 %collective-permute-start.14 = (bf16[2,256,128]{2,1,0:T(8,128)(2,1)S(1)}, bf16[2,256,128]{2,1,0:T(8,128)(2,1)S(1)}, u32[]{:S(2)}, u32[]{:S(2)}) collective-permute-start(bf16[2,256,128]{2,1,0:T(8,128)(2,1)S(1)} %get-tuple-element.41), channel_id=1, source_target_pairs={{0,1},{1,0},{2,3},{3,2},{4,5},{5,4},{6,7},{7,6},{8,9},{9,8},{10,11... | collective-permute-start | bytes 393224 | tf_op jit(solution)/shard_map/ppermute | solution.py:401
  20.1 7.6 %collective-permute-start.10 = (bf16[2,256,128]{2,1,0:T(8,128)(2,1)S(1)}, bf16[2,256,128]{2,1,0:T(8,128)(2,1)S(1)}, u32[]{:S(2)}, u32[]{:S(2)}) collective-permute-start(bf16[2,256,128]{2,1,0:T(8,128)(2,1)S(1)} %collective-permute-done.8.kv_ref), channel_id=1, source_target_pairs={{0,2},{2,0},{4,6},{6,4},{8,10},{10,8},{12,14},{14,12},{16,18},{18,... | collective-permute-start | bytes 393224 | tf_op jit(solution)/shard_map/ppermute | solution.py:381
  20.2 7.5 %collective-permute-start.11 = (bf16[2,256,128]{2,1,0:T(8,128)(2,1)S(1)}, bf16[2,256,128]{2,1,0:T(8,128)(2,1)S(1)}, u32[]{:S(2)}, u32[]{:S(2)}) collective-permute-start(bf16[2,256,128]{2,1,0:T(8,128)(2,1)S(1)} %collective-permute-done.8.kv_ref), channel_id=1, source_target_pairs={{0,8},{2,4},{4,2},{6,14},{8,0},{10,12},{12,10},{14,6},{16,24},{18,... | collective-permute-start | bytes 393224 | tf_op jit(solution)/shard_map/ppermute | solution.py:382
  24.0 13.3 %collective-permute-start.7 = (bf16[4,256,128]{2,1,0:T(8,128)(2,1)S(1)}, bf16[4,256,128]{2,1,0:T(8,128)(2,1)S(1)}, u32[]{:S(2)}, u32[]{:S(2)}) collective-permute-start(bf16[4,256,128]{2,1,0:T(8,128)(2,1)S(1)} %get-tuple-element.34), channel_id=1, source_target_pairs={{0,8},{2,4},{4,2},{6,14},{8,0},{10,12},{12,10},{14,6},{16,24},{18,... | collective-permute-start | bytes 786440 | tf_op jit(solution)/shard_map/ppermute | solution.py:382
  25.9 11.4 %collective-permute-start.6 = (bf16[4,256,128]{2,1,0:T(8,128)(2,1)S(1)}, bf16[4,256,128]{2,1,0:T(8,128)(2,1)S(1)}, u32[]{:S(2)}, u32[]{:S(2)}) collective-permute-start(bf16[4,256,128]{2,1,0:T(8,128)(2,1)S(1)} %get-tuple-element.33), channel_id=1, source_target_pairs={{0,2},{2,0},{4,6},{6,4},{8,10},{10,8},{12,14},{14,12},{16,18},{18,... | collective-permute-start | bytes 786440 | tf_op jit(solution)/shard_map/ppermute | solution.py:381
  26.2 5.7 %collective-permute-start.15 = (bf16[2,256,128]{2,1,0:T(8,128)(2,1)S(1)}, bf16[2,256,128]{2,1,0:T(8,128)(2,1)S(1)}, u32[]{:S(2)}, u32[]{:S(2)}) collective-permute-start(bf16[2,256,128]{2,1,0:T(8,128)(2,1)S(1)} %get-tuple-element.42), channel_id=1, source_target_pairs={{0,1},{1,0},{2,3},{3,2},{4,5},{5,4},{6,7},{7,6},{8,9},{9,8},{10,11... | collective-permute-start | bytes 393224 | tf_op jit(solution)/shard_map/ppermute | solution.py:402
  27.7 5.5 %collective-permute-start.16 = (bf16[2,256,128]{2,1,0:T(8,128)(2,1)S(1)}, bf16[2,256,128]{2,1,0:T(8,128)(2,1)S(1)}, u32[]{:S(2)}, u32[]{:S(2)}) collective-permute-start(bf16[2,256,128]{2,1,0:T(8,128)(2,1)S(1)} %collective-permute-done.14.kv_ref), channel_id=1, source_target_pairs={{0,2},{2,0},{4,6},{6,4},{8,10},{10,8},{12,14},{14,12},{16,18},{18,... | collective-permute-start | bytes 393224 | tf_op jit(solution)/shard_map/ppermute | solution.py:381
  27.7 5.7 %collective-permute-start.17 = (bf16[2,256,128]{2,1,0:T(8,128)(2,1)S(1)}, bf16[2,256,128]{2,1,0:T(8,128)(2,1)S(1)}, u32[]{:S(2)}, u32[]{:S(2)}) collective-permute-start(bf16[2,256,128]{2,1,0:T(8,128)(2,1)S(1)} %collective-permute-done.14.kv_ref), channel_id=1, source_target_pairs={{0,8},{2,4},{4,2},{6,14},{8,0},{10,12},{12,10},{14,6},{16,24},{18,... | collective-permute-start | bytes 393224 | tf_op jit(solution)/shard_map/ppermute | solution.py:382
  31.9 7.2 %collective-permute-start.13 = (bf16[4,256,128]{2,1,0:T(8,128)(2,1)S(1)}, bf16[4,256,128]{2,1,0:T(8,128)(2,1)S(1)}, u32[]{:S(2)}, u32[]{:S(2)}) collective-permute-start(bf16[4,256,128]{2,1,0:T(8,128)(2,1)S(1)} %get-tuple-element.40), channel_id=1, source_target_pairs={{0,8},{2,4},{4,2},{6,14},{8,0},{10,12},{12,10},{14,6},{16,24},{18,... | collective-permute-start | bytes 786440 | tf_op jit(solution)/shard_map/ppermute | solution.py:382
  33.2 5.9 %collective-permute-start.12 = (bf16[4,256,128]{2,1,0:T(8,128)(2,1)S(1)}, bf16[4,256,128]{2,1,0:T(8,128)(2,1)S(1)}, u32[]{:S(2)}, u32[]{:S(2)}) collective-permute-start(bf16[4,256,128]{2,1,0:T(8,128)(2,1)S(1)} %get-tuple-element.39), channel_id=1, source_target_pairs={{0,2},{2,0},{4,6},{6,4},{8,10},{10,8},{12,14},{14,12},{16,18},{18,... | collective-permute-start | bytes 786440 | tf_op jit(solution)/shard_map/ppermute | solution.py:381
  36.7 6.4 %collective-permute-start.19 = (bf16[4,256,128]{2,1,0:T(8,128)(2,1)S(1)}, bf16[4,256,128]{2,1,0:T(8,128)(2,1)S(1)}, u32[]{:S(2)}, u32[]{:S(2)}) collective-permute-start(bf16[4,256,128]{2,1,0:T(8,128)(2,1)S(1)} %get-tuple-element.46), channel_id=1, source_target_pairs={{0,8},{2,4},{4,2},{6,14},{8,0},{10,12},{12,10},{14,6},{16,24},{18,... | collective-permute-start | bytes 786440 | tf_op jit(solution)/shard_map/ppermute | solution.py:382
  37.3 5.8 %collective-permute-start.18 = (bf16[4,256,128]{2,1,0:T(8,128)(2,1)S(1)}, bf16[4,256,128]{2,1,0:T(8,128)(2,1)S(1)}, u32[]{:S(2)}, u32[]{:S(2)}) collective-permute-start(bf16[4,256,128]{2,1,0:T(8,128)(2,1)S(1)} %get-tuple-element.45), channel_id=1, source_target_pairs={{0,2},{2,0},{4,6},{6,4},{8,10},{10,8},{12,14},{14,12},{16,18},{18,... | collective-permute-start | bytes 786440 | tf_op jit(solution)/shard_map/ppermute | solution.py:381
  37.5 15.8 %collective-permute-start.20 = (bf16[4,256,128]{2,1,0:T(8,128)(2,1)S(1)}, bf16[4,256,128]{2,1,0:T(8,128)(2,1)S(1)}, u32[]{:S(2)}, u32[]{:S(2)}) collective-permute-start(bf16[4,256,128]{2,1,0:T(8,128)(2,1)S(1)} %pad_maximum_fusion), channel_id=1, source_target_pairs={{0,1},{1,0},{2,3},{3,2},{4,5},{5,4},{6,7},{7,6},{8,9},{9,8},{10,11... | collective-permute-start | bytes 786440 | tf_op jit(solution)/shard_map/ppermute | solution.py:420
  39.2 14.1 %collective-permute-start.21 = (bf16[3,256,128]{2,1,0:T(8,128)(2,1)S(1)}, bf16[3,256,128]{2,1,0:T(8,128)(2,1)S(1)}, u32[]{:S(2)}, u32[]{:S(2)}) collective-permute-start(bf16[3,256,128]{2,1,0:T(8,128)(2,1)S(1)} %pad_maximum_fusion.1), channel_id=1, source_target_pairs={{0,1},{1,0},{2,3},{3,2},{4,5},{5,4},{6,7},{7,6},{8,9},{9,8},{10,11... | collective-permute-start | bytes 589832 | tf_op jit(solution)/shard_map/ppermute | solution.py:420
  43.3 10.0 %collective-permute-start.22 = (bf16[2,256,128]{2,1,0:T(8,128)(2,1)S(1)}, bf16[2,256,128]{2,1,0:T(8,128)(2,1)S(1)}, u32[]{:S(2)}, u32[]{:S(2)}) collective-permute-start(bf16[2,256,128]{2,1,0:T(8,128)(2,1)S(1)} %get-tuple-element.53), channel_id=1, source_target_pairs={{0,1},{1,0},{2,3},{3,2},{4,5},{5,4},{6,7},{7,6},{8,9},{9,8},{10,11... | collective-permute-start | bytes 393224 | tf_op jit(solution)/shard_map/ppermute | solution.py:420
